TPU v7x, 32 devices: a whole 2x2x4 slice. The times are simulated.
32 devices in a mesh: server: 4 (over z), worker: 8 (over y, x, core).
Axes of the slice: x: 2, y: 2, z: 4, core: 2. Of those that a mesh axis runs over, the one named last changes fastest.
Arguments:
- sgt: bfloat16 [4096, 18, 2048], P(('server', 'worker')), may hold values from -6 to 6
- ownership: int32 [4096], replicated, may hold values from 0 to 4095, as said below
- sub_points: int32 [8, 4, 96], P('worker', None, 'server'), may hold values from 0 to 4095, as said below
- moments: float32 [8, 4, 6, 96], P('worker', None, None, 'server'), may hold values from -0.25 to 0.25
- slip: bfloat16 [8, 4, 96, 512], P('worker', None, 'server'), may hold values from -0.25 to 0.25
Outputs:
- seismogram: float32 [8, 4, 3, 2048], P('worker', 'server')
- spectra_out: float32 [8, 4, 3, 44], P('worker', 'server')
Inputs may be any that keep to these rules, and one draw needn't show every extreme that they name: A permutation: fault point p is stored in row ownership[p] of sgt, which lies on the device of index ownership[p] // 128 along server+worker. `sub_points`: of the 96 subfaults that one device holds (4 ruptures times 24 subfaults), at most 4 are stored on any one device, and that number is reached; a point may recur.
All inputs are finite; a program needn't handle non-finite values.
Results may differ from a plain program's by a relative error of at most 0.0043.
Values may be sent and summed in bfloat16 or wider, within the bound.
No kernel may reach another device: no remote copies, remote signals or barrier semaphores. Data moves between devices by JAX's collectives and lax.ppermute only.
A program may use at most 192 MiB of HBM per device.

v0:
```python
import math

import jax
import jax.numpy as jnp
from jax import lax
from jax.sharding import PartitionSpec as P

PERIODS = 44


DAMPING = 0.05


def dft_tables(n_time):
    n_freq = n_time // 2
    time_index = jnp.arange(n_time, dtype=jnp.int32)
    freq_index = jnp.arange(n_freq, dtype=jnp.int32)
    wrapped = time_index[:, None] * freq_index[None, :] % n_time
    angles = wrapped.astype(jnp.float32) * (2.0 * math.pi / n_time)
    forward = jnp.concatenate([jnp.cos(angles), -jnp.sin(angles)], axis=1).astype(jnp.bfloat16)
    weight = jnp.where(freq_index == 0, 1.0, 2.0).astype(jnp.float32)
    inverse = jnp.concatenate(
        [weight[:, None] * jnp.cos(angles.T), -weight[:, None] * jnp.sin(angles.T)], axis=0
    )
    return (forward, inverse)


def oscillator_peaks(spec, inverse, n_time, n_periods):
    n_freq = n_time // 2
    omega_freq = jnp.arange(n_freq, dtype=jnp.int32).astype(jnp.float32) * (2.0 * math.pi / n_time)
    low = math.log(4.0 / n_time)
    high = math.log(0.25)
    steps_osc = jnp.arange(n_periods, dtype=jnp.int32).astype(jnp.float32)
    omega_osc = 2.0 * math.pi * jnp.exp(low + (high - low) * steps_osc / (n_periods - 1))
    den_real = omega_osc[:, None] ** 2 - omega_freq[None, :] ** 2
    den_imag = 2.0 * DAMPING * omega_osc[:, None] * omega_freq[None, :]
    den_square = den_real * den_real + den_imag * den_imag
    gain_osc = omega_osc[:, None] ** 2 / den_square
    spec_real = spec[:, None, :n_freq]
    spec_imag = spec[:, None, n_freq:]
    acc_real = -gain_osc * (spec_real * den_real + spec_imag * den_imag)
    acc_imag = -gain_osc * (spec_imag * den_real - spec_real * den_imag)
    stacked = jnp.concatenate([acc_real, acc_imag], axis=-1).reshape(3 * n_periods, n_time)
    accel = jnp.dot(stacked, inverse, precision=lax.Precision.HIGHEST) / n_time
    return jnp.max(jnp.abs(accel), axis=-1).reshape(3, n_periods)


def contract_moment(green_rows, weight_rows):
    count = green_rows.shape[0]
    n_time = green_rows.shape[-1]
    shaped = green_rows.reshape(count, 3, 6, n_time)
    summed = jnp.zeros((count, 3, n_time), jnp.float32)
    for component in range(6):
        summed = summed + weight_rows[:, component][:, None, None] * shaped[:, :, component, :]
    return summed.astype(jnp.bfloat16)


def exchange_rows(operand):
    return lax.all_to_all(operand, ("server", "worker"), split_axis=0, concat_axis=0, tiled=True)


def exchange_blocks(operand):
    return lax.all_to_all(operand, ("server", "worker"), split_axis=0, concat_axis=0, tiled=True)


def shards(sgt, ownership, sub_points, moments, slip):
    n_server = lax.axis_size("server")
    n_worker = lax.axis_size("worker")
    devices = n_server * n_worker
    pts_dev = sgt.shape[0]
    n_time = sgt.shape[2]
    n_freq = n_time // 2
    rup_w = sub_points.shape[1]
    sub_dev = sub_points.shape[2]
    requests = rup_w * sub_dev
    capacity = 4 * sub_dev // (3 * n_worker)
    points = sub_points.reshape(requests)
    slots = ownership[points]
    owner_dev = slots // pts_dev
    local_row = slots % pts_dev
    onehot = (owner_dev[:, None] == jnp.arange(devices, dtype=jnp.int32)[None, :]).astype(jnp.int32)
    before = jnp.cumsum(onehot, axis=0) - onehot
    slot_rank = jnp.sum(before * onehot, axis=1)
    target = owner_dev * capacity + slot_rank
    wanted = (
        jnp.full((devices * capacity,), -1, jnp.int32)
        .at[target]
        .set(local_row)
        .reshape(devices, capacity)
    )
    weights = jnp.transpose(moments[0], (0, 2, 1)).reshape(requests, 6)
    forward, inverse = dft_tables(n_time)
    slip_spec = jnp.dot(
        slip.reshape(requests, slip.shape[3]),
        forward[: slip.shape[3]],
        preferred_element_type=jnp.float32,
    )
    asked = exchange_rows(wanted)
    safe_rows = jnp.clip(asked, 0, pts_dev - 1).reshape(devices * capacity)
    payload = sgt[safe_rows].reshape(devices, capacity, 18, n_time)
    returned = exchange_blocks(payload)
    traces = contract_moment(returned.reshape(devices * capacity, 18, n_time)[target], weights)
    trace_spec = jnp.dot(
        traces.reshape(requests * 3, n_time), forward, preferred_element_type=jnp.float32
    ).reshape(rup_w, sub_dev, 3, n_time)
    slip_shaped = slip_spec.reshape(rup_w, sub_dev, 1, n_time)
    real_part = jnp.sum(
        slip_shaped[..., :n_freq] * trace_spec[..., :n_freq]
        - slip_shaped[..., n_freq:] * trace_spec[..., n_freq:],
        axis=1,
    )
    imag_part = jnp.sum(
        slip_shaped[..., :n_freq] * trace_spec[..., n_freq:]
        + slip_shaped[..., n_freq:] * trace_spec[..., :n_freq],
        axis=1,
    )
    partial_spec = jnp.concatenate([real_part, imag_part], axis=-1)
    spec = lax.psum_scatter(partial_spec, "server", scatter_dimension=0, tiled=True)[0]
    seismo = jnp.dot(spec, inverse, precision=lax.Precision.HIGHEST) / n_time
    peaks = oscillator_peaks(spec, inverse, n_time, PERIODS)
    return (seismo.reshape(1, 1, 3, n_time), peaks.reshape(1, 1, 3, PERIODS))


def solution(mesh):
    placed = (
        P(("server", "worker"), None, None),
        P(),
        P("worker", None, "server"),
        P("worker", None, None, "server"),
        P("worker", None, "server", None),
    )
    return jax.shard_map(
        shards,
        mesh=mesh,
        in_specs=placed,
        out_specs=(P("worker", "server", None, None), P("worker", "server", None, None)),
        check_vma=False,
    )
```

profile of v0, /device:TPU:0, one launch (start us, length us, event | category | flops | bytes accessed | tf_op | source)
XLA Modules:
  0.0 398.0 jit_solution(10416062805482361333)
XLA Ops:
  7.2 0.0 copy-start
  7.2 0.8 reshape.434
  8.0 1.6 gather_fusion
  9.7 0.1 fusion.35
  9.7 0.1 reduce_window_sum.11
  9.9 0.2 select_reduce_fusion
  10.1 0.9 scatter_custom_fusion
  11.0 0.1 all_to_all.9
  11.1 14.3 %all_to_all.14 = s32[32,1,4]{2,1,0:T(1,128)S(1)} all-to-all(s32[32,1,4]{2,1,0:T(1,128)S(1)} %bitcast.72), channel_id=1, replica_groups=mesh['server'=4,'worker'=8] {'server','worker'}, dimensions={0} | all-to-all | bytes 1024 | tf_op jit(solution)/shard_map/all_to_all | solution.py:59
  25.3 0.1 clamp_reduce_fusion
  25.4 0.1 min.12
  25.5 24.9 %gather_fusion.1 = bf16[128,18,2048]{2,0,1:T(8,128)(2,1)} fusion(bf16[128,18,2048]{2,0,1:T(8,128)(2,1)} %param.5, s32[1024]{0:T(1024)S(1)} %pad_clamp_fusion.1), kind=kCustom, calls=%fused_computation.1 | custom fusion | bytes 18874880 | tf_op jit(solution)/shard_map/gather | solution.py:100
  50.4 14.6 %reshape.435 = bf16[32,4,18,2048]{3,1,0,2:T(4,128)(2,1)} reshape(bf16[128,18,2048]{2,0,1:T(8,128)(2,1)} %gather_fusion.1) | data formatting | bytes 18874368 | tf_op jit(solution)/shard_map/reshape | solution.py:100
  64.9 9.2 %copy.22 = bf16[32,4,18,2048]{3,1,2,0:T(4,128)(2,1)} copy(bf16[32,4,18,2048]{3,1,0,2:T(4,128)(2,1)} %reshape.435) | data formatting | bytes 18874368 | tf_op jit(solution)/shard_map/reshape | solution.py:100
  74.1 0.0 copy-start.6
  74.1 3.8 all-to-all-start.1
  78.0 0.2 all-reduce.3.cloned.1.call-start
  78.2 0.0 copy-done.6
  78.2 0.1 reshape.433
  78.3 0.1 mul.387
  78.4 0.1 mul.393
  78.5 0.1 mul.396
  78.6 0.1 mul.399
  78.6 0.1 mul.402
  78.7 0.1 mul.405
  78.9 33.8 %negate_convert_fusion = (bf16[2048,1024]{1,0:T(8,128)(2,1)S(1)}, bf16[2048,1024]{1,0:T(8,128)(2,1)S(1)}) fusion(), kind=kLoop, calls=%fused_computation.28 | loop fusion | flops 35651584 | bytes 8388608 | tf_op jit(solution)/shard_map/convert.7
  112.7 0.0 copy-start.2
  112.7 0.0 copy-start.4
  112.7 0.0 copy-done
  112.7 0.5 fusion.28
  113.2 1.5 copy-done.2
  114.7 1.3 copy-done.4
  116.0 0.1 slice_bitcast_fusion.1
  116.1 35.0 %sine_multiply_fusion = (f32[1024,2048]{1,0:T(8,128)}, f32[1024,2048]{1,0:T(8,128)}) fusion(f32[1024]{0:T(1024)S(1)} %fusion.37, f32[1024]{0:T(1024)S(1)} %fusion.36), kind=kLoop, calls=%fused_computation.24 | loop fusion | flops 33554432 | bytes 16785408 | tf_op jit(solution)/shard_map/mul | solution.py:23
  151.0 136.2 %all-to-all-done.1 = bf16[32,4,18,2048]{3,1,2,0:T(4,128)(2,1)} async-done(((bf16[32,4,18,2048]{3,1,2,0:T(4,128)(2,1)}), bf16[32,4,18,2048]{3,1,2,0:T(4,128)(2,1)}, u32[]{:S(2)}, u32[]{:S(2)}) %all-to-all-start.1) | async-done | bytes 9437216 | tf_op jit(solution)/shard_map/all_to_all | solution.py:63
  287.2 13.8 %copy.23 = bf16[32,4,18,2048]{3,2,1,0:T(8,128)(2,1)} copy(bf16[32,4,18,2048]{3,1,2,0:T(4,128)(2,1)} %all-to-all-done.1) | data formatting | bytes 18874368 | tf_op jit(solution)/shard_map/all_to_all | solution.py:63
  301.0 12.2 %gather_fusion.2 = bf16[96,18,2048]{2,1,0:T(8,128)(2,1)} fusion(bf16[128,18,2048]{2,1,0:T(8,128)(2,1)} %bitcast.63, s32[1024]{0:T(1024)S(1)} %pad_clamp_fusion), kind=kCustom, calls=%fused_computation.2 | custom fusion | bytes 14156160 | tf_op jit(solution)/shard_map/gather | solution.py:102
  313.2 7.6 %copy.24 = bf16[96,18,2048]{2,0,1:T(8,128)(2,1)S(1)} copy(bf16[96,18,2048]{2,1,0:T(8,128)(2,1)} %gather_fusion.2) | data formatting | bytes 14155776 | tf_op jit(solution)/shard_map/gather | solution.py:102
  320.8 0.0 copy-start.3
  320.8 0.0 copy-start.5
  320.8 2.6 fusion.48
  323.4 0.0 copy-done.3
  323.4 1.7 copy-done.5
  325.1 5.5 %fusion.3 = f32[4,24,3,2048]{3,1,2,0:T(8,128)S(1)} fusion(bf16[2048,1024]{1,0:T(8,128)(2,1)S(1)} %copy-done.3, bf16[2048,1024]{1,0:T(8,128)(2,1)S(1)} %copy-done.5, bf16[4,24,3,2048]{3,1,0,2:T(8,128)(2,1)S(1)} %bitcast.67, bf16[4,24,3,2048]{3,1,0,2:T(8,128)(2,1)S(1)} %bitcast.68, bf16[4,24,3,2048]{3,1,0,2:T(8,128)(2,1)S(1)} %bitcast.69, ...), kind=kOutput, calls=%fused_computation.17 | convolution fusion | flops 2443313152 | bytes 17828096 | tf_op jit(solution)/shard_map/dot_general | solution.py:103
  330.6 0.0 copy-start.7
  330.6 0.6 subtract_reduce_fusion
  331.2 0.7 pad_maximum_fusion.14
  331.8 0.0 all-reduce.3.cloned.1.call-update
  331.9 0.1 divide_negate_fusion
  332.0 0.0 copy-done.7
  332.0 0.6 dynamic-slice
  332.6 30.0 %all-reduce.3.cloned.1.call-done = f32[4,3,2048]{2,1,0:T(4,128)} async-done(((f32[4,3,2048]{2,1,0:T(4,128)}), f32[4,3,2048]{2,1,0:T(4,128)}) %all-reduce.3.cloned.1.call-update) | async-done | bytes 98320
  362.6 1.4 dynamic-slice_bitcast_fusion
  364.0 0.2 add_multiply_fusion
  364.2 0.1 mul.442
  364.3 0.1 mul.446
  364.3 11.8 %fusion.26 = f32[1,1,3,2048]{3,2,1,0:T(4,128)S(1)} fusion(f32[3,2048]{1,0:T(4,128)S(1)} %dynamic-slice_bitcast_fusion, f32[1024,2048]{1,0:T(8,128)} %get-tuple-element.37, f32[1024,2048]{1,0:T(8,128)} %get-tuple-element.38), kind=kOutput, calls=%fused_computation.49 | convolution fusion | flops 155195392 | bytes 16826368 | tf_op jit(solution)/shard_map/dot_general | solution.py:119
  376.1 0.0 copy-start.1
  376.1 13.3 %fusion.30 = f32[132]{0:T(256)S(1)} fusion(f32[1024,2048]{1,0:T(8,128)} %get-tuple-element.37, f32[1024,2048]{1,0:T(8,128)} %get-tuple-element.38, f32[132,1024]{1,0:T(8,128)S(1)} %mul.446, f32[132,1024]{1,0:T(8,128)S(1)} %mul.442), kind=kOutput, calls=%fused_computation.52 | convolution fusion | flops 6649053184 | bytes 17859088 | tf_op jit(solution)/shard_map/dot_general | solution.py:44
  389.4 0.7 reshape_reshape.3
  390.1 0.6 copy.26
  390.7 0.0 copy-done.1
  (13 shorter events, 0.1 us)
Async XLA Ops:
  7.2 105.6 %copy-start = (bf16[1,4,24,512]{3,2,1,0:T(8,128)(2,1)S(1)}, bf16[1,4,24,512]{3,2,1,0:T(8,128)(2,1)}, u32[]{:S(2)}) copy-start(bf16[1,4,24,512]{3,2,1,0:T(8,128)(2,1)} %param.9) | copy-start | bytes 294916
  74.1 4.1 %copy-start.6 = (f32[1,4,6,24]{3,1,2,0:T(4,128)S(1)}, f32[1,4,6,24]{3,1,2,0:T(4,128)}, u32[]{:S(2)}) copy-start(f32[1,4,6,24]{3,1,2,0:T(4,128)} %param.8) | copy-start | bytes 6916
  74.1 213.1 %all-to-all-start.1 = ((bf16[32,4,18,2048]{3,1,2,0:T(4,128)(2,1)}), bf16[32,4,18,2048]{3,1,2,0:T(4,128)(2,1)}, u32[]{:S(2)}, u32[]{:S(2)}) async-start(bf16[32,4,18,2048]{3,1,2,0:T(4,128)(2,1)} %copy.22), calls=%async_computation.1 | async-start | bytes 18874368 | tf_op jit(solution)/shard_map/all_to_all | solution.py:63
  78.0 284.6 %all-reduce.3.cloned.1.call-start = ((), (), s32[]{:S(2)}) async-start(), calls=%async_computation.2 | async-start | bytes 262144
  112.7 2.0 copy-start.2
  112.7 3.3 copy-start.4
  320.8 2.6 copy-start.3
  320.8 4.3 %copy-start.5 = (bf16[2048,1024]{1,0:T(8,128)(2,1)S(1)}, bf16[2048,1024]{1,0:T(8,128)(2,1)}, u32[]{:S(2)}) copy-start(bf16[2048,1024]{1,0:T(8,128)(2,1)} %copy-done.4) | copy-start | bytes 12582916
  330.6 1.4 copy-start.7
  376.1 14.6 %copy-start.1 = (bf16[1,4,24,512]{3,2,1,0:T(8,128)(2,1)S(1)}, bf16[1,4,24,512]{3,2,1,0:T(8,128)(2,1)}, u32[]{:S(2)}) copy-start(bf16[1,4,24,512]{3,2,1,0:T(8,128)(2,1)} %param.9) | copy-start | bytes 294916
Sparse Core Ops, SparseCore 0:
  332.0 30.5 all-reduce.2
where the time goes:
time: 406 us; the launch traced here: 398 us
  waiting for transfers between devices  166 us (41%)
  local copies, waits for them, and re-layouts  96.8 us (24%)
  other arithmetic  70.9 us (17%)
  matrix products  31.1 us (8%)
  between operations  14.7 us (4%)
  blocking collectives  14.3 us (4%)
    all_to_all x1, waiting for transfers between devices, exchange_blocks(): lax.all_to_all(operand, ('server', 'worker'), split_axis=0, concat_axis=0...  136 us
    mul x1, other arithmetic, dft_tables(): -weight[:, None] * jnp.sin(angles.T)  35 us
    another operation x1, other arithmetic  33.8 us
    unnamed x2, waiting for transfers between devices  30 us
    gather x1, local copies, waits for them, and re-layouts, shards(): payload = sgt[safe_rows].reshape(devices, capacity, 18, n_time)  24.9 us
    reshape x2, local copies, waits for them, and re-layouts, shards(): payload = sgt[safe_rows].reshape(devices, capacity, 18, n_time)  23.8 us
    gather x2, local copies, waits for them, and re-layouts, shards(): returned.reshape(devices * capacity, 18, n_time)[target]  19.8 us
    all_to_all x1, blocking collectives, exchange_rows(): lax.all_to_all(operand, ('server', 'worker'), split_axis=0, concat_axis=0...  14.3 us
  transfers between devices with their start and end apart: 2, of which 2 were waited for; matrix products, arithmetic and copies ran while one was open for 18% of the time, Pallas kernels for 0%

commit v1 on v0

v1 whole, which is shorter than its diff:
```python
import functools
import math

import jax
import jax.numpy as jnp
import numpy as np
from jax import lax
from jax.experimental import pallas as pl
from jax.experimental.pallas import tpu as pltpu
from jax.sharding import PartitionSpec as P

PERIODS = 44
DAMPING = 0.05
ROWS = 48
GROUP = 8
PAD = 32
STEP = 32
F32 = jnp.float32
BF16 = jnp.bfloat16


def nn(a, b):
    return lax.dot_general(a, b, (((1,), (0,)), ((), ())), preferred_element_type=F32)


def nt(a, b):
    return lax.dot_general(a, b, (((1,), (1,)), ((), ())), preferred_element_type=F32)


def iota(shape, dim):
    return lax.broadcasted_iota(jnp.int32, shape, dim)


def hilo(x):
    hi = x.astype(BF16)
    return hi, (x - hi.astype(F32)).astype(BF16)


def angle(product, n_time):
    return (2.0 * math.pi / n_time) * (product % n_time)


def forward_bases(n_time):
    half = n_time // 2
    quarter = half // 2
    freq = np.concatenate([2 * np.arange(quarter), 2 * np.arange(quarter) + 1])
    coarse = angle(np.arange(half // STEP)[:, None] * STEP * freq[None, :], n_time)
    fine = angle(np.arange(STEP)[:, None] * freq[None, :], n_time)
    return [f(x).astype(np.float32) for x in (coarse, fine) for f in (np.cos, np.sin)]


def inverse_bases(n_time):
    half = n_time // 2
    quarter = half // 2
    time = np.arange(half)
    coarse = angle(np.arange(quarter // STEP)[:, None] * 2 * STEP * time[None, :], n_time)
    even = angle(np.arange(STEP)[:, None] * 2 * time[None, :], n_time)
    odd = angle((np.arange(STEP)[:, None] * 2 + 1) * time[None, :], n_time)
    return [f(x).astype(np.float32) for x in (coarse, even, odd) for f in (np.cos, np.sin)]


def pack_kernel(capacity, own_ref, pts_ref, mom_ref, slip_ref, out_ref, scr):
    devices = out_ref.shape[0]
    slots = devices * capacity
    rup_w, sub = pts_ref.shape
    n_slip = slip_ref.shape[2]
    own = own_ref[...]
    blocks = own.shape[0]
    both = jnp.concatenate([own // 128, own % 128], axis=0).astype(F32).astype(BF16)
    spread = iota((128, 6), 0)
    comp = iota((128, 6), 1)
    spread_hi = ((spread < 18) & (spread % 6 == comp)).astype(F32).astype(BF16)
    spread_lo = ((spread >= PAD) & (spread < PAD + 18) & ((spread - PAD) % 6 == comp)).astype(F32).astype(BF16)
    earlier = (iota((sub, sub), 0) < iota((sub, sub), 1)).astype(F32).astype(BF16)
    carry = jnp.zeros((devices, 1), F32)
    slip_acc = jnp.zeros((slots, n_slip), F32)
    tail_acc = jnp.zeros((slots, 128), F32)
    lane = iota((slots, 128), 1)
    for r in range(rup_w):
        p = pts_ref[r : r + 1, :]
        in_lane = (iota((128, sub), 0) == p % 128).astype(F32).astype(BF16)
        found = nn(both, in_lane)
        in_block = (iota((blocks, sub), 0) == p // 128).astype(F32)
        dev = jnp.sum(found[:blocks] * in_block, axis=0, keepdims=True)
        loc = jnp.sum(found[blocks:] * in_block, axis=0, keepdims=True)
        onehot = (iota((devices, sub), 0).astype(F32) == dev).astype(F32)
        before = nn(onehot.astype(BF16), earlier) + carry
        rank = jnp.sum(before * onehot, axis=0, keepdims=True)
        carry = carry + jnp.sum(onehot, axis=1, keepdims=True)
        target = dev * capacity + rank
        pick = (iota((slots, sub), 0).astype(F32) == target).astype(F32)
        pick16 = pick.astype(BF16)
        hi, lo = hilo(mom_ref[r])
        expanded = nn(spread_hi, hi) + nn(spread_lo, lo)
        slip_acc = slip_acc + nn(pick16, slip_ref[r])
        tail = nt(pick16, expanded.astype(BF16))
        row = jnp.sum(pick * loc, axis=1, keepdims=True)
        rup = jnp.sum(pick, axis=1, keepdims=True) * float(r)
        tail = tail + jnp.where((lane >= 64) & (lane < 96), row, 0.0) + jnp.where(lane >= 96, rup, 0.0)
        tail_acc = tail_acc + tail
    scr[:, :n_slip] = slip_acc
    scr[:, n_slip:] = tail_acc
    for d in range(devices):
        out_ref[d] = scr[d * capacity : (d + 1) * capacity, :].astype(BF16)


def owner_kernel(
    n_worker, n_server, rec_ref, sgt_ref, ca_ref, sa_ref, cb_ref, sb_ref, *refs
):
    out_refs = refs[: n_worker]
    rec_s, wb_s, idx_v, idx_s, rows_s, tab_s, tr_s, row_sems, idx_sem = refs[n_worker :]
    devices, capacity, width = rec_ref.shape
    slots = devices * capacity
    n_time = sgt_ref.shape[2]
    half = n_time // 2
    quarter = half // 2
    n_slip = width - 128
    for d in range(devices):
        rec_s[d * capacity : (d + 1) * capacity, :] = rec_ref[d].astype(F32)
    tail = rec_s[:, n_slip:].astype(BF16)
    selector = iota((8, 128), 1)
    row_of = nt((selector == 64).astype(F32).astype(BF16), tail)
    rup_of = nt((selector == 96).astype(F32).astype(BF16), tail)[:1]
    idx_v[...] = row_of.astype(jnp.int32)
    to_smem = pltpu.make_async_copy(idx_v, idx_s, idx_sem)
    to_smem.start()
    to_smem.wait()

    def fetch(s):
        return pltpu.make_async_copy(sgt_ref.at[idx_s[0, s]], rows_s.at[s], row_sems.at[s])

    def start(s, carry):
        fetch(s).start()
        return carry

    lax.fori_loop(0, slots, start, 0)

    l_in = iota((128, GROUP * PAD), 0)
    l_out = iota((128, GROUP * PAD), 1) % PAD
    wb_s[0] = nn(tail, (l_in == l_out).astype(F32).astype(BF16))
    wb_s[1] = nn(tail, (l_in == l_out + PAD).astype(F32).astype(BF16))

    wide = 256
    for lc in range(half // wide):
        sl = slice(lc * wide, (lc + 1) * wide)
        sl2 = slice(half + lc * wide, half + (lc + 1) * wide)
        cb = cb_ref[:, sl]
        sb = sb_ref[:, sl]

        def table(a, carry):
            ca = ca_ref[pl.ds(a, 1), sl]
            sa = sa_ref[pl.ds(a, 1), sl]
            at = pl.ds(pl.multiple_of(a * STEP, STEP), STEP)
            tab_s[at, sl] = (ca * cb - sa * sb).astype(BF16)
            tab_s[at, sl2] = (-(sa * cb + ca * sb)).astype(BF16)
            return carry

        lax.fori_loop(0, half // STEP, table, 0)

    lane = iota((GROUP, GROUP * PAD), 1)
    mine = lane // PAD == iota((GROUP, GROUP * PAD), 0)
    comp = (lane % PAD) // 6
    masks = [mine & (comp == c) for c in range(3)]
    keep = iota((GROUP, PAD, 512), 1) < 18

    def contract(g, carry):
        at = pl.ds(pl.multiple_of(g * GROUP, GROUP), GROUP)
        for i in range(GROUP):
            fetch(g * GROUP + i).wait()
        pieces = [jnp.where(m, wb_s[p, at, :], 0.0) for p in range(2) for m in masks]
        left = jnp.concatenate(pieces, axis=0).astype(BF16)
        for n in range(n_time // 512):
            sl = slice(n * 512, (n + 1) * 512)
            rows = rows_s[at, :, sl]
            rows = jnp.concatenate([rows, jnp.zeros((GROUP, PAD - 18, 512), BF16)], axis=1)
            out = nn(left, rows.reshape(GROUP * PAD, 512))
            both = out[: 3 * GROUP] + out[3 * GROUP :]
            for c in range(3):
                tr_s[c, at, sl] = both[c * GROUP : (c + 1) * GROUP]
        return carry

    lax.fori_loop(0, slots // GROUP, contract, 0)

    ruptures = n_worker * n_server
    shape = (ruptures, slots)
    out_row = iota(shape, 0)
    to_worker = (iota(shape, 1) // capacity) % n_worker
    me_w = lax.axis_index("worker")
    me_s = lax.axis_index("server")
    rup_int = rup_of.astype(jnp.int32)
    where_to = ((to_worker ^ me_w) * n_server) + (rup_int ^ me_s)
    seg = (out_row == where_to).astype(F32).astype(BF16)
    slip = rec_s[:, :n_slip].astype(BF16)
    for q in range(2):
        re = slice(q * quarter, (q + 1) * quarter)
        im = slice(half + q * quarter, half + (q + 1) * quarter)
        slip_re = nn(slip, tab_s[:n_slip, re])
        slip_im = nn(slip, tab_s[:n_slip, im])
        for c in range(3):
            x = jnp.concatenate([tr_s[c, :, :half], tr_s[c, :, half:]], axis=0).astype(BF16)
            u_re = nn(x, tab_s[:, re])
            u_im = nn(x, tab_s[:, im])
            if q == 0:
                t_re = u_re[:slots] + u_re[slots:]
                t_im = u_im[:slots] + u_im[slots:]
            else:
                t_re = u_re[:slots] - u_re[slots:]
                t_im = u_im[:slots] - u_im[slots:]
            for cols, prod in (
                (re, slip_re * t_re - slip_im * t_im),
                (im, slip_re * t_im + slip_im * t_re),
            ):
                hi, lo = hilo(prod)
                total = nn(seg, hi) + nn(seg, lo)
                for k in range(n_worker):
                    ref = out_refs[k]
                    ref[c, :, cols] = total[k * n_server : (k + 1) * n_server].astype(ref.dtype)


def sum_kernel(n_server, *refs):
    own_ref = refs[0]
    out_refs = refs[-n_server:]
    for c in range(3):
        total = own_ref[c]
        for ref in refs[1:-n_server]:
            total = total + ref[c].astype(F32)
        for j in range(n_server):
            out_refs[j][c : c + 1, :] = total[j : j + 1].astype(out_refs[j].dtype)


def table_kernel(cc_ref, sc_ref, ce_ref, se_ref, co_ref, so_ref, hi_ref, lo_ref, gr_ref, gi_ref):
    half = hi_ref.shape[2]
    quarter = half // 2
    n_time = 2 * half
    wide = 256
    for q, (cf_ref, sf_ref) in enumerate(((ce_ref, se_ref), (co_ref, so_ref))):
        for lc in range(half // wide):
            sl = slice(lc * wide, (lc + 1) * wide)
            cf = cf_ref[:, sl]
            sf = sf_ref[:, sl]

            def table(a, carry):
                ca = cc_ref[pl.ds(a, 1), sl]
                sa = sc_ref[pl.ds(a, 1), sl]
                for base, value in ((0, ca * cf - sa * sf), (quarter, -(sa * cf + ca * sf))):
                    at = pl.ds(pl.multiple_of(base + a * STEP, STEP), STEP)
                    hi, lo = hilo(value)
                    hi_ref[q, at, sl] = hi
                    lo_ref[q, at, sl] = lo
                return carry

            lax.fori_loop(0, quarter // STEP, table, 0)
    shape = gr_ref.shape
    low = math.log(4.0 / n_time)
    high = math.log(0.25)
    period = iota(shape, 0)
    slot = iota(shape, 1)
    freq = jnp.where(slot < quarter, 2 * slot, 2 * (slot - quarter) + 1)
    omega_freq = freq.astype(F32) * (2.0 * math.pi / n_time)
    omega_osc = 2.0 * math.pi * jnp.exp(low + (high - low) * period.astype(F32) / (PERIODS - 1))
    den_real = omega_osc * omega_osc - omega_freq * omega_freq
    den_imag = 2.0 * DAMPING * omega_osc * omega_freq
    weight = jnp.where(freq == 0, 1.0, 2.0) / n_time
    gain = weight * (omega_osc * omega_osc / (den_real * den_real + den_imag * den_imag))
    gr_ref[...] = jnp.where(period < PERIODS, -gain * den_real, weight)
    gi_ref[...] = jnp.where(period < PERIODS, -gain * den_imag, 0.0)


def final_kernel(n_server, *refs):
    spec_refs = refs[:n_server]
    hi_ref, lo_ref, gr_ref, gi_ref, seis_ref, peak_ref = refs[n_server:]
    half = hi_ref.shape[2]
    quarter = half // 2
    spec = spec_refs[0][...]
    for ref in spec_refs[1:]:
        spec = spec + ref[...].astype(F32)
    gr = gr_ref[...]
    gi = gi_ref[...]
    sums = []
    for q in range(2):
        cols = slice(q * quarter, (q + 1) * quarter)
        cols_im = slice(half + q * quarter, half + (q + 1) * quarter)
        lefts = []
        for c in range(3):
            re = spec[c : c + 1, cols]
            im = spec[c : c + 1, cols_im]
            g_re = gr[:, cols]
            g_im = gi[:, cols]
            lefts.append(jnp.concatenate([re * g_re + im * g_im, im * g_re - re * g_im], axis=1))
        hi, lo = hilo(jnp.concatenate(lefts, axis=0))
        first = nn(jnp.concatenate([hi, lo], axis=0), hi_ref[q])
        sums.append(first[: 3 * ROWS] + first[3 * ROWS :] + nn(hi, lo_ref[q]))
    even, odd = sums
    peak = jnp.max(jnp.abs(even) + jnp.abs(odd), axis=1, keepdims=True)
    for c in range(3):
        row = c * ROWS + PERIODS
        seis_ref[c : c + 1, :half] = even[row : row + 1] + odd[row : row + 1]
        seis_ref[c : c + 1, half:] = even[row : row + 1] - odd[row : row + 1]
        column = jnp.broadcast_to(peak[c * ROWS : (c + 1) * ROWS], (ROWS, 128))
        column = jnp.concatenate([column, jnp.zeros((128 - ROWS, 128), F32)], axis=0)
        peak_ref[c : c + 1, :] = column.T[:1, :PERIODS]


def vmem():
    return pl.BlockSpec(memory_space=pltpu.VMEM)


def params(mib):
    return pltpu.CompilerParams(vmem_limit_bytes=mib << 20)


def shards(n_server, n_worker, sgt, ownership, sub_points, moments, slip):
    devices = n_server * n_worker
    n_time = sgt.shape[2]
    half = n_time // 2
    rup_w = sub_points.shape[1]
    sub_dev = sub_points.shape[2]
    n_slip = slip.shape[3]
    capacity = 4 * sub_dev // (3 * n_worker)
    slots = devices * capacity
    width = n_slip + 128
    assert rup_w == n_server and sgt.shape[0] == 128 and slots % 16 == 0

    record = pl.pallas_call(
        functools.partial(pack_kernel, capacity),
        out_shape=jax.ShapeDtypeStruct((devices, capacity, width), BF16),
        in_specs=[vmem()] * 4,
        out_specs=vmem(),
        scratch_shapes=[pltpu.VMEM((slots, width), F32)],
        compiler_params=params(32),
        name="pack",
    )(ownership.reshape(-1, 128), sub_points[0], moments[0], slip[0])
    record = lax.all_to_all(record, ("server", "worker"), split_axis=0, concat_axis=0, tiled=True)

    chunk = (3, n_server, n_time)
    sums = pl.pallas_call(
        functools.partial(owner_kernel, n_worker, n_server),
        out_shape=[jax.ShapeDtypeStruct(chunk, BF16 if k else F32) for k in range(n_worker)],
        in_specs=[vmem(), pl.BlockSpec(memory_space=pl.ANY)] + [vmem()] * 4,
        out_specs=[vmem()] * n_worker,
        scratch_shapes=[
            pltpu.VMEM((slots, width), F32),
            pltpu.VMEM((2, slots, GROUP * PAD), F32),
            pltpu.VMEM((8, slots), jnp.int32),
            pltpu.SMEM((8, slots), jnp.int32),
            pltpu.VMEM((slots, 18, n_time), BF16),
            pltpu.VMEM((half, n_time), BF16),
            pltpu.VMEM((3, slots, n_time), F32),
            pltpu.SemaphoreType.DMA((slots,)),
            pltpu.SemaphoreType.DMA,
        ],
        compiler_params=params(56),
        cost_estimate=pl.CostEstimate(flops=10**10, bytes_accessed=2 * 10**7, transcendentals=0),
        name="owner",
    )(record, sgt, *[jnp.asarray(x) for x in forward_bases(n_time)])

    bases, first = lax.optimization_barrier(
        (tuple(jnp.asarray(x) for x in inverse_bases(n_time)), sums[0])
    )
    tables = pl.pallas_call(
        table_kernel,
        out_shape=[jax.ShapeDtypeStruct((2, half, half), BF16)] * 2
        + [jax.ShapeDtypeStruct((ROWS, half), F32)] * 2,
        in_specs=[vmem()] * 6,
        out_specs=[vmem()] * 4,
        compiler_params=params(24),
        cost_estimate=pl.CostEstimate(flops=10**9, bytes_accessed=10**7, transcendentals=0),
        name="inverse_tables",
    )(*bases)

    arrived = [
        lax.ppermute(sums[k], "worker", [(j, j ^ k) for j in range(n_worker)])
        for k in range(1, n_worker)
    ]
    partial = pl.pallas_call(
        functools.partial(sum_kernel, n_server),
        out_shape=[jax.ShapeDtypeStruct((3, n_time), BF16 if j else F32) for j in range(n_server)],
        in_specs=[vmem()] * n_worker,
        out_specs=[vmem()] * n_server,
        compiler_params=params(16),
        name="worker_sum",
    )(first, *arrived)
    arrived = [
        lax.ppermute(partial[j], "server", [(i, i ^ j) for i in range(n_server)])
        for j in range(1, n_server)
    ]
    seis, peaks = pl.pallas_call(
        functools.partial(final_kernel, n_server),
        out_shape=[
            jax.ShapeDtypeStruct((3, n_time), F32),
            jax.ShapeDtypeStruct((3, PERIODS), F32),
        ],
        in_specs=[vmem()] * (n_server + 4),
        out_specs=[vmem()] * 2,
        compiler_params=params(32),
        name="finish",
    )(partial[0], *arrived, *tables)
    return seis.reshape(1, 1, 3, n_time), peaks.reshape(1, 1, 3, PERIODS)


def solution(mesh):
    placed = (
        P(("server", "worker"), None, None),
        P(),
        P("worker", None, "server"),
        P("worker", None, None, "server"),
        P("worker", None, "server", None),
    )
    return jax.shard_map(
        functools.partial(shards, mesh.shape["server"], mesh.shape["worker"]),
        mesh=mesh,
        in_specs=placed,
        out_specs=(P("worker", "server", None, None), P("worker", "server", None, None)),
        check_vma=False,
    )
```

time: 406 us -> 74.5 us (0.18); the launches traced: 398 us -> 73.8 us
  waiting for transfers between devices: 166 us -> 6.64 us
  local copies, waits for them, and re-layouts: 96.8 us -> 19.7 us
  other arithmetic: 70.9 us -> 0 us
  matrix products: 31.1 us -> 0 us
  Pallas kernels: 0 us -> 24.1 us
  starting transfers between devices: 4.05 us -> 22.6 us
  blocking collectives: 14.3 us -> 0 us
  between operations: 14.7 us -> 0.75 us
    all_to_all x1, waiting for transfers between devices: 136 us -> 0.01 us  [shards(): lax.all_to_all(record, ('server', 'worker'), split_axis=0, concat_axis=0,...]
    gather x4 -> x0, local copies, waits for them, and re-layouts: 46.3 us -> none  [the longest x1 24.9 us: shards(): payload = sgt[safe_rows].reshape(devices, capacity, 18, n_time)]
    mul x3 -> x0, other arithmetic: 35.1 us -> none  [the longest x1 35 us: dft_tables(): -weight[:, None] * jnp.sin(angles.T)]
    another operation x2 -> x0, other arithmetic: 34 us -> none
    dot_general x4 -> x0, matrix products: 31.1 us -> none  [the longest x1 13.3 us: oscillator_peaks(): accel = jnp.dot(stacked, inverse, precision=lax.Precision.HIGHEST) / n_time]
    unnamed x2 -> x0, waiting for transfers between devices: 30 us -> none
    reshape x4 -> x0, local copies, waits for them, and re-layouts: 24.6 us -> none  [the longest x2 23.8 us: shards(): payload = sgt[safe_rows].reshape(devices, capacity, 18, n_time)]
    pallas_call x0 -> x5, Pallas kernels: none -> 24.1 us  [the longest x1 17.1 us: shards(): pl.pallas_call(functools.partial(owner_kernel, n_worker, n_server), out_s...]
  transfers between devices with their start and end apart: 2 -> 11, of which waited for: 2 -> 4; matrix products, arithmetic and copies ran while one was open for 18% -> 19% of each run, Pallas kernels for 0% -> 4%
where the time goes in v1:
time: 74.5 us; the launch traced here: 73.8 us
  Pallas kernels  24.1 us (32%)
  starting transfers between devices  22.6 us (30%)
  local copies, waits for them, and re-layouts  19.7 us (26%)
  waiting for transfers between devices  6.64 us (9%)
  between operations  0.75 us (1%)
    unnamed x26, local copies, waits for them, and re-layouts  19.7 us
    pallas_call x1, Pallas kernels, shards(): pl.pallas_call(functools.partial(owner_kernel, n_worker, n_server), out_s...  17.1 us
    ppermute x7, starting transfers between devices, shards(): lax.ppermute(sums[k], 'worker', [(j, j ^ k) for j in range(n_worker)])  10.9 us
    all_to_all x1, starting transfers between devices, shards(): lax.all_to_all(record, ('server', 'worker'), split_axis=0, concat_axis=0,...  7.3 us
    ppermute x7, waiting for transfers between devices, shards(): lax.ppermute(sums[k], 'worker', [(j, j ^ k) for j in range(n_worker)])  4.94 us
    ppermute x3, starting transfers between devices, shards(): lax.ppermute(partial[j], 'server', [(i, i ^ j) for i in range(n_server)])  4.45 us
    pallas_call x1, Pallas kernels, shards(): pl.pallas_call(table_kernel, out_shape=[jax.ShapeDtypeStruct((2, half, ha...  2.79 us
    pallas_call x1, Pallas kernels, shards(): pl.pallas_call(functools.partial(final_kernel, n_server), out_shape=[jax....  2.17 us
  transfers between devices with their start and end apart: 11, of which 4 were waited for; matrix products, arithmetic and copies ran while one was open for 19% of the time, Pallas kernels for 4%

profile of v1, /device:TPU:0, one launch (start us, length us, event | category | flops | bytes accessed | tf_op | source)
XLA Modules:
  0.0 73.8 jit_solution(14177680554523558921)
XLA Ops:
  0.6 0.7 copy.22
  1.3 0.0 copy-start.1
  1.3 0.9 %copy-done.1 = bf16[1,4,24,512]{3,2,1,0:T(8,128)(2,1)S(1)} copy-done((bf16[1,4,24,512]{3,2,1,0:T(8,128)(2,1)S(1)}, bf16[1,4,24,512]{3,2,1,0:T(8,128)(2,1)}, u32[]{:S(2)}) %copy-start.1) | copy-done | bytes 98328
  2.2 0.0 copy-start.2
  2.2 0.7 copy-done.2
  3.0 0.0 copy-start.3
  3.0 0.7 copy-done.3
  3.6 2.0 %pack.1 = bf16[32,4,640]{2,1,0:T(4,128)(2,1)} custom-call(s32[32,128]{1,0:T(8,128)S(1)} %bitcast.11, s32[4,24]{1,0:T(4,128)S(1)} %bitcast.12, f32[4,6,24]{2,1,0:T(8,128)S(1)} %bitcast.9, bf16[4,24,512]{2,1,0:T(8,128)(2,1)S(1)} %bitcast.8), custom_call_target="tpu_custom_call" | custom-call | tf_op jit(solution)/shard_map/pack/pallas_call | solution.py:324
  5.6 7.3 %all-to-all-start = ((bf16[32,4,640]{2,1,0:T(4,128)(2,1)}), bf16[32,4,640]{2,1,0:T(4,128)(2,1)S(1)}, u32[]{:S(2)}, u32[]{:S(2)}) async-start(bf16[32,4,640]{2,1,0:T(4,128)(2,1)} %pack.1), calls=%async_computation | async-start | bytes 327680 | tf_op jit(solution)/shard_map/all_to_all | solution.py:333
  12.9 13.9 %copy.18.sgt_ref = bf16[128,18,2048]{2,1,0:T(8,128)(2,1)} copy(bf16[128,18,2048]{2,0,1:T(8,128)(2,1)} %param.15) | data formatting | bytes 18874368 | tf_op args[0]
  26.9 0.0 copy-start.4
  26.9 0.0 copy-start.5
  26.9 0.0 copy-start.6
  26.9 0.0 copy-start.7
  26.9 0.0 copy-start.8
  26.9 0.0 copy-start.9
  26.9 0.0 all-to-all-done.rec_ref
  26.9 0.0 copy-start.10
  26.9 0.7 copy-done.10
  27.6 17.1 %owner.1 = (f32[3,4,2048]{2,1,0:T(4,128)}, bf16[3,4,2048]{2,1,0:T(4,128)(2,1)}, bf16[3,4,2048]{2,1,0:T(4,128)(2,1)}, bf16[3,4,2048]{2,1,0:T(4,128)(2,1)}, bf16[3...) custom-call(bf16[32,4,640]{2,1,0:T(4,128)(2,1)} %copy-done.10, ...), custom_call_target="tpu_custom_call" | custom-call | flops 10000000000 | bytes 20000000 | tf_op jit(solution)/shard_map/owner/pallas_call | solution.py:336
  44.7 0.3 collective-permute-start
  45.0 6.1 %collective-permute-start.1 = (bf16[3,4,2048]{2,1,0:T(4,128)(2,1)}, bf16[3,4,2048]{2,1,0:T(4,128)(2,1)S(1)}, u32[]{:S(2)}, u32[]{:S(2)}) collective-permute-start(bf16[3,4,2048]{2,1,0:T(4,128)(2,1)} %get-tuple-element.30), channel_id=1, source_target_pairs={{0,2},{1,3},{2,0},{3,1},{4,6},{5,7},{6,4},{7,5},{8,10},{9,11},{10,... | collective-permute-start | bytes 147464 | tf_op jit(solution)/shard_map/ppermute | solution.py:372
  51.1 0.0 collective-permute-start.2
  51.1 1.3 %collective-permute-start.3 = (bf16[3,4,2048]{2,1,0:T(4,128)(2,1)}, bf16[3,4,2048]{2,1,0:T(4,128)(2,1)S(1)}, u32[]{:S(2)}, u32[]{:S(2)}) collective-permute-start(bf16[3,4,2048]{2,1,0:T(4,128)(2,1)} %get-tuple-element.32), channel_id=1, source_target_pairs={{0,4},{1,5},{2,6},{3,7},{4,0},{5,1},{6,2},{7,3},{8,12},{9,13},{10,... | collective-permute-start | bytes 147464 | tf_op jit(solution)/shard_map/ppermute | solution.py:372
  52.4 0.2 collective-permute-start.4
  52.6 0.0 collective-permute-done.refs_1_
  52.6 2.7 %collective-permute-start.5 = (bf16[3,4,2048]{2,1,0:T(4,128)(2,1)}, bf16[3,4,2048]{2,1,0:T(4,128)(2,1)S(1)}, u32[]{:S(2)}, u32[]{:S(2)}) collective-permute-start(bf16[3,4,2048]{2,1,0:T(4,128)(2,1)} %get-tuple-element.34), channel_id=1, source_target_pairs={{0,6},{1,7},{2,4},{3,5},{4,2},{5,3},{6,0},{7,1},{8,14},{9,15},{10,... | collective-permute-start | bytes 147464 | tf_op jit(solution)/shard_map/ppermute | solution.py:372
  55.3 0.0 collective-permute-done.1.refs_2_
  55.3 0.2 collective-permute-start.6
  55.5 0.0 collective-permute-done.2.refs_3_
  55.5 0.0 collective-permute-done.3.refs_4_
  55.5 1.1 %collective-permute-done.4.refs_5_ = bf16[3,4,2048]{2,1,0:T(4,128)(2,1)S(1)} collective-permute-done((bf16[3,4,2048]{2,1,0:T(4,128)(2,1)}, bf16[3,4,2048]{2,1,0:T(4,128)(2,1)S(1)}, u32[]{:S(2)}, u32[]{:S(2)}) %collective-permute-start.4) | collective-permute-done | bytes 49184 | tf_op jit(solution)/shard_map/ppermute | solution.py:372
  56.6 1.4 %collective-permute-done.5.refs_6_ = bf16[3,4,2048]{2,1,0:T(4,128)(2,1)S(1)} collective-permute-done((bf16[3,4,2048]{2,1,0:T(4,128)(2,1)}, bf16[3,4,2048]{2,1,0:T(4,128)(2,1)S(1)}, u32[]{:S(2)}, u32[]{:S(2)}) %collective-permute-start.5) | collective-permute-done | bytes 49184 | tf_op jit(solution)/shard_map/ppermute | solution.py:372
  58.0 2.4 %collective-permute-done.6.refs_7_ = bf16[3,4,2048]{2,1,0:T(4,128)(2,1)S(1)} collective-permute-done((bf16[3,4,2048]{2,1,0:T(4,128)(2,1)}, bf16[3,4,2048]{2,1,0:T(4,128)(2,1)S(1)}, u32[]{:S(2)}, u32[]{:S(2)}) %collective-permute-start.6) | collective-permute-done | bytes 49184 | tf_op jit(solution)/shard_map/ppermute | solution.py:372
  60.5 0.0 copy-start
  60.5 0.9 %copy-done = f32[3,4,2048]{2,1,0:T(4,128)S(1)} copy-done((f32[3,4,2048]{2,1,0:T(4,128)S(1)}, f32[3,4,2048]{2,1,0:T(4,128)}, u32[]{:S(2)}) %copy-start) | copy-done | bytes 98328
  61.4 0.1 worker_sum.1
  61.5 1.2 %collective-permute-start.7 = (bf16[3,2048]{1,0:T(4,128)(2,1)S(1)}, bf16[3,2048]{1,0:T(4,128)(2,1)S(1)}, u32[]{:S(2)}, u32[]{:S(2)}) collective-permute-start(bf16[3,2048]{1,0:T(4,128)(2,1)S(1)} %get-tuple-element.37), channel_id=1, source_target_pairs={{0,8},{8,0},{16,24},{24,16},{1,9},{9,1},{17,25},{25,17},{2,10},{10... | collective-permute-start | bytes 36872 | tf_op jit(solution)/shard_map/ppermute | solution.py:384
  62.7 2.2 %collective-permute-start.8 = (bf16[3,2048]{1,0:T(4,128)(2,1)S(1)}, bf16[3,2048]{1,0:T(4,128)(2,1)S(1)}, u32[]{:S(2)}, u32[]{:S(2)}) collective-permute-start(bf16[3,2048]{1,0:T(4,128)(2,1)S(1)} %get-tuple-element.38), channel_id=1, source_target_pairs={{0,16},{8,24},{16,0},{24,8},{1,17},{9,25},{17,1},{25,9},{2,18},{10... | collective-permute-start | bytes 36872 | tf_op jit(solution)/shard_map/ppermute | solution.py:384
  64.9 1.0 %collective-permute-start.9 = (bf16[3,2048]{1,0:T(4,128)(2,1)S(1)}, bf16[3,2048]{1,0:T(4,128)(2,1)S(1)}, u32[]{:S(2)}, u32[]{:S(2)}) collective-permute-start(bf16[3,2048]{1,0:T(4,128)(2,1)S(1)} %get-tuple-element.39), channel_id=1, source_target_pairs={{0,24},{8,16},{16,8},{24,0},{1,25},{9,17},{17,9},{25,1},{2,26},{10... | collective-permute-start | bytes 36872 | tf_op jit(solution)/shard_map/ppermute | solution.py:384
  65.9 0.0 copy-done.4
  65.9 0.0 copy-done.5
  65.9 0.0 copy-done.6
  65.9 0.0 copy-done.7
  65.9 0.0 copy-done.8
  65.9 0.0 copy-done.9
  66.0 2.8 %inverse_tables.1 = (bf16[2,1024,1024]{2,1,0:T(8,128)(2,1)S(1)}, bf16[2,1024,1024]{2,1,0:T(8,128)(2,1)S(1)}, f32[48,1024]{1,0:T(8,128)S(1)}, f32[48,1024]{1,0:T(8,128)S(1)}) custom-call(f32[16,1024]{1,0:T(8,128)S(1)} %copy-done.9, f32[16,1024]{1,0:T(8,128)S(1)} %copy-done.8, f32[32,1024]{1,0:T(8,128)S(1)} %copy-done.7, f32[32,1024]{1,0:T(8,128)S(1)} %copy-done.6, ...), custom_call_target="tpu_custom_call" | custom-call | flops 1000000000 | bytes 10000000 | tf_op jit(solution)/shard_map/inverse_tables/pallas_call | solution.py:360
  68.8 0.0 collective-permute-done.7.refs_1_
  68.8 0.0 collective-permute-done.8.refs_2_
  68.8 1.7 %collective-permute-done.9.refs_3_ = bf16[3,2048]{1,0:T(4,128)(2,1)S(1)} collective-permute-done((bf16[3,2048]{1,0:T(4,128)(2,1)S(1)}, bf16[3,2048]{1,0:T(4,128)(2,1)S(1)}, u32[]{:S(2)}, u32[]{:S(2)}) %collective-permute-start.9) | collective-permute-done | bytes 12320 | tf_op jit(solution)/shard_map/ppermute | solution.py:384
  70.5 2.2 %finish.1 = (f32[3,2048]{1,0:T(4,128)S(1)}, f32[3,44]{1,0:T(4,128)S(1)}) custom-call(f32[3,2048]{1,0:T(4,128)S(1)} %get-tuple-element.36.refs_0_, bf16[3,2048]{1,0:T(4,128)(2,1)S(1)} %collective-permute-done.7.refs_1_, bf16[3,2048]{1,0:T(4,128)(2,1)S(1)} %collective-permute-done.8.refs_2_, bf16[3,2048]{1,0:T(4,128)(2,1)S(1)} %collective-permute-done.9.refs_3_, ...), custom_call_target="tpu_custom_call" | custom-call | tf_op jit(solution)/shard_map/finish/pallas_call | solution.py:387
  72.6 0.6 copy.19
  73.3 0.6 copy.20
Async XLA Ops:
  1.3 0.9 %copy-start.1 = (bf16[1,4,24,512]{3,2,1,0:T(8,128)(2,1)S(1)}, bf16[1,4,24,512]{3,2,1,0:T(8,128)(2,1)}, u32[]{:S(2)}) copy-start(bf16[1,4,24,512]{3,2,1,0:T(8,128)(2,1)} %param.19) | copy-start | bytes 294916
  2.2 0.7 copy-start.2
  3.0 0.7 copy-start.3
  5.6 21.3 %all-to-all-start = ((bf16[32,4,640]{2,1,0:T(4,128)(2,1)}), bf16[32,4,640]{2,1,0:T(4,128)(2,1)S(1)}, u32[]{:S(2)}, u32[]{:S(2)}) async-start(bf16[32,4,640]{2,1,0:T(4,128)(2,1)} %pack.1), calls=%async_computation | async-start | bytes 327680 | tf_op jit(solution)/shard_map/all_to_all | solution.py:333
  26.9 39.1 %copy-start.4 = (f32[32,1024]{1,0:T(8,128)S(1)}, f32[32,1024]{1,0:T(8,128)}, u32[]{:S(2)}) copy-start(f32[32,1024]{1,0:T(8,128)} %constant.29.clone.so_ref) | copy-start | bytes 393220
  26.9 39.1 %copy-start.5 = (f32[32,1024]{1,0:T(8,128)S(1)}, f32[32,1024]{1,0:T(8,128)}, u32[]{:S(2)}) copy-start(f32[32,1024]{1,0:T(8,128)} %constant.28.clone.co_ref) | copy-start | bytes 393220
  26.9 39.1 %copy-start.6 = (f32[32,1024]{1,0:T(8,128)S(1)}, f32[32,1024]{1,0:T(8,128)}, u32[]{:S(2)}) copy-start(f32[32,1024]{1,0:T(8,128)} %constant.27.clone.se_ref) | copy-start | bytes 393220
  26.9 39.1 %copy-start.7 = (f32[32,1024]{1,0:T(8,128)S(1)}, f32[32,1024]{1,0:T(8,128)}, u32[]{:S(2)}) copy-start(f32[32,1024]{1,0:T(8,128)} %constant.26.clone.ce_ref) | copy-start | bytes 393220
  26.9 39.1 %copy-start.8 = (f32[16,1024]{1,0:T(8,128)S(1)}, f32[16,1024]{1,0:T(8,128)}, u32[]{:S(2)}) copy-start(f32[16,1024]{1,0:T(8,128)} %constant.25.clone.sc_ref) | copy-start | bytes 196612
  26.9 39.1 %copy-start.9 = (f32[16,1024]{1,0:T(8,128)S(1)}, f32[16,1024]{1,0:T(8,128)}, u32[]{:S(2)}) copy-start(f32[16,1024]{1,0:T(8,128)} %constant.24.clone.cc_ref) | copy-start | bytes 196612
  26.9 0.7 copy-start.10
  44.7 8.0 %collective-permute-start = (bf16[3,4,2048]{2,1,0:T(4,128)(2,1)}, bf16[3,4,2048]{2,1,0:T(4,128)(2,1)S(1)}, u32[]{:S(2)}, u32[]{:S(2)}) collective-permute-start(bf16[3,4,2048]{2,1,0:T(4,128)(2,1)} %get-tuple-element.29), channel_id=1, source_target_pairs={{0,1},{1,0},{2,3},{3,2},{4,5},{5,4},{6,7},{7,6},{8,9},{9,8},{10,11... | collective-permute-start | bytes 147464 | tf_op jit(solution)/shard_map/ppermute | solution.py:372
  45.0 10.4 %collective-permute-start.1 = (bf16[3,4,2048]{2,1,0:T(4,128)(2,1)}, bf16[3,4,2048]{2,1,0:T(4,128)(2,1)S(1)}, u32[]{:S(2)}, u32[]{:S(2)}) collective-permute-start(bf16[3,4,2048]{2,1,0:T(4,128)(2,1)} %get-tuple-element.30), channel_id=1, source_target_pairs={{0,2},{1,3},{2,0},{3,1},{4,6},{5,7},{6,4},{7,5},{8,10},{9,11},{10,... | collective-permute-start | bytes 147464 | tf_op jit(solution)/shard_map/ppermute | solution.py:372
  51.1 4.4 %collective-permute-start.2 = (bf16[3,4,2048]{2,1,0:T(4,128)(2,1)}, bf16[3,4,2048]{2,1,0:T(4,128)(2,1)S(1)}, u32[]{:S(2)}, u32[]{:S(2)}) collective-permute-start(bf16[3,4,2048]{2,1,0:T(4,128)(2,1)} %get-tuple-element.31), channel_id=1, source_target_pairs={{0,3},{1,2},{2,1},{3,0},{4,7},{5,6},{6,5},{7,4},{8,11},{9,10},{10,... | collective-permute-start | bytes 147464 | tf_op jit(solution)/shard_map/ppermute | solution.py:372
  51.1 4.4 %collective-permute-start.3 = (bf16[3,4,2048]{2,1,0:T(4,128)(2,1)}, bf16[3,4,2048]{2,1,0:T(4,128)(2,1)S(1)}, u32[]{:S(2)}, u32[]{:S(2)}) collective-permute-start(bf16[3,4,2048]{2,1,0:T(4,128)(2,1)} %get-tuple-element.32), channel_id=1, source_target_pairs={{0,4},{1,5},{2,6},{3,7},{4,0},{5,1},{6,2},{7,3},{8,12},{9,13},{10,... | collective-permute-start | bytes 147464 | tf_op jit(solution)/shard_map/ppermute | solution.py:372
  52.4 4.2 %collective-permute-start.4 = (bf16[3,4,2048]{2,1,0:T(4,128)(2,1)}, bf16[3,4,2048]{2,1,0:T(4,128)(2,1)S(1)}, u32[]{:S(2)}, u32[]{:S(2)}) collective-permute-start(bf16[3,4,2048]{2,1,0:T(4,128)(2,1)} %get-tuple-element.33), channel_id=1, source_target_pairs={{0,5},{1,4},{2,7},{3,6},{4,1},{5,0},{6,3},{7,2},{8,13},{9,12},{10,... | collective-permute-start | bytes 147464 | tf_op jit(solution)/shard_map/ppermute | solution.py:372
  52.6 5.4 %collective-permute-start.5 = (bf16[3,4,2048]{2,1,0:T(4,128)(2,1)}, bf16[3,4,2048]{2,1,0:T(4,128)(2,1)S(1)}, u32[]{:S(2)}, u32[]{:S(2)}) collective-permute-start(bf16[3,4,2048]{2,1,0:T(4,128)(2,1)} %get-tuple-element.34), channel_id=1, source_target_pairs={{0,6},{1,7},{2,4},{3,5},{4,2},{5,3},{6,0},{7,1},{8,14},{9,15},{10,... | collective-permute-start | bytes 147464 | tf_op jit(solution)/shard_map/ppermute | solution.py:372
  55.3 5.1 %collective-permute-start.6 = (bf16[3,4,2048]{2,1,0:T(4,128)(2,1)}, bf16[3,4,2048]{2,1,0:T(4,128)(2,1)S(1)}, u32[]{:S(2)}, u32[]{:S(2)}) collective-permute-start(bf16[3,4,2048]{2,1,0:T(4,128)(2,1)} %get-tuple-element.35), channel_id=1, source_target_pairs={{0,7},{1,6},{2,5},{3,4},{4,3},{5,2},{6,1},{7,0},{8,15},{9,14},{10,... | collective-permute-start | bytes 147464 | tf_op jit(solution)/shard_map/ppermute | solution.py:372
  60.5 0.9 %copy-start = (f32[3,4,2048]{2,1,0:T(4,128)S(1)}, f32[3,4,2048]{2,1,0:T(4,128)}, u32[]{:S(2)}) copy-start(f32[3,4,2048]{2,1,0:T(4,128)} %get-tuple-element.28.refs_0_) | copy-start | bytes 294916
  61.5 7.3 %collective-permute-start.7 = (bf16[3,2048]{1,0:T(4,128)(2,1)S(1)}, bf16[3,2048]{1,0:T(4,128)(2,1)S(1)}, u32[]{:S(2)}, u32[]{:S(2)}) collective-permute-start(bf16[3,2048]{1,0:T(4,128)(2,1)S(1)} %get-tuple-element.37), channel_id=1, source_target_pairs={{0,8},{8,0},{16,24},{24,16},{1,9},{9,1},{17,25},{25,17},{2,10},{10... | collective-permute-start | bytes 36872 | tf_op jit(solution)/shard_map/ppermute | solution.py:384
  62.7 6.1 %collective-permute-start.8 = (bf16[3,2048]{1,0:T(4,128)(2,1)S(1)}, bf16[3,2048]{1,0:T(4,128)(2,1)S(1)}, u32[]{:S(2)}, u32[]{:S(2)}) collective-permute-start(bf16[3,2048]{1,0:T(4,128)(2,1)S(1)} %get-tuple-element.38), channel_id=1, source_target_pairs={{0,16},{8,24},{16,0},{24,8},{1,17},{9,25},{17,1},{25,9},{2,18},{10... | collective-permute-start | bytes 36872 | tf_op jit(solution)/shard_map/ppermute | solution.py:384
  64.9 5.5 %collective-permute-start.9 = (bf16[3,2048]{1,0:T(4,128)(2,1)S(1)}, bf16[3,2048]{1,0:T(4,128)(2,1)S(1)}, u32[]{:S(2)}, u32[]{:S(2)}) collective-permute-start(bf16[3,2048]{1,0:T(4,128)(2,1)S(1)} %get-tuple-element.39), channel_id=1, source_target_pairs={{0,24},{8,16},{16,8},{24,0},{1,25},{9,17},{17,9},{25,1},{2,26},{10... | collective-permute-start | bytes 36872 | tf_op jit(solution)/shard_map/ppermute | solution.py:384

commit v2 on v1

v2 whole, which is shorter than its diff:
```python
import functools
import math

import jax
import jax.numpy as jnp
import numpy as np
from jax import lax
from jax.experimental import pallas as pl
from jax.experimental.pallas import tpu as pltpu
from jax.sharding import PartitionSpec as P

PERIODS = 44
DAMPING = 0.05
ROWS = 48
STEP = 32
PTS = 128
ROW_LANE = 64
RUP_LANE = 96
F32 = jnp.float32
BF16 = jnp.bfloat16


def nn(a, b):
    return lax.dot_general(a, b, (((1,), (0,)), ((), ())), preferred_element_type=F32)


def nt(a, b):
    return lax.dot_general(a, b, (((1,), (1,)), ((), ())), preferred_element_type=F32)


def iota(shape, dim):
    return lax.broadcasted_iota(jnp.int32, shape, dim)


def hilo(x):
    hi = x.astype(BF16)
    return hi, (x - hi.astype(F32)).astype(BF16)


def angle(product, n_time):
    return (2.0 * math.pi / n_time) * (product % n_time)


def forward_bases(n_time):
    half = n_time // 2
    quarter = half // 2
    freq = np.concatenate([2 * np.arange(quarter), 2 * np.arange(quarter) + 1])
    coarse = angle(np.arange(half // STEP)[:, None] * STEP * freq[None, :], n_time)
    fine = angle(np.arange(STEP)[:, None] * freq[None, :], n_time)
    return np.concatenate([f(x) for x in (coarse, fine) for f in (np.cos, np.sin)]).astype(np.float32)


def inverse_bases(n_time):
    half = n_time // 2
    quarter = half // 2
    time = np.arange(half)
    coarse = angle(np.arange(quarter // STEP)[:, None] * 2 * STEP * time[None, :], n_time)
    even = angle(np.arange(STEP)[:, None] * 2 * time[None, :], n_time)
    odd = angle((np.arange(STEP)[:, None] * 2 + 1) * time[None, :], n_time)
    return [
        np.concatenate([f(x) for x in (coarse, fine) for f in (np.cos, np.sin)]).astype(np.float32)
        for fine in (even, odd)
    ]


def pack_kernel(capacity, own_ref, pts_ref, mom_ref, slip_ref, out_ref, scr):
    devices = out_ref.shape[0]
    slots = devices * capacity
    rup_w, sub = pts_ref.shape
    n_slip = slip_ref.shape[2]
    own = own_ref[...]
    blocks = own.shape[0]
    both = jnp.concatenate([own // PTS, own % PTS], axis=0).astype(F32).astype(BF16)
    spread = iota((128, 6), 0)
    comp = iota((128, 6), 1)
    spread_hi = (spread == comp).astype(F32).astype(BF16)
    spread_lo = (spread == comp + 6).astype(F32).astype(BF16)
    earlier = (iota((sub, sub), 0) < iota((sub, sub), 1)).astype(F32).astype(BF16)
    carry = jnp.zeros((devices, 1), F32)
    slip_acc = jnp.zeros((slots, n_slip), F32)
    tail_acc = jnp.zeros((slots, 128), F32)
    lane = iota((slots, 128), 1)
    for r in range(rup_w):
        p = pts_ref[r : r + 1, :]
        in_lane = (iota((128, sub), 0) == p % 128).astype(F32).astype(BF16)
        found = nn(both, in_lane)
        in_block = (iota((blocks, sub), 0) == p // 128).astype(F32)
        dev = jnp.sum(found[:blocks] * in_block, axis=0, keepdims=True)
        loc = jnp.sum(found[blocks:] * in_block, axis=0, keepdims=True)
        onehot = (iota((devices, sub), 0).astype(F32) == dev).astype(F32)
        before = nn(onehot.astype(BF16), earlier) + carry
        rank = jnp.sum(before * onehot, axis=0, keepdims=True)
        carry = carry + jnp.sum(onehot, axis=1, keepdims=True)
        target = dev * capacity + rank
        pick = (iota((slots, sub), 0).astype(F32) == target).astype(F32)
        pick16 = pick.astype(BF16)
        mom = jnp.concatenate([mom_ref[m, r : r + 1, :] for m in range(6)], axis=0)
        hi, lo = hilo(mom)
        expanded = nn(spread_hi, hi) + nn(spread_lo, lo)
        slip_acc = slip_acc + nn(pick16, slip_ref[r])
        tail = nt(pick16, expanded.astype(BF16))
        row = jnp.sum(pick * loc, axis=1, keepdims=True)
        rup = jnp.sum(pick, axis=1, keepdims=True) * float(r)
        tail = tail + jnp.where(lane == ROW_LANE, row, 0.0) + jnp.where(lane == RUP_LANE, rup, 0.0)
        tail_acc = tail_acc + tail
    scr[:, :n_slip] = slip_acc
    scr[:, n_slip:] = tail_acc
    for d in range(devices):
        out_ref[d] = scr[d * capacity : (d + 1) * capacity, :].astype(BF16)


def owner_kernel(stages, rec_ref, sgt_ref, tab_ref, *refs):
    first = stages[0][1]
    out_refs = refs[:first]
    rec_s, x_s, sgt_s, tab_s, sems = refs[first:]
    devices, capacity, width = rec_ref.shape
    slots = devices * capacity
    n_time = sgt_ref.shape[2]
    half = n_time // 2
    quarter = half // 2
    n_slip = width - 128
    wide = 512

    def rows_copy(c):
        at = slice(6 * c, 6 * c + 6)
        return pltpu.make_async_copy(sgt_ref.at[at], sgt_s.at[at], sems.at[c])

    def table_copy(i):
        at = slice(i * quarter, (i + 1) * quarter)
        return pltpu.make_async_copy(tab_ref.at[:, at], tab_s.at[:, at], sems.at[3 + i])

    for c in range(3):
        rows_copy(c).start()
    for i in (0, 2, 1, 3):
        table_copy(i).start()
    for d in range(devices):
        rec_s[d * capacity : (d + 1) * capacity, :] = rec_ref[d].astype(F32)
    tail = rec_s[:, n_slip:]
    row = tail[:, ROW_LANE : ROW_LANE + 1]
    here = iota((slots, PTS), 1).astype(F32) == row
    left = jnp.concatenate(
        [
            jnp.concatenate(
                [jnp.where(here, tail[:, 6 * p + m : 6 * p + m + 1], 0.0).astype(BF16) for m in range(6)],
                axis=1,
            )
            for p in range(2)
        ],
        axis=0,
    )
    for c in range(3):
        rows_copy(c).wait()
        for n in range(n_time // wide):
            rows = sgt_s[6 * c : 6 * c + 6, :, n * wide : (n + 1) * wide].reshape(6 * PTS, wide)
            out = nn(left, rows)
            h, at = divmod(n * wide, half)
            x_s[c, h * slots : (h + 1) * slots, at : at + wide] = (out[:slots] + out[slots:]).astype(BF16)

    ruptures = math.prod(radix for _, radix, _, _ in stages)
    shape = (ruptures, slots)
    rup = nt((iota((8, 128), 1) == RUP_LANE).astype(F32).astype(BF16), tail.astype(BF16))[:1].astype(jnp.int32)
    worker = (iota((1, slots), 1) // capacity) % lax.axis_size("worker")
    apart = {"worker": worker ^ lax.axis_index("worker"), "server": rup ^ lax.axis_index("server")}
    where_to = jnp.zeros((1, slots), jnp.int32)
    for axis, radix, shift, _ in stages:
        where_to = where_to * radix + ((apart[axis] >> shift) & (radix - 1))
    seg = (iota(shape, 0) == where_to).astype(F32).astype(BF16)
    slip = rec_s[:, :n_slip].astype(BF16)
    part = ruptures // first
    for q in range(2):
        re = slice(q * quarter, (q + 1) * quarter)
        im = slice(half + q * quarter, half + (q + 1) * quarter)
        table_copy(q).wait()
        table_copy(q + 2).wait()
        slip_re = nn(slip, tab_s[:n_slip, re])
        slip_im = nn(slip, tab_s[:n_slip, im])
        for c in range(3):
            x = x_s[c]
            u_re = nn(x, tab_s[:, re])
            u_im = nn(x, tab_s[:, im])
            if q == 0:
                t_re = u_re[:slots] + u_re[slots:]
                t_im = u_im[:slots] + u_im[slots:]
            else:
                t_re = u_re[:slots] - u_re[slots:]
                t_im = u_im[:slots] - u_im[slots:]
            for cols, prod in (
                (re, slip_re * t_re - slip_im * t_im),
                (im, slip_re * t_im + slip_im * t_re),
            ):
                hi, lo = hilo(prod)
                total = nn(seg, hi) + nn(seg, lo)
                for k in range(first):
                    ref = out_refs[k]
                    ref[c, :, cols] = total[k * part : (k + 1) * part].astype(ref.dtype)


def sum_kernel(radix, *refs):
    own_ref = refs[0]
    out_refs = refs[-radix:]
    part = out_refs[0].shape[1]
    for c in range(3):
        total = own_ref[c]
        for ref in refs[1:-radix]:
            total = total + ref[c].astype(F32)
        for k in range(radix):
            out_refs[k][c] = total[k * part : (k + 1) * part].astype(out_refs[k].dtype)


def forward_table_kernel(base_ref, tab_ref):
    half = tab_ref.shape[0]
    count = half // STEP
    wide = 256
    for lc in range(half // wide):
        sl = slice(lc * wide, (lc + 1) * wide)
        sl2 = slice(half + lc * wide, half + (lc + 1) * wide)
        cb = base_ref[2 * count : 2 * count + STEP, sl]
        sb = base_ref[2 * count + STEP :, sl]

        def table(a, carry):
            ca = base_ref[pl.ds(a, 1), sl]
            sa = base_ref[pl.ds(count + a, 1), sl]
            at = pl.ds(pl.multiple_of(a * STEP, STEP), STEP)
            tab_ref[at, sl] = (ca * cb - sa * sb).astype(BF16)
            tab_ref[at, sl2] = (-(sa * cb + ca * sb)).astype(BF16)
            return carry

        lax.fori_loop(0, half // STEP, table, 0)


def inverse_table_kernel(base_ref, hi_ref, lo_ref):
    half = hi_ref.shape[0]
    quarter = half // 2
    count = quarter // STEP
    wide = 256
    for lc in range(half // wide):
        sl = slice(lc * wide, (lc + 1) * wide)
        cf = base_ref[2 * count : 2 * count + STEP, sl]
        sf = base_ref[2 * count + STEP :, sl]

        def table(a, carry):
            ca = base_ref[pl.ds(a, 1), sl]
            sa = base_ref[pl.ds(count + a, 1), sl]
            for base, value in ((0, ca * cf - sa * sf), (quarter, -(sa * cf + ca * sf))):
                at = pl.ds(pl.multiple_of(base + a * STEP, STEP), STEP)
                hi, lo = hilo(value)
                hi_ref[at, sl] = hi
                lo_ref[at, sl] = lo
            return carry

        lax.fori_loop(0, count, table, 0)


def gain_kernel(gr_ref, gi_ref):
    half = gr_ref.shape[1]
    quarter = half // 2
    n_time = 2 * half
    shape = gr_ref.shape
    low = math.log(4.0 / n_time)
    high = math.log(0.25)
    period = iota(shape, 0)
    slot = iota(shape, 1)
    freq = jnp.where(slot < quarter, 2 * slot, 2 * (slot - quarter) + 1)
    omega_freq = freq.astype(F32) * (2.0 * math.pi / n_time)
    omega_osc = 2.0 * math.pi * jnp.exp(low + (high - low) * period.astype(F32) / (PERIODS - 1))
    den_real = omega_osc * omega_osc - omega_freq * omega_freq
    den_imag = 2.0 * DAMPING * omega_osc * omega_freq
    weight = jnp.where(freq == 0, 1.0, 2.0) / n_time
    gain = weight * (omega_osc * omega_osc / (den_real * den_real + den_imag * den_imag))
    gr_ref[...] = jnp.where(period < PERIODS, -gain * den_real, weight)
    gi_ref[...] = jnp.where(period < PERIODS, -gain * den_imag, 0.0)


def final_kernel(count, *refs):
    spec_refs = refs[:count]
    *tables, gr_ref, gi_ref, seis_ref, peak_ref = refs[count:]
    half = gr_ref.shape[1]
    quarter = half // 2
    spec = []
    for c in range(3):
        total = spec_refs[0][c]
        for ref in spec_refs[1:]:
            total = total + ref[c].astype(F32)
        spec.append(total)
    gr = gr_ref[...]
    gi = gi_ref[...]
    sums = []
    for q in range(2):
        cols = slice(q * quarter, (q + 1) * quarter)
        cols_im = slice(half + q * quarter, half + (q + 1) * quarter)
        lefts = []
        for c in range(3):
            re = spec[c][:, cols]
            im = spec[c][:, cols_im]
            g_re = gr[:, cols]
            g_im = gi[:, cols]
            lefts.append(jnp.concatenate([re * g_re + im * g_im, im * g_re - re * g_im], axis=1))
        hi, lo = hilo(jnp.concatenate(lefts, axis=0))
        hi_ref, lo_ref = tables[2 * q : 2 * q + 2]
        first = nn(jnp.concatenate([hi, lo], axis=0), hi_ref[...])
        sums.append(first[: 3 * ROWS] + first[3 * ROWS :] + nn(hi, lo_ref[...]))
    even, odd = sums
    peak = jnp.max(jnp.abs(even) + jnp.abs(odd), axis=1, keepdims=True)
    for c in range(3):
        row = c * ROWS + PERIODS
        seis_ref[c, :, :half] = even[row : row + 1] + odd[row : row + 1]
        seis_ref[c, :, half:] = even[row : row + 1] - odd[row : row + 1]
        column = jnp.broadcast_to(peak[c * ROWS : (c + 1) * ROWS], (ROWS, 128))
        column = jnp.concatenate([column, jnp.zeros((128 - ROWS, 128), F32)], axis=0)
        peak_ref[c] = column.T[:1, :PERIODS]


def vmem():
    return pl.BlockSpec(memory_space=pltpu.VMEM)


def params(mib):
    return pltpu.CompilerParams(vmem_limit_bytes=mib << 20)


def exchange_plan(n_worker, n_server):
    stages = []
    for axis, size in (("worker", n_worker), ("server", n_server)):
        bits = size.bit_length() - 1
        assert size == 1 << bits
        shift = 0
        while shift < bits:
            step = 1 if (bits - shift) % 2 else 2
            stages.append((axis, 1 << step, shift, size))
            shift += step
    return stages


def send(parts, stage):
    axis, radix, shift, size = stage
    return [
        lax.ppermute(parts[k], axis, [(i, i ^ (k << shift)) for i in range(size)])
        for k in range(1, radix)
    ]


def sent_type(stages, i):
    return F32 if i == 0 or i == len(stages) - 1 else BF16


def shards(n_server, n_worker, sgt, ownership, sub_points, moments, slip):
    devices = n_server * n_worker
    n_time = sgt.shape[2]
    half = n_time // 2
    rup_w = sub_points.shape[1]
    sub_dev = sub_points.shape[2]
    n_slip = slip.shape[3]
    capacity = 4 * sub_dev // (3 * n_worker)
    slots = devices * capacity
    width = n_slip + 128
    stages = exchange_plan(n_worker, n_server)
    assert rup_w == n_server and sgt.shape[0] == PTS and slots % 16 == 0

    record = pl.pallas_call(
        functools.partial(pack_kernel, capacity),
        out_shape=jax.ShapeDtypeStruct((devices, capacity, width), BF16),
        in_specs=[vmem()] * 4,
        out_specs=vmem(),
        scratch_shapes=[pltpu.VMEM((slots, width), F32)],
        compiler_params=params(56),
        name="pack",
    )(ownership.reshape(-1, 128), sub_points[0], jnp.transpose(moments[0], (1, 0, 2)), slip[0])
    record = lax.all_to_all(record, ("server", "worker"), split_axis=0, concat_axis=0, tiled=True)

    table = pl.pallas_call(
        forward_table_kernel,
        out_shape=jax.ShapeDtypeStruct((half, n_time), BF16),
        in_specs=[vmem()],
        out_specs=vmem(),
        compiler_params=params(8),
        cost_estimate=pl.CostEstimate(flops=10**9, bytes_accessed=10**7, transcendentals=0),
        name="forward_table",
    )(jnp.asarray(forward_bases(n_time)))
    bases = [jnp.asarray(x) for x in inverse_bases(n_time)]
    inverse = pl.pallas_call(
        inverse_table_kernel,
        out_shape=[jax.ShapeDtypeStruct((half, half), BF16)] * 2,
        in_specs=[vmem()],
        out_specs=[vmem()] * 2,
        compiler_params=params(8),
        cost_estimate=pl.CostEstimate(flops=10**9, bytes_accessed=10**7, transcendentals=0),
        name="inverse_table",
    )
    gain = pl.pallas_call(
        gain_kernel,
        out_shape=[jax.ShapeDtypeStruct((ROWS, half), F32)] * 2,
        out_specs=[vmem()] * 2,
        compiler_params=params(2),
        name="gain",
    )()
    tables = []

    def part_shapes(i):
        count = math.prod(radix for _, radix, _, _ in stages[i + 1 :])
        return [
            jax.ShapeDtypeStruct((3, count, n_time), sent_type(stages, i) if k else F32)
            for k in range(stages[i][1])
        ]

    parts = pl.pallas_call(
        functools.partial(owner_kernel, stages),
        out_shape=part_shapes(0),
        in_specs=[vmem(), pl.BlockSpec(memory_space=pl.ANY), pl.BlockSpec(memory_space=pl.ANY)],
        out_specs=[vmem()] * stages[0][1],
        scratch_shapes=[
            pltpu.VMEM((slots, width), F32),
            pltpu.VMEM((3, 2 * slots, half), BF16),
            pltpu.VMEM((18, PTS, n_time), BF16),
            pltpu.VMEM((half, n_time), BF16),
            pltpu.SemaphoreType.DMA((7,)),
        ],
        compiler_params=params(52),
        cost_estimate=pl.CostEstimate(flops=10**10, bytes_accessed=2 * 10**7, transcendentals=0),
        name="owner",
    )(record, jnp.transpose(sgt, (1, 0, 2)), table)
    arrived = send(parts, stages[0])
    for i in range(1, len(stages)):
        radix = stages[i][1]
        parts = pl.pallas_call(
            functools.partial(sum_kernel, radix),
            out_shape=part_shapes(i),
            in_specs=[vmem()] * (1 + len(arrived)),
            out_specs=[vmem()] * radix,
            compiler_params=params(4),
            name=f"sum_{i}",
        )(parts[0], *arrived)
        arrived = send(parts, stages[i])
        if i >= len(stages) - 2:
            base, own = lax.optimization_barrier((bases[len(tables) // 2], parts[0]))
            pair = inverse(base)
            tables += pair
            own, *pair = lax.optimization_barrier((own, *pair))
            parts = [own]
            tables = tables[:-2] + pair
    count = 1 + len(arrived)
    seis, peaks = pl.pallas_call(
        functools.partial(final_kernel, count),
        out_shape=[
            jax.ShapeDtypeStruct((3, 1, n_time), F32),
            jax.ShapeDtypeStruct((3, 1, PERIODS), F32),
        ],
        in_specs=[vmem()] * (count + 6),
        out_specs=[vmem()] * 2,
        compiler_params=params(20),
        name="finish",
    )(parts[0], *arrived, *tables, *gain)
    return (
        jnp.transpose(seis, (1, 0, 2)).reshape(1, 1, 3, n_time),
        jnp.transpose(peaks, (1, 0, 2)).reshape(1, 1, 3, PERIODS),
    )


def solution(mesh):
    placed = (
        P(("server", "worker"), None, None),
        P(),
        P("worker", None, "server"),
        P("worker", None, None, "server"),
        P("worker", None, "server", None),
    )
    return jax.shard_map(
        functools.partial(shards, mesh.shape["server"], mesh.shape["worker"]),
        mesh=mesh,
        in_specs=placed,
        out_specs=(P("worker", "server", None, None), P("worker", "server", None, None)),
        check_vma=False,
    )
```

time: 74.5 us -> 49.3 us (0.66)
  local copies, waits for them, and re-layouts: 19.7 us -> 2.99 us
  starting transfers between devices: 22.6 us -> 15.8 us
  Pallas kernels: 24.1 us -> 21 us
  waiting for transfers between devices: 6.64 us -> 8.57 us
    unnamed x26 -> x8, local copies, waits for them, and re-layouts: 19.7 us -> 2.99 us
    ppermute x10 -> x7, starting transfers between devices: 15.3 us -> 8.47 us  [send(): lax.ppermute(parts[k], axis, [(i, i ^ k << shift) for i in range(size)])]
    pallas_call x4 -> x8, Pallas kernels: 22.1 us -> 18.1 us  [the longest x1 10.6 us: shards(): pl.pallas_call(functools.partial(owner_kernel, stages), out_shape=part_sh...]
    all_to_all x1, waiting for transfers between devices: 0.01 us -> 3.7 us  [shards(): lax.all_to_all(record, ('server', 'worker'), split_axis=0, concat_axis=0,...]
    ppermute x10 -> x7, waiting for transfers between devices: 6.64 us -> 4.87 us  [send(): lax.ppermute(parts[k], axis, [(i, i ^ k << shift) for i in range(size)])]
    pallas_call x1, Pallas kernels: 2.01 us -> 2.93 us  [shards(): pl.pallas_call(functools.partial(pack_kernel, capacity), out_shape=jax.Sh...]
  transfers between devices with their start and end apart: 11 -> 8, of which waited for: 4 -> 4; matrix products, arithmetic and copies ran while one was open for 19% -> 0% of each run, Pallas kernels for 4% -> 9%
where the time goes in v2:
time: 49.3 us; the launch traced here: 49.1 us
  Pallas kernels  21 us (43%)
  starting transfers between devices  15.8 us (32%)
  waiting for transfers between devices  8.57 us (17%)
  local copies, waits for them, and re-layouts  2.99 us (6%)
  between operations  0.74 us (2%)
    pallas_call x1, Pallas kernels, shards(): pl.pallas_call(functools.partial(owner_kernel, stages), out_shape=part_sh...  10.6 us
    ppermute x7, starting transfers between devices, send(): lax.ppermute(parts[k], axis, [(i, i ^ k << shift) for i in range(size)])  8.47 us
    all_to_all x1, starting transfers between devices, shards(): lax.all_to_all(record, ('server', 'worker'), split_axis=0, concat_axis=0,...  7.3 us
    ppermute x7, waiting for transfers between devices, send(): lax.ppermute(parts[k], axis, [(i, i ^ k << shift) for i in range(size)])  4.87 us
    all_to_all x1, waiting for transfers between devices, shards(): lax.all_to_all(record, ('server', 'worker'), split_axis=0, concat_axis=0,...  3.7 us
    unnamed x8, local copies, waits for them, and re-layouts  2.99 us
    pallas_call x1, Pallas kernels, shards(): pl.pallas_call(functools.partial(pack_kernel, capacity), out_shape=jax.Sh...  2.93 us
    pallas_call x1, Pallas kernels, shards(): pl.pallas_call(functools.partial(final_kernel, count), out_shape=[jax.Sha...  2.75 us
  transfers between devices with their start and end apart: 8, of which 4 were waited for; matrix products, arithmetic and copies ran while one was open for 0% of the time, Pallas kernels for 9%

profile of v2, /device:TPU:0, one launch (start us, length us, event | category | flops | bytes accessed | tf_op | source)
XLA Modules:
  0.0 49.1 jit_solution(5525440697580926723)
XLA Ops:
  0.6 2.9 %pack.1 = bf16[32,4,640]{2,1,0:T(4,128)(2,1)} custom-call(s32[32,128]{1,0:T(8,128)} %bitcast.14, s32[4,24]{1,0:T(4,128)} %bitcast.16, f32[6,4,24]{2,1,0:T(4,128)} %bitcast.15, bf16[4,24,512]{2,1,0:T(8,128)(2,1)} %bitcast.13), custom_call_target="tpu_custom_call" | custom-call | tf_op jit(solution)/shard_map/pack/pallas_call | solution.py:359
  3.6 7.3 %all-to-all-start = ((bf16[32,4,640]{2,1,0:T(4,128)(2,1)}), bf16[32,4,640]{2,1,0:T(4,128)(2,1)S(1)}, u32[]{:S(2)}, u32[]{:S(2)}) async-start(bf16[32,4,640]{2,1,0:T(4,128)(2,1)} %pack.1), calls=%async_computation | async-start | bytes 327680 | tf_op jit(solution)/shard_map/all_to_all | solution.py:368
  10.9 0.0 copy-start.1
  10.9 1.0 %copy-done.1 = f32[128,1024]{1,0:T(8,128)S(1)} copy-done((f32[128,1024]{1,0:T(8,128)S(1)}, f32[128,1024]{1,0:T(8,128)}, u32[]{:S(2)}) %copy-start.1) | copy-done | bytes 524312
  11.9 1.9 %forward_table.1.tab_ref = bf16[1024,2048]{1,0:T(8,128)(2,1)S(1)} custom-call(f32[128,1024]{1,0:T(8,128)S(1)} %copy-done.1), custom_call_target="tpu_custom_call" | custom-call | flops 1000000000 | bytes 10000000 | tf_op jit(solution)/shard_map/forward_table/pallas_call | solution.py:370
  13.8 0.0 copy-start
  13.8 1.9 %copy-done = bf16[1024,2048]{1,0:T(8,128)(2,1)} copy-done((bf16[1024,2048]{1,0:T(8,128)(2,1)}, bf16[1024,2048]{1,0:T(8,128)(2,1)S(1)}, u32[]{:S(2)}) %copy-start) | copy-done | bytes 4194328
  15.7 3.7 %all-to-all-done.rec_ref = bf16[32,4,640]{2,1,0:T(4,128)(2,1)S(1)} async-done(((bf16[32,4,640]{2,1,0:T(4,128)(2,1)}), bf16[32,4,640]{2,1,0:T(4,128)(2,1)S(1)}, u32[]{:S(2)}, u32[]{:S(2)}) %all-to-all-start) | async-done | bytes 163872 | tf_op jit(solution)/shard_map/all_to_all | solution.py:368
  19.4 0.0 copy-start.3
  19.4 10.6 %owner.1 = (f32[3,16,2048]{2,1,0:T(8,128)S(1)}, f32[3,16,2048]{2,1,0:T(8,128)S(1)}) custom-call(bf16[32,4,640]{2,1,0:T(4,128)(2,1)S(1)} %all-to-all-done.rec_ref, bf16[18,128,2048]{2,1,0:T(8,128)(2,1)} %bitcast.17, bf16[1024,2048]{1,0:T(8,128)(2,1)} %copy-done), custom_call_target="tpu_custom_call" | custom-call | flops 10000000000 | bytes 20000000 | tf_op jit(solution)/shard_map/owner/pallas_call | solution.py:405
  30.0 0.4 collective-permute-start
  30.5 0.1 gain.1
  30.6 1.2 %collective-permute-done.refs_1_ = f32[3,16,2048]{2,1,0:T(8,128)S(1)} collective-permute-done((f32[3,16,2048]{2,1,0:T(8,128)S(1)}, f32[3,16,2048]{2,1,0:T(8,128)S(1)}, u32[]{:S(2)}, u32[]{:S(2)}) %collective-permute-start) | collective-permute-done | bytes 393248 | tf_op jit(solution)/shard_map/ppermute | solution.py:337
  31.9 0.0 copy-start.2
  31.9 0.6 %collective-permute-start.1 = (bf16[3,4,2048]{2,1,0:T(4,128)(2,1)S(1)}, bf16[3,4,2048]{2,1,0:T(4,128)(2,1)S(1)}, u32[]{:S(2)}, u32[]{:S(2)}) collective-permute-start(bf16[3,4,2048]{2,1,0:T(4,128)(2,1)S(1)} %get-tuple-element.38), channel_id=1, source_target_pairs={{0,2},{1,3},{2,0},{3,1},{4,6},{5,7},{6,4},{7,5},{8,10},{9,11},{10,... | collective-permute-start | bytes 147464 | tf_op jit(solution)/shard_map/ppermute | solution.py:337
  32.5 1.0 %collective-permute-start.2 = (bf16[3,4,2048]{2,1,0:T(4,128)(2,1)S(1)}, bf16[3,4,2048]{2,1,0:T(4,128)(2,1)S(1)}, u32[]{:S(2)}, u32[]{:S(2)}) collective-permute-start(bf16[3,4,2048]{2,1,0:T(4,128)(2,1)S(1)} %get-tuple-element.39), channel_id=1, source_target_pairs={{0,4},{1,5},{2,6},{3,7},{4,0},{5,1},{6,2},{7,3},{8,12},{9,13},{10,... | collective-permute-start | bytes 147464 | tf_op jit(solution)/shard_map/ppermute | solution.py:337
  33.5 1.9 %collective-permute-start.3 = (bf16[3,4,2048]{2,1,0:T(4,128)(2,1)S(1)}, bf16[3,4,2048]{2,1,0:T(4,128)(2,1)S(1)}, u32[]{:S(2)}, u32[]{:S(2)}) collective-permute-start(bf16[3,4,2048]{2,1,0:T(4,128)(2,1)S(1)} %get-tuple-element.40), channel_id=1, source_target_pairs={{0,6},{1,7},{2,4},{3,5},{4,2},{5,3},{6,0},{7,1},{8,14},{9,15},{10,... | collective-permute-start | bytes 147464 | tf_op jit(solution)/shard_map/ppermute | solution.py:337
  35.5 0.0 copy-done.3
  35.5 1.3 %inverse_table.2 = (bf16[1024,1024]{1,0:T(8,128)(2,1)S(1)}, bf16[1024,1024]{1,0:T(8,128)(2,1)S(1)}) custom-call(f32[96,1024]{1,0:T(8,128)S(1)} %copy-done.3), custom_call_target="tpu_custom_call" | custom-call | flops 1000000000 | bytes 10000000 | tf_op jit(solution)/shard_map/inverse_table/pallas_call | solution.py:435
  36.8 0.0 collective-permute-done.1.refs_1_
  36.8 0.0 collective-permute-done.2.refs_2_
  36.8 1.7 %collective-permute-done.3.refs_3_ = bf16[3,4,2048]{2,1,0:T(4,128)(2,1)S(1)} collective-permute-done((bf16[3,4,2048]{2,1,0:T(4,128)(2,1)S(1)}, bf16[3,4,2048]{2,1,0:T(4,128)(2,1)S(1)}, u32[]{:S(2)}, u32[]{:S(2)}) %collective-permute-start.3) | collective-permute-done | bytes 49184 | tf_op jit(solution)/shard_map/ppermute | solution.py:337
  38.6 0.8 %collective-permute-start.4 = (f32[3,1,2048]{2,1,0:T(1,128)S(1)}, f32[3,1,2048]{2,1,0:T(1,128)S(1)}, u32[]{:S(2)}, u32[]{:S(2)}) collective-permute-start(f32[3,1,2048]{2,1,0:T(1,128)S(1)} %get-tuple-element.47), channel_id=1, source_target_pairs={{0,8},{8,0},{16,24},{24,16},{1,9},{9,1},{17,25},{25,17},{2,10},{10... | collective-permute-start | bytes 73736 | tf_op jit(solution)/shard_map/ppermute | solution.py:337
  39.3 1.3 %collective-permute-start.5 = (f32[3,1,2048]{2,1,0:T(1,128)S(1)}, f32[3,1,2048]{2,1,0:T(1,128)S(1)}, u32[]{:S(2)}, u32[]{:S(2)}) collective-permute-start(f32[3,1,2048]{2,1,0:T(1,128)S(1)} %get-tuple-element.48), channel_id=1, source_target_pairs={{0,16},{8,24},{16,0},{24,8},{1,17},{9,25},{17,1},{25,9},{2,18},{10... | collective-permute-start | bytes 73736 | tf_op jit(solution)/shard_map/ppermute | solution.py:337
  40.7 2.3 %collective-permute-start.6 = (f32[3,1,2048]{2,1,0:T(1,128)S(1)}, f32[3,1,2048]{2,1,0:T(1,128)S(1)}, u32[]{:S(2)}, u32[]{:S(2)}) collective-permute-start(f32[3,1,2048]{2,1,0:T(1,128)S(1)} %get-tuple-element.49), channel_id=1, source_target_pairs={{0,24},{8,16},{16,8},{24,0},{1,25},{9,17},{17,9},{25,1},{2,26},{10... | collective-permute-start | bytes 73736 | tf_op jit(solution)/shard_map/ppermute | solution.py:337
  43.0 0.0 copy-done.2
  43.0 1.3 %inverse_table.3 = (bf16[1024,1024]{1,0:T(8,128)(2,1)S(1)}, bf16[1024,1024]{1,0:T(8,128)(2,1)S(1)}) custom-call(f32[96,1024]{1,0:T(8,128)S(1)} %copy-done.2), custom_call_target="tpu_custom_call" | custom-call | flops 1000000000 | bytes 10000000 | tf_op jit(solution)/shard_map/inverse_table/pallas_call | solution.py:435
  44.4 0.0 collective-permute-done.4.refs_1_
  44.4 0.0 collective-permute-done.5.refs_2_
  44.4 1.9 %collective-permute-done.6.refs_3_ = f32[3,1,2048]{2,1,0:T(1,128)S(1)} collective-permute-done((f32[3,1,2048]{2,1,0:T(1,128)S(1)}, f32[3,1,2048]{2,1,0:T(1,128)S(1)}, u32[]{:S(2)}, u32[]{:S(2)}) %collective-permute-start.6) | collective-permute-done | bytes 24608 | tf_op jit(solution)/shard_map/ppermute | solution.py:337
  46.3 2.7 %finish.1 = (f32[3,1,2048]{2,1,0:T(1,128)}, f32[3,1,44]{2,1,0:T(1,128)}) custom-call(f32[3,1,2048]{2,1,0:T(1,128)S(1)} %get-tuple-element.46.refs_0_, f32[3,1,2048]{2,1,0:T(1,128)S(1)} %collective-permute-done.4.refs_1_, f32[3,1,2048]{2,1,0:T(1,128)S(1)} %collective-permute-done.5.refs_2_, f32[3,1,2048]{2,1,0:T(1,128)S(1)} %collective-permute-done.6.refs_3_, ...), custom_call_target="tpu_custom_call" | custom-call | tf_op jit(solution)/shard_map/finish/pallas_call | solution.py:441
  (2 shorter events, 0.1 us)
Async XLA Ops:
  3.6 15.9 %all-to-all-start = ((bf16[32,4,640]{2,1,0:T(4,128)(2,1)}), bf16[32,4,640]{2,1,0:T(4,128)(2,1)S(1)}, u32[]{:S(2)}, u32[]{:S(2)}) async-start(bf16[32,4,640]{2,1,0:T(4,128)(2,1)} %pack.1), calls=%async_computation | async-start | bytes 327680 | tf_op jit(solution)/shard_map/all_to_all | solution.py:368
  10.9 1.0 %copy-start.1 = (f32[128,1024]{1,0:T(8,128)S(1)}, f32[128,1024]{1,0:T(8,128)}, u32[]{:S(2)}) copy-start(f32[128,1024]{1,0:T(8,128)} %constant.6.clone.base_ref) | copy-start | bytes 1572868
  13.8 2.0 %copy-start = (bf16[1024,2048]{1,0:T(8,128)(2,1)}, bf16[1024,2048]{1,0:T(8,128)(2,1)S(1)}, u32[]{:S(2)}) copy-start(bf16[1024,2048]{1,0:T(8,128)(2,1)S(1)} %forward_table.1.tab_ref) | copy-start | bytes 12582916
  19.4 16.0 %copy-start.3 = (f32[96,1024]{1,0:T(8,128)S(1)}, f32[96,1024]{1,0:T(8,128)}, u32[]{:S(2)}) copy-start(f32[96,1024]{1,0:T(8,128)} %constant.7.clone.base_ref) | copy-start | bytes 1179652
  30.0 1.8 %collective-permute-start = (f32[3,16,2048]{2,1,0:T(8,128)S(1)}, f32[3,16,2048]{2,1,0:T(8,128)S(1)}, u32[]{:S(2)}, u32[]{:S(2)}) collective-permute-start(f32[3,16,2048]{2,1,0:T(8,128)S(1)} %get-tuple-element.31), channel_id=1, source_target_pairs={{0,1},{1,0},{2,3},{3,2},{4,5},{5,4},{6,7},{7,6},{8,9},{9,8},{10,11... | collective-permute-start | bytes 1179656 | tf_op jit(solution)/shard_map/ppermute | solution.py:337
  31.9 11.1 %copy-start.2 = (f32[96,1024]{1,0:T(8,128)S(1)}, f32[96,1024]{1,0:T(8,128)}, u32[]{:S(2)}) copy-start(f32[96,1024]{1,0:T(8,128)} %constant.8.clone.base_ref) | copy-start | bytes 1179652
  31.9 4.9 %collective-permute-start.1 = (bf16[3,4,2048]{2,1,0:T(4,128)(2,1)S(1)}, bf16[3,4,2048]{2,1,0:T(4,128)(2,1)S(1)}, u32[]{:S(2)}, u32[]{:S(2)}) collective-permute-start(bf16[3,4,2048]{2,1,0:T(4,128)(2,1)S(1)} %get-tuple-element.38), channel_id=1, source_target_pairs={{0,2},{1,3},{2,0},{3,1},{4,6},{5,7},{6,4},{7,5},{8,10},{9,11},{10,... | collective-permute-start | bytes 147464 | tf_op jit(solution)/shard_map/ppermute | solution.py:337
  32.5 4.3 %collective-permute-start.2 = (bf16[3,4,2048]{2,1,0:T(4,128)(2,1)S(1)}, bf16[3,4,2048]{2,1,0:T(4,128)(2,1)S(1)}, u32[]{:S(2)}, u32[]{:S(2)}) collective-permute-start(bf16[3,4,2048]{2,1,0:T(4,128)(2,1)S(1)} %get-tuple-element.39), channel_id=1, source_target_pairs={{0,4},{1,5},{2,6},{3,7},{4,0},{5,1},{6,2},{7,3},{8,12},{9,13},{10,... | collective-permute-start | bytes 147464 | tf_op jit(solution)/shard_map/ppermute | solution.py:337
  33.5 5.0 %collective-permute-start.3 = (bf16[3,4,2048]{2,1,0:T(4,128)(2,1)S(1)}, bf16[3,4,2048]{2,1,0:T(4,128)(2,1)S(1)}, u32[]{:S(2)}, u32[]{:S(2)}) collective-permute-start(bf16[3,4,2048]{2,1,0:T(4,128)(2,1)S(1)} %get-tuple-element.40), channel_id=1, source_target_pairs={{0,6},{1,7},{2,4},{3,5},{4,2},{5,3},{6,0},{7,1},{8,14},{9,15},{10,... | collective-permute-start | bytes 147464 | tf_op jit(solution)/shard_map/ppermute | solution.py:337
  38.6 5.8 %collective-permute-start.4 = (f32[3,1,2048]{2,1,0:T(1,128)S(1)}, f32[3,1,2048]{2,1,0:T(1,128)S(1)}, u32[]{:S(2)}, u32[]{:S(2)}) collective-permute-start(f32[3,1,2048]{2,1,0:T(1,128)S(1)} %get-tuple-element.47), channel_id=1, source_target_pairs={{0,8},{8,0},{16,24},{24,16},{1,9},{9,1},{17,25},{25,17},{2,10},{10... | collective-permute-start | bytes 73736 | tf_op jit(solution)/shard_map/ppermute | solution.py:337
  39.3 5.0 %collective-permute-start.5 = (f32[3,1,2048]{2,1,0:T(1,128)S(1)}, f32[3,1,2048]{2,1,0:T(1,128)S(1)}, u32[]{:S(2)}, u32[]{:S(2)}) collective-permute-start(f32[3,1,2048]{2,1,0:T(1,128)S(1)} %get-tuple-element.48), channel_id=1, source_target_pairs={{0,16},{8,24},{16,0},{24,8},{1,17},{9,25},{17,1},{25,9},{2,18},{10... | collective-permute-start | bytes 73736 | tf_op jit(solution)/shard_map/ppermute | solution.py:337
  40.7 5.6 %collective-permute-start.6 = (f32[3,1,2048]{2,1,0:T(1,128)S(1)}, f32[3,1,2048]{2,1,0:T(1,128)S(1)}, u32[]{:S(2)}, u32[]{:S(2)}) collective-permute-start(f32[3,1,2048]{2,1,0:T(1,128)S(1)} %get-tuple-element.49), channel_id=1, source_target_pairs={{0,24},{8,16},{16,8},{24,0},{1,25},{9,17},{17,9},{25,1},{2,26},{10... | collective-permute-start | bytes 73736 | tf_op jit(solution)/shard_map/ppermute | solution.py:337

commit v3 on v2

--- a/solution.py
+++ b/solution.py
@@ -44,10 +44,15 @@
 def forward_bases(n_time):
     half = n_time // 2
     quarter = half // 2
-    freq = np.concatenate([2 * np.arange(quarter), 2 * np.arange(quarter) + 1])
-    coarse = angle(np.arange(half // STEP)[:, None] * STEP * freq[None, :], n_time)
-    fine = angle(np.arange(STEP)[:, None] * freq[None, :], n_time)
-    return np.concatenate([f(x) for x in (coarse, fine) for f in (np.cos, np.sin)]).astype(np.float32)
+    bases = []
+    for odd in range(2):
+        freq = 2 * np.arange(quarter) + odd
+        coarse = angle(np.arange(half // STEP)[:, None] * STEP * freq[None, :], n_time)
+        fine = angle(np.arange(STEP)[:, None] * freq[None, :], n_time)
+        bases.append(
+            np.concatenate([f(x) for x in (coarse, fine) for f in (np.cos, np.sin)]).astype(np.float32)
+        )
+    return bases
 
 
 def inverse_bases(n_time):
@@ -63,78 +68,112 @@
     ]
 
 
-def pack_kernel(capacity, own_ref, pts_ref, mom_ref, slip_ref, out_ref, scr):
-    devices = out_ref.shape[0]
+def ordered(stages, apart):
+    place = jnp.zeros_like(apart["worker"])
+    for axis, radix, shift, _ in stages:
+        place = place * radix + ((apart[axis] >> shift) & (radix - 1))
+    return place
+
+
+def pack_kernel(stages, capacity, *refs):
+    sources, refs = refs[:4], refs[4:]
+    first = stages[0][1]
+    out_refs = refs[:first]
+    scr, own_ref, pts_ref, mom_ref, slip_ref, sems = refs[first:]
+    copies = [
+        pltpu.make_async_copy(src, dst, sems.at[i])
+        for i, (src, dst) in enumerate(zip(sources, (own_ref, pts_ref, mom_ref, slip_ref)))
+    ]
+    for copy in copies:
+        copy.start()
+    devices = math.prod(radix for _, radix, _, _ in stages)
+    n_worker = lax.axis_size("worker")
+    me = lax.axis_index("server") * n_worker + lax.axis_index("worker")
     slots = devices * capacity
     rup_w, sub = pts_ref.shape
+    asked = rup_w * sub
     n_slip = slip_ref.shape[2]
-    own = own_ref[...]
-    blocks = own.shape[0]
-    both = jnp.concatenate([own // PTS, own % PTS], axis=0).astype(F32).astype(BF16)
+    earlier = (iota((asked, asked), 0) < iota((asked, asked), 1)).astype(F32).astype(BF16)
     spread = iota((128, 6), 0)
     comp = iota((128, 6), 1)
     spread_hi = (spread == comp).astype(F32).astype(BF16)
     spread_lo = (spread == comp + 6).astype(F32).astype(BF16)
-    earlier = (iota((sub, sub), 0) < iota((sub, sub), 1)).astype(F32).astype(BF16)
-    carry = jnp.zeros((devices, 1), F32)
-    slip_acc = jnp.zeros((slots, n_slip), F32)
-    tail_acc = jnp.zeros((slots, 128), F32)
-    lane = iota((slots, 128), 1)
-    for r in range(rup_w):
-        p = pts_ref[r : r + 1, :]
-        in_lane = (iota((128, sub), 0) == p % 128).astype(F32).astype(BF16)
-        found = nn(both, in_lane)
-        in_block = (iota((blocks, sub), 0) == p // 128).astype(F32)
-        dev = jnp.sum(found[:blocks] * in_block, axis=0, keepdims=True)
-        loc = jnp.sum(found[blocks:] * in_block, axis=0, keepdims=True)
-        onehot = (iota((devices, sub), 0).astype(F32) == dev).astype(F32)
-        before = nn(onehot.astype(BF16), earlier) + carry
-        rank = jnp.sum(before * onehot, axis=0, keepdims=True)
-        carry = carry + jnp.sum(onehot, axis=1, keepdims=True)
-        target = dev * capacity + rank
-        pick = (iota((slots, sub), 0).astype(F32) == target).astype(F32)
-        pick16 = pick.astype(BF16)
-        mom = jnp.concatenate([mom_ref[m, r : r + 1, :] for m in range(6)], axis=0)
-        hi, lo = hilo(mom)
-        expanded = nn(spread_hi, hi) + nn(spread_lo, lo)
-        slip_acc = slip_acc + nn(pick16, slip_ref[r])
-        tail = nt(pick16, expanded.astype(BF16))
-        row = jnp.sum(pick * loc, axis=1, keepdims=True)
-        rup = jnp.sum(pick, axis=1, keepdims=True) * float(r)
-        tail = tail + jnp.where(lane == ROW_LANE, row, 0.0) + jnp.where(lane == RUP_LANE, rup, 0.0)
-        tail_acc = tail_acc + tail
-    scr[:, :n_slip] = slip_acc
-    scr[:, n_slip:] = tail_acc
+    for copy in copies:
+        copy.wait()
+    own = own_ref[...]
+    blocks = own.shape[0]
+    both = jnp.concatenate([own // PTS, own % PTS], axis=0).astype(F32).astype(BF16)
+    p = jnp.concatenate([pts_ref[r : r + 1, :] for r in range(rup_w)], axis=1)
+    in_lane = (iota((128, asked), 0) == p % 128).astype(F32).astype(BF16)
+    found = nn(both, in_lane)
+    in_block = (iota((blocks, asked), 0) == p // 128).astype(F32)
+    dev = jnp.sum(found[:blocks] * in_block, axis=0, keepdims=True)
+    loc = jnp.sum(found[blocks:] * in_block, axis=0, keepdims=True)
+    onehot = (iota((devices, asked), 0).astype(F32) == dev).astype(F32)
+    before = nn(onehot.astype(BF16), earlier)
+    rank = jnp.sum(before * onehot, axis=0, keepdims=True)
+    away = dev.astype(jnp.int32) ^ me
+    chunk = ordered(stages, {"worker": away % n_worker, "server": away // n_worker})
+    target = chunk.astype(F32) * capacity + rank
+    pick = (iota((slots, asked), 0).astype(F32) == target).astype(F32)
+    pick16 = pick.astype(BF16)
+    mom = jnp.concatenate(
+        [
+            jnp.concatenate([mom_ref[m, r : r + 1, :] for r in range(rup_w)], axis=1)
+            for m in range(6)
+        ],
+        axis=0,
+    )
+    hi, lo = hilo(mom)
+    rup = (iota((1, asked), 1) // sub).astype(F32)
+    lane = iota((128, asked), 0)
+    expanded = nn(spread_hi, hi) + nn(spread_lo, lo)
+    expanded = jnp.where(lane == ROW_LANE, loc, jnp.where(lane == RUP_LANE, rup, expanded))
+    scr[:, n_slip:] = nt(pick16, expanded.astype(BF16))
+    slip = slip_ref[...].astype(F32).reshape(asked, n_slip).astype(BF16)
+    scr[:, :n_slip] = nn(pick16, slip)
+    part = out_refs[0].shape[0]
     for d in range(devices):
-        out_ref[d] = scr[d * capacity : (d + 1) * capacity, :].astype(BF16)
-
-
-def owner_kernel(stages, rec_ref, sgt_ref, tab_ref, *refs):
+        out_refs[d // part][d % part] = scr[d * capacity : (d + 1) * capacity, :].astype(BF16)
+
+
+def pass_kernel(seen, count, *refs):
+    radix = len(refs) - count
+    in_refs, out_refs = refs[:count], refs[count:]
+    rest = in_refs[0].shape[0] // (seen * radix)
+    for o in range(seen):
+        for k in range(radix):
+            for j in range(rest):
+                for i in range(count):
+                    at = (o * count + i) * rest + j
+                    out_refs[k][at] = in_refs[i][(o * radix + k) * rest + j]
+
+
+def owner_kernel(stages, sgt_ref, even_ref, odd_ref, *refs):
     first = stages[0][1]
-    out_refs = refs[:first]
-    rec_s, x_s, sgt_s, tab_s, sems = refs[first:]
-    devices, capacity, width = rec_ref.shape
+    last = stages[-1][1]
+    rec_refs = refs[:last]
+    out_refs = refs[last : last + first]
+    rec_s, x_s, sgt_s, sems = refs[last + first :]
+    part, capacity, width = rec_refs[0].shape
+    devices = last * part
     slots = devices * capacity
     n_time = sgt_ref.shape[2]
     half = n_time // 2
     quarter = half // 2
     n_slip = width - 128
     wide = 512
-
-    def rows_copy(c):
-        at = slice(6 * c, 6 * c + 6)
-        return pltpu.make_async_copy(sgt_ref.at[at], sgt_s.at[at], sems.at[c])
-
-    def table_copy(i):
-        at = slice(i * quarter, (i + 1) * quarter)
-        return pltpu.make_async_copy(tab_ref.at[:, at], tab_s.at[:, at], sems.at[3 + i])
+    steps = n_time // wide
+
+    def rows_copy(c, n):
+        at = (slice(6 * c, 6 * c + 6), slice(None), slice(n * wide, (n + 1) * wide))
+        return pltpu.make_async_copy(sgt_ref.at[at], sgt_s.at[at], sems.at[c * steps + n])
 
     for c in range(3):
-        rows_copy(c).start()
-    for i in (0, 2, 1, 3):
-        table_copy(i).start()
+        for n in range(steps):
+            rows_copy(c, n).start()
     for d in range(devices):
-        rec_s[d * capacity : (d + 1) * capacity, :] = rec_ref[d].astype(F32)
+        rec_s[d * capacity : (d + 1) * capacity, :] = rec_refs[d // part][d % part].astype(F32)
     tail = rec_s[:, n_slip:]
     row = tail[:, ROW_LANE : ROW_LANE + 1]
     here = iota((slots, PTS), 1).astype(F32) == row
@@ -149,8 +188,8 @@
         axis=0,
     )
     for c in range(3):
-        rows_copy(c).wait()
-        for n in range(n_time // wide):
+        for n in range(steps):
+            rows_copy(c, n).wait()
             rows = sgt_s[6 * c : 6 * c + 6, :, n * wide : (n + 1) * wide].reshape(6 * PTS, wide)
             out = nn(left, rows)
             h, at = divmod(n * wide, half)
@@ -159,25 +198,26 @@
     ruptures = math.prod(radix for _, radix, _, _ in stages)
     shape = (ruptures, slots)
     rup = nt((iota((8, 128), 1) == RUP_LANE).astype(F32).astype(BF16), tail.astype(BF16))[:1].astype(jnp.int32)
-    worker = (iota((1, slots), 1) // capacity) % lax.axis_size("worker")
-    apart = {"worker": worker ^ lax.axis_index("worker"), "server": rup ^ lax.axis_index("server")}
-    where_to = jnp.zeros((1, slots), jnp.int32)
-    for axis, radix, shift, _ in stages:
-        where_to = where_to * radix + ((apart[axis] >> shift) & (radix - 1))
+    chunk = iota((1, slots), 1) // capacity
+    apart = {"worker": jnp.zeros_like(chunk), "server": rup ^ lax.axis_index("server")}
+    for axis, radix, shift, _ in stages[-2::-1]:
+        if axis == "worker":
+            apart[axis] = apart[axis] | ((chunk % radix) << shift)
+        chunk = chunk // radix
+    where_to = ordered(stages, apart)
     seg = (iota(shape, 0) == where_to).astype(F32).astype(BF16)
     slip = rec_s[:, :n_slip].astype(BF16)
     part = ruptures // first
     for q in range(2):
         re = slice(q * quarter, (q + 1) * quarter)
         im = slice(half + q * quarter, half + (q + 1) * quarter)
-        table_copy(q).wait()
-        table_copy(q + 2).wait()
-        slip_re = nn(slip, tab_s[:n_slip, re])
-        slip_im = nn(slip, tab_s[:n_slip, im])
+        tab_ref = (even_ref, odd_ref)[q]
+        slip_re = nn(slip, tab_ref[:n_slip, :quarter])
+        slip_im = nn(slip, tab_ref[:n_slip, quarter:])
         for c in range(3):
             x = x_s[c]
-            u_re = nn(x, tab_s[:, re])
-            u_im = nn(x, tab_s[:, im])
+            u_re = nn(x, tab_ref[:, :quarter])
+            u_im = nn(x, tab_ref[:, quarter:])
             if q == 0:
                 t_re = u_re[:slots] + u_re[slots:]
                 t_im = u_im[:slots] + u_im[slots:]
@@ -209,11 +249,12 @@
 
 def forward_table_kernel(base_ref, tab_ref):
     half = tab_ref.shape[0]
+    quarter = half // 2
     count = half // STEP
     wide = 256
-    for lc in range(half // wide):
+    for lc in range(quarter // wide):
         sl = slice(lc * wide, (lc + 1) * wide)
-        sl2 = slice(half + lc * wide, half + (lc + 1) * wide)
+        sl2 = slice(quarter + lc * wide, quarter + (lc + 1) * wide)
         cb = base_ref[2 * count : 2 * count + STEP, sl]
         sb = base_ref[2 * count + STEP :, sl]
 
@@ -225,7 +266,7 @@
             tab_ref[at, sl2] = (-(sa * cb + ca * sb)).astype(BF16)
             return carry
 
-        lax.fori_loop(0, half // STEP, table, 0)
+        lax.fori_loop(0, count, table, 0)
 
 
 def inverse_table_kernel(base_ref, hi_ref, lo_ref):
@@ -314,6 +355,10 @@
     return pl.BlockSpec(memory_space=pltpu.VMEM)
 
 
+def hbm():
+    return pl.BlockSpec(memory_space=pltpu.HBM)
+
+
 def params(mib):
     return pltpu.CompilerParams(vmem_limit_bytes=mib << 20)
 
@@ -337,6 +382,12 @@
         lax.ppermute(parts[k], axis, [(i, i ^ (k << shift)) for i in range(size)])
         for k in range(1, radix)
     ]
+
+
+def beside(kernel, base, own):
+    base, own = lax.optimization_barrier((jnp.asarray(base), own))
+    own, *made = lax.optimization_barrier((own, *kernel(base)))
+    return own, made
 
 
 def sent_type(stages, i):
@@ -356,27 +407,68 @@
     stages = exchange_plan(n_worker, n_server)
     assert rup_w == n_server and sgt.shape[0] == PTS and slots % 16 == 0
 
-    record = pl.pallas_call(
-        functools.partial(pack_kernel, capacity),
-        out_shape=jax.ShapeDtypeStruct((devices, capacity, width), BF16),
-        in_specs=[vmem()] * 4,
-        out_specs=vmem(),
-        scratch_shapes=[pltpu.VMEM((slots, width), F32)],
-        compiler_params=params(56),
-        name="pack",
-    )(ownership.reshape(-1, 128), sub_points[0], jnp.transpose(moments[0], (1, 0, 2)), slip[0])
-    record = lax.all_to_all(record, ("server", "worker"), split_axis=0, concat_axis=0, tiled=True)
-
-    table = pl.pallas_call(
+    forward = pl.pallas_call(
         forward_table_kernel,
-        out_shape=jax.ShapeDtypeStruct((half, n_time), BF16),
+        out_shape=[jax.ShapeDtypeStruct((half, half), BF16)],
         in_specs=[vmem()],
-        out_specs=vmem(),
-        compiler_params=params(8),
+        out_specs=[vmem()],
+        compiler_params=params(4),
         cost_estimate=pl.CostEstimate(flops=10**9, bytes_accessed=10**7, transcendentals=0),
         name="forward_table",
-    )(jnp.asarray(forward_bases(n_time)))
-    bases = [jnp.asarray(x) for x in inverse_bases(n_time)]
+    )
+
+    def record_shapes(i):
+        chunk = (devices // stages[i][1], capacity, width)
+        return [jax.ShapeDtypeStruct(chunk, BF16)] * stages[i][1]
+
+    records = pl.pallas_call(
+        functools.partial(pack_kernel, stages, capacity),
+        out_shape=record_shapes(0),
+        in_specs=[hbm()] * 4,
+        out_specs=[vmem()] * stages[0][1],
+        scratch_shapes=[
+            pltpu.VMEM((slots, width), F32),
+            pltpu.VMEM((ownership.shape[0] // 128, 128), jnp.int32),
+            pltpu.VMEM((rup_w, sub_dev), jnp.int32),
+            pltpu.VMEM((6, rup_w, sub_dev), F32),
+            pltpu.VMEM((rup_w, sub_dev, n_slip), BF16),
+            pltpu.SemaphoreType.DMA((4,)),
+        ],
+        compiler_params=params(12),
+        name="pack",
+    )(
+        *[
+            pltpu.with_memory_space_constraint(x, pltpu.HBM)
+            for x in (
+                ownership.reshape(-1, 128),
+                sub_points[0],
+                jnp.transpose(moments[0], (1, 0, 2)),
+                slip[0],
+            )
+        ]
+    )
+    seen = 1
+    bases = forward_bases(n_time)
+    forwards = []
+    for i in range(len(stages)):
+        arrived = send(records, stages[i])
+        own = records[0]
+        if i >= len(stages) - 2:
+            own, table = beside(forward, bases[len(forwards)], own)
+            forwards += table
+        records = [own, *arrived]
+        if i + 1 < len(stages):
+            count = len(records)
+            records = pl.pallas_call(
+                functools.partial(pass_kernel, seen, count),
+                out_shape=record_shapes(i + 1),
+                in_specs=[vmem()] * count,
+                out_specs=[vmem()] * stages[i + 1][1],
+                compiler_params=params(2),
+                name=f"pass_{i}",
+            )(*records)
+            seen *= count
+
     inverse = pl.pallas_call(
         inverse_table_kernel,
         out_shape=[jax.ShapeDtypeStruct((half, half), BF16)] * 2,
@@ -394,6 +486,7 @@
         name="gain",
     )()
     tables = []
+    bases = inverse_bases(n_time)
 
     def part_shapes(i):
         count = math.prod(radix for _, radix, _, _ in stages[i + 1 :])
@@ -405,19 +498,18 @@
     parts = pl.pallas_call(
         functools.partial(owner_kernel, stages),
         out_shape=part_shapes(0),
-        in_specs=[vmem(), pl.BlockSpec(memory_space=pl.ANY), pl.BlockSpec(memory_space=pl.ANY)],
+        in_specs=[hbm()] + [vmem()] * (2 + stages[-1][1]),
         out_specs=[vmem()] * stages[0][1],
         scratch_shapes=[
             pltpu.VMEM((slots, width), F32),
             pltpu.VMEM((3, 2 * slots, half), BF16),
             pltpu.VMEM((18, PTS, n_time), BF16),
-            pltpu.VMEM((half, n_time), BF16),
-            pltpu.SemaphoreType.DMA((7,)),
+            pltpu.SemaphoreType.DMA((12,)),
         ],
-        compiler_params=params(52),
+        compiler_params=params(32),
         cost_estimate=pl.CostEstimate(flops=10**10, bytes_accessed=2 * 10**7, transcendentals=0),
         name="owner",
-    )(record, jnp.transpose(sgt, (1, 0, 2)), table)
+    )(pltpu.with_memory_space_constraint(jnp.transpose(sgt, (1, 0, 2)), pltpu.HBM), *forwards, *records)
     arrived = send(parts, stages[0])
     for i in range(1, len(stages)):
         radix = stages[i][1]
@@ -431,12 +523,9 @@
         )(parts[0], *arrived)
         arrived = send(parts, stages[i])
         if i >= len(stages) - 2:
-            base, own = lax.optimization_barrier((bases[len(tables) // 2], parts[0]))
-            pair = inverse(base)
+            own, pair = beside(inverse, bases[len(tables) // 2], parts[0])
+            parts = [own]
             tables += pair
-            own, *pair = lax.optimization_barrier((own, *pair))
-            parts = [own]
-            tables = tables[:-2] + pair
     count = 1 + len(arrived)
     seis, peaks = pl.pallas_call(
         functools.partial(final_kernel, count),

time: 49.3 us -> 51.8 us (1.051)
  waiting for transfers between devices: 8.57 us -> 12.2 us
  local copies, waits for them, and re-layouts: 2.99 us -> 0.97 us
  starting transfers between devices: 15.8 us -> 17.5 us
  Pallas kernels: 21 us -> 20.2 us
    ppermute x7 -> x14, starting transfers between devices: 8.47 us -> 17.5 us  [send(): lax.ppermute(parts[k], axis, [(i, i ^ k << shift) for i in range(size)])]
    ppermute x7 -> x14, waiting for transfers between devices: 4.87 us -> 12.2 us  [send(): lax.ppermute(parts[k], axis, [(i, i ^ k << shift) for i in range(size)])]
    all_to_all x1 -> x0, starting transfers between devices: 7.3 us -> none  [shards(): lax.all_to_all(record, ('server', 'worker'), split_axis=0, concat_axis=0,...]
    all_to_all x1 -> x0, waiting for transfers between devices: 3.7 us -> none  [shards(): lax.all_to_all(record, ('server', 'worker'), split_axis=0, concat_axis=0,...]
    unnamed x8, local copies, waits for them, and re-layouts: 2.99 us -> 0.97 us
    pallas_call x4 -> x7, Pallas kernels: 7.47 us -> 6.17 us  [the longest x4 4.52 us: beside(): own, *made = lax.optimization_barrier((own, *kernel(base)))]
  transfers between devices with their start and end apart: 8 -> 14, of which waited for: 4 -> 9; matrix products, arithmetic and copies ran while one was open for 0% -> 0% of each run, Pallas kernels for 9% -> 9%
where the time goes in v3:
time: 51.8 us; the launch traced here: 51.7 us
  Pallas kernels  20.2 us (39%)
  starting transfers between devices  17.5 us (34%)
  waiting for transfers between devices  12.2 us (24%)
  local copies, waits for them, and re-layouts  0.97 us (2%)
  between operations  0.78 us (2%)
    ppermute x14, starting transfers between devices, send(): lax.ppermute(parts[k], axis, [(i, i ^ k << shift) for i in range(size)])  17.5 us
    ppermute x14, waiting for transfers between devices, send(): lax.ppermute(parts[k], axis, [(i, i ^ k << shift) for i in range(size)])  12.2 us
    pallas_call x1, Pallas kernels, shards(): pl.pallas_call(functools.partial(owner_kernel, stages), out_shape=part_sh...  11.1 us
    pallas_call x4, Pallas kernels, beside(): own, *made = lax.optimization_barrier((own, *kernel(base)))  4.52 us
    pallas_call x1, Pallas kernels, shards(): pl.pallas_call(functools.partial(final_kernel, count), out_shape=[jax.Sha...  2.8 us
    pallas_call x1, Pallas kernels, shards(): pl.pallas_call(functools.partial(pack_kernel, stages, capacity), out_shap...  1.61 us
  transfers between devices with their start and end apart: 14, of which 9 were waited for; matrix products, arithmetic and copies ran while one was open for 0% of the time, Pallas kernels for 9%

profile of v3, /device:TPU:0, one launch (start us, length us, event | category | flops | bytes accessed | tf_op | source)
XLA Modules:
  0.0 51.7 jit_solution(1808343615977639)
XLA Ops:
  0.6 0.0 copy-start.2
  0.6 1.6 %pack.1 = (bf16[16,4,640]{2,1,0:T(4,128)(2,1)S(1)}, bf16[16,4,640]{2,1,0:T(4,128)(2,1)S(1)}) custom-call(s32[32,128]{1,0:T(8,128)} %bitcast.14, s32[4,24]{1,0:T(4,128)} %bitcast.16, f32[6,4,24]{2,1,0:T(4,128)} %bitcast.15, bf16[4,24,512]{2,1,0:T(8,128)(2,1)} %bitcast.13), custom_call_target="tpu_custom_call" | custom-call | tf_op jit(solution)/shard_map/pack/pallas_call | solution.py:424
  2.3 0.5 %collective-permute-start = (bf16[16,4,640]{2,1,0:T(4,128)(2,1)S(1)}, bf16[16,4,640]{2,1,0:T(4,128)(2,1)S(1)}, u32[]{:S(2)}, u32[]{:S(2)}) collective-permute-start(bf16[16,4,640]{2,1,0:T(4,128)(2,1)S(1)} %get-tuple-element.49), channel_id=1, source_target_pairs={{0,1},{1,0},{2,3},{3,2},{4,5},{5,4},{6,7},{7,6},{8,9},{9,8},{10,11... | collective-permute-start | bytes 245768 | tf_op jit(solution)/shard_map/ppermute | solution.py:382
  2.8 0.9 %collective-permute-done.refs_1_ = bf16[16,4,640]{2,1,0:T(4,128)(2,1)S(1)} collective-permute-done((bf16[16,4,640]{2,1,0:T(4,128)(2,1)S(1)}, bf16[16,4,640]{2,1,0:T(4,128)(2,1)S(1)}, u32[]{:S(2)}, u32[]{:S(2)}) %collective-permute-start) | collective-permute-done | bytes 81952 | tf_op jit(solution)/shard_map/ppermute | solution.py:382
  3.7 2.9 %collective-permute-start.1 = (bf16[8,4,640]{2,1,0:T(4,128)(2,1)S(1)}, bf16[8,4,640]{2,1,0:T(4,128)(2,1)S(1)}, u32[]{:S(2)}, u32[]{:S(2)}) collective-permute-start(bf16[8,4,640]{2,1,0:T(4,128)(2,1)S(1)} %get-tuple-element.55), channel_id=1, source_target_pairs={{0,2},{1,3},{2,0},{3,1},{4,6},{5,7},{6,4},{7,5},{8,10},{9,11},{10,... | collective-permute-start | bytes 122888 | tf_op jit(solution)/shard_map/ppermute | solution.py:382
  6.6 1.5 %collective-permute-start.2 = (bf16[8,4,640]{2,1,0:T(4,128)(2,1)S(1)}, bf16[8,4,640]{2,1,0:T(4,128)(2,1)S(1)}, u32[]{:S(2)}, u32[]{:S(2)}) collective-permute-start(bf16[8,4,640]{2,1,0:T(4,128)(2,1)S(1)} %get-tuple-element.56), channel_id=1, source_target_pairs={{0,4},{1,5},{2,6},{3,7},{4,0},{5,1},{6,2},{7,3},{8,12},{9,13},{10,... | collective-permute-start | bytes 122888 | tf_op jit(solution)/shard_map/ppermute | solution.py:382
  8.1 0.0 collective-permute-start.3
  8.2 0.0 copy-start.3
  8.2 0.9 %copy-done.3 = f32[128,512]{1,0:T(8,128)S(1)} copy-done((f32[128,512]{1,0:T(8,128)S(1)}, f32[128,512]{1,0:T(8,128)}, u32[]{:S(2)}) %copy-start.3) | copy-done | bytes 262168
  9.1 0.9 %forward_table.2.even_ref = bf16[1024,1024]{1,0:T(8,128)(2,1)S(1)} custom-call(f32[128,512]{1,0:T(8,128)S(1)} %copy-done.3), custom_call_target="tpu_custom_call" | custom-call | flops 1000000000 | bytes 10000000 | tf_op jit(solution)/shard_map/forward_table/pallas_call | solution.py:389
  10.1 0.0 collective-permute-done.1.refs_1_
  10.1 0.6 %collective-permute-done.2.refs_2_ = bf16[8,4,640]{2,1,0:T(4,128)(2,1)S(1)} collective-permute-done((bf16[8,4,640]{2,1,0:T(4,128)(2,1)S(1)}, bf16[8,4,640]{2,1,0:T(4,128)(2,1)S(1)}, u32[]{:S(2)}, u32[]{:S(2)}) %collective-permute-start.2) | collective-permute-done | bytes 40992 | tf_op jit(solution)/shard_map/ppermute | solution.py:382
  10.6 2.4 %collective-permute-done.3.refs_3_ = bf16[8,4,640]{2,1,0:T(4,128)(2,1)S(1)} collective-permute-done((bf16[8,4,640]{2,1,0:T(4,128)(2,1)S(1)}, bf16[8,4,640]{2,1,0:T(4,128)(2,1)S(1)}, u32[]{:S(2)}, u32[]{:S(2)}) %collective-permute-start.3) | collective-permute-done | bytes 40992 | tf_op jit(solution)/shard_map/ppermute | solution.py:382
  13.1 1.6 %collective-permute-start.4 = (bf16[8,4,640]{2,1,0:T(4,128)(2,1)S(1)}, bf16[8,4,640]{2,1,0:T(4,128)(2,1)S(1)}, u32[]{:S(2)}, u32[]{:S(2)}) collective-permute-start(bf16[8,4,640]{2,1,0:T(4,128)(2,1)S(1)} %get-tuple-element.63), channel_id=1, source_target_pairs={{0,8},{8,0},{16,24},{24,16},{1,9},{9,1},{17,25},{25,17},{2,10},{10... | collective-permute-start | bytes 122888 | tf_op jit(solution)/shard_map/ppermute | solution.py:382
  14.7 2.6 %collective-permute-start.5 = (bf16[8,4,640]{2,1,0:T(4,128)(2,1)S(1)}, bf16[8,4,640]{2,1,0:T(4,128)(2,1)S(1)}, u32[]{:S(2)}, u32[]{:S(2)}) collective-permute-start(bf16[8,4,640]{2,1,0:T(4,128)(2,1)S(1)} %get-tuple-element.64), channel_id=1, source_target_pairs={{0,16},{8,24},{16,0},{24,8},{1,17},{9,25},{17,1},{25,9},{2,18},{10... | collective-permute-start | bytes 122888 | tf_op jit(solution)/shard_map/ppermute | solution.py:382
  17.3 0.2 collective-permute-start.6
  17.5 0.0 copy-done.2
  17.5 0.9 %forward_table.3.odd_ref = bf16[1024,1024]{1,0:T(8,128)(2,1)S(1)} custom-call(f32[128,512]{1,0:T(8,128)S(1)} %copy-done.2), custom_call_target="tpu_custom_call" | custom-call | flops 1000000000 | bytes 10000000 | tf_op jit(solution)/shard_map/forward_table/pallas_call | solution.py:389
  18.5 0.0 collective-permute-done.4.refs_1_
  18.5 2.0 %collective-permute-done.5.refs_2_ = bf16[8,4,640]{2,1,0:T(4,128)(2,1)S(1)} collective-permute-done((bf16[8,4,640]{2,1,0:T(4,128)(2,1)S(1)}, bf16[8,4,640]{2,1,0:T(4,128)(2,1)S(1)}, u32[]{:S(2)}, u32[]{:S(2)}) %collective-permute-start.5) | collective-permute-done | bytes 40992 | tf_op jit(solution)/shard_map/ppermute | solution.py:382
  20.5 2.6 %collective-permute-done.6.refs_3_ = bf16[8,4,640]{2,1,0:T(4,128)(2,1)S(1)} collective-permute-done((bf16[8,4,640]{2,1,0:T(4,128)(2,1)S(1)}, bf16[8,4,640]{2,1,0:T(4,128)(2,1)S(1)}, u32[]{:S(2)}, u32[]{:S(2)}) %collective-permute-start.6) | collective-permute-done | bytes 40992 | tf_op jit(solution)/shard_map/ppermute | solution.py:382
  23.1 0.0 copy-start.1
  23.1 11.1 %owner.1 = (f32[3,16,2048]{2,1,0:T(8,128)S(1)}, f32[3,16,2048]{2,1,0:T(8,128)S(1)}) custom-call(bf16[18,128,2048]{2,1,0:T(8,128)(2,1)} %bitcast.17, bf16[1024,1024]{1,0:T(8,128)(2,1)S(1)} %forward_table.2.even_ref, bf16[1024,1024]{1,0:T(8,128)(2,1)S(1)} %forward_table.3.odd_ref, bf16[8,4,640]{2,1,0:T(4,128)(2,1)S(1)} %get-tuple-element.62.refs_0_, ...), custom_call_target="tpu_custom_call" | custom-call | flops 10000000000 | bytes 20000000 | tf_op jit(solution)/shard_map/owner/pallas_call | solution.py:498
  34.2 0.1 collective-permute-start.7
  34.3 0.1 gain.1
  34.4 1.6 %collective-permute-done.7.refs_1_ = f32[3,16,2048]{2,1,0:T(8,128)S(1)} collective-permute-done((f32[3,16,2048]{2,1,0:T(8,128)S(1)}, f32[3,16,2048]{2,1,0:T(8,128)S(1)}, u32[]{:S(2)}, u32[]{:S(2)}) %collective-permute-start.7) | collective-permute-done | bytes 393248 | tf_op jit(solution)/shard_map/ppermute | solution.py:382
  36.0 0.0 copy-start
  36.1 0.6 %collective-permute-start.8 = (bf16[3,4,2048]{2,1,0:T(4,128)(2,1)S(1)}, bf16[3,4,2048]{2,1,0:T(4,128)(2,1)S(1)}, u32[]{:S(2)}, u32[]{:S(2)}) collective-permute-start(bf16[3,4,2048]{2,1,0:T(4,128)(2,1)S(1)} %get-tuple-element.74), channel_id=1, source_target_pairs={{0,2},{1,3},{2,0},{3,1},{4,6},{5,7},{6,4},{7,5},{8,10},{9,11},{10,... | collective-permute-start | bytes 147464 | tf_op jit(solution)/shard_map/ppermute | solution.py:382
  36.7 0.5 collective-permute-start.9
  37.2 2.5 %collective-permute-start.10 = (bf16[3,4,2048]{2,1,0:T(4,128)(2,1)S(1)}, bf16[3,4,2048]{2,1,0:T(4,128)(2,1)S(1)}, u32[]{:S(2)}, u32[]{:S(2)}) collective-permute-start(bf16[3,4,2048]{2,1,0:T(4,128)(2,1)S(1)} %get-tuple-element.76), channel_id=1, source_target_pairs={{0,6},{1,7},{2,4},{3,5},{4,2},{5,3},{6,0},{7,1},{8,14},{9,15},{10,... | collective-permute-start | bytes 147464 | tf_op jit(solution)/shard_map/ppermute | solution.py:382
  39.6 0.0 copy-done.1
  39.6 1.3 %inverse_table.2 = (bf16[1024,1024]{1,0:T(8,128)(2,1)S(1)}, bf16[1024,1024]{1,0:T(8,128)(2,1)S(1)}) custom-call(f32[96,1024]{1,0:T(8,128)S(1)} %copy-done.1), custom_call_target="tpu_custom_call" | custom-call | flops 1000000000 | bytes 10000000 | tf_op jit(solution)/shard_map/inverse_table/pallas_call | solution.py:389
  41.0 0.0 collective-permute-done.8.refs_1_
  41.0 0.3 collective-permute-done.9.refs_2_
  41.3 0.9 %collective-permute-done.10.refs_3_ = bf16[3,4,2048]{2,1,0:T(4,128)(2,1)S(1)} collective-permute-done((bf16[3,4,2048]{2,1,0:T(4,128)(2,1)S(1)}, bf16[3,4,2048]{2,1,0:T(4,128)(2,1)S(1)}, u32[]{:S(2)}, u32[]{:S(2)}) %collective-permute-start.10) | collective-permute-done | bytes 49184 | tf_op jit(solution)/shard_map/ppermute | solution.py:382
  42.2 0.1 collective-permute-start.11
  42.3 1.0 %collective-permute-start.12 = (f32[3,1,2048]{2,1,0:T(1,128)S(1)}, f32[3,1,2048]{2,1,0:T(1,128)S(1)}, u32[]{:S(2)}, u32[]{:S(2)}) collective-permute-start(f32[3,1,2048]{2,1,0:T(1,128)S(1)} %get-tuple-element.84), channel_id=1, source_target_pairs={{0,16},{8,24},{16,0},{24,8},{1,17},{9,25},{17,1},{25,9},{2,18},{10... | collective-permute-start | bytes 73736 | tf_op jit(solution)/shard_map/ppermute | solution.py:382
  43.3 3.4 %collective-permute-start.13 = (f32[3,1,2048]{2,1,0:T(1,128)S(1)}, f32[3,1,2048]{2,1,0:T(1,128)S(1)}, u32[]{:S(2)}, u32[]{:S(2)}) collective-permute-start(f32[3,1,2048]{2,1,0:T(1,128)S(1)} %get-tuple-element.85), channel_id=1, source_target_pairs={{0,24},{8,16},{16,8},{24,0},{1,25},{9,17},{17,9},{25,1},{2,26},{10... | collective-permute-start | bytes 73736 | tf_op jit(solution)/shard_map/ppermute | solution.py:382
  46.6 0.0 copy-done
  46.6 1.3 %inverse_table.3 = (bf16[1024,1024]{1,0:T(8,128)(2,1)S(1)}, bf16[1024,1024]{1,0:T(8,128)(2,1)S(1)}) custom-call(f32[96,1024]{1,0:T(8,128)S(1)} %copy-done), custom_call_target="tpu_custom_call" | custom-call | flops 1000000000 | bytes 10000000 | tf_op jit(solution)/shard_map/inverse_table/pallas_call | solution.py:389
  48.0 0.0 collective-permute-done.11.refs_1_
  48.0 0.0 collective-permute-done.12.refs_2_
  48.0 0.9 %collective-permute-done.13.refs_3_ = f32[3,1,2048]{2,1,0:T(1,128)S(1)} collective-permute-done((f32[3,1,2048]{2,1,0:T(1,128)S(1)}, f32[3,1,2048]{2,1,0:T(1,128)S(1)}, u32[]{:S(2)}, u32[]{:S(2)}) %collective-permute-start.13) | collective-permute-done | bytes 24608 | tf_op jit(solution)/shard_map/ppermute | solution.py:382
  48.9 2.8 %finish.1 = (f32[3,1,2048]{2,1,0:T(1,128)}, f32[3,1,44]{2,1,0:T(1,128)}) custom-call(f32[3,1,2048]{2,1,0:T(1,128)S(1)} %get-tuple-element.82.refs_0_, f32[3,1,2048]{2,1,0:T(1,128)S(1)} %collective-permute-done.11.refs_1_, f32[3,1,2048]{2,1,0:T(1,128)S(1)} %collective-permute-done.12.refs_2_, f32[3,1,2048]{2,1,0:T(1,128)S(1)} %collective-permute-done.13.refs_3_, ...), custom_call_target="tpu_custom_call" | custom-call | tf_op jit(solution)/shard_map/finish/pallas_call | solution.py:530
  (4 shorter events, 0.1 us)
Async XLA Ops:
  0.6 16.9 %copy-start.2 = (f32[128,512]{1,0:T(8,128)S(1)}, f32[128,512]{1,0:T(8,128)}, u32[]{:S(2)}) copy-start(f32[128,512]{1,0:T(8,128)} %constant.9.clone.base_ref) | copy-start | bytes 786436
  2.3 1.4 %collective-permute-start = (bf16[16,4,640]{2,1,0:T(4,128)(2,1)S(1)}, bf16[16,4,640]{2,1,0:T(4,128)(2,1)S(1)}, u32[]{:S(2)}, u32[]{:S(2)}) collective-permute-start(bf16[16,4,640]{2,1,0:T(4,128)(2,1)S(1)} %get-tuple-element.49), channel_id=1, source_target_pairs={{0,1},{1,0},{2,3},{3,2},{4,5},{5,4},{6,7},{7,6},{8,9},{9,8},{10,11... | collective-permute-start | bytes 245768 | tf_op jit(solution)/shard_map/ppermute | solution.py:382
  3.7 6.3 %collective-permute-start.1 = (bf16[8,4,640]{2,1,0:T(4,128)(2,1)S(1)}, bf16[8,4,640]{2,1,0:T(4,128)(2,1)S(1)}, u32[]{:S(2)}, u32[]{:S(2)}) collective-permute-start(bf16[8,4,640]{2,1,0:T(4,128)(2,1)S(1)} %get-tuple-element.55), channel_id=1, source_target_pairs={{0,2},{1,3},{2,0},{3,1},{4,6},{5,7},{6,4},{7,5},{8,10},{9,11},{10,... | collective-permute-start | bytes 122888 | tf_op jit(solution)/shard_map/ppermute | solution.py:382
  6.6 4.0 %collective-permute-start.2 = (bf16[8,4,640]{2,1,0:T(4,128)(2,1)S(1)}, bf16[8,4,640]{2,1,0:T(4,128)(2,1)S(1)}, u32[]{:S(2)}, u32[]{:S(2)}) collective-permute-start(bf16[8,4,640]{2,1,0:T(4,128)(2,1)S(1)} %get-tuple-element.56), channel_id=1, source_target_pairs={{0,4},{1,5},{2,6},{3,7},{4,0},{5,1},{6,2},{7,3},{8,12},{9,13},{10,... | collective-permute-start | bytes 122888 | tf_op jit(solution)/shard_map/ppermute | solution.py:382
  8.1 4.9 %collective-permute-start.3 = (bf16[8,4,640]{2,1,0:T(4,128)(2,1)S(1)}, bf16[8,4,640]{2,1,0:T(4,128)(2,1)S(1)}, u32[]{:S(2)}, u32[]{:S(2)}) collective-permute-start(bf16[8,4,640]{2,1,0:T(4,128)(2,1)S(1)} %get-tuple-element.57), channel_id=1, source_target_pairs={{0,6},{1,7},{2,4},{3,5},{4,2},{5,3},{6,0},{7,1},{8,14},{9,15},{10,... | collective-permute-start | bytes 122888 | tf_op jit(solution)/shard_map/ppermute | solution.py:382
  8.2 0.9 %copy-start.3 = (f32[128,512]{1,0:T(8,128)S(1)}, f32[128,512]{1,0:T(8,128)}, u32[]{:S(2)}) copy-start(f32[128,512]{1,0:T(8,128)} %constant.8.clone.base_ref) | copy-start | bytes 786436
  13.1 5.4 %collective-permute-start.4 = (bf16[8,4,640]{2,1,0:T(4,128)(2,1)S(1)}, bf16[8,4,640]{2,1,0:T(4,128)(2,1)S(1)}, u32[]{:S(2)}, u32[]{:S(2)}) collective-permute-start(bf16[8,4,640]{2,1,0:T(4,128)(2,1)S(1)} %get-tuple-element.63), channel_id=1, source_target_pairs={{0,8},{8,0},{16,24},{24,16},{1,9},{9,1},{17,25},{25,17},{2,10},{10... | collective-permute-start | bytes 122888 | tf_op jit(solution)/shard_map/ppermute | solution.py:382
  14.7 5.8 %collective-permute-start.5 = (bf16[8,4,640]{2,1,0:T(4,128)(2,1)S(1)}, bf16[8,4,640]{2,1,0:T(4,128)(2,1)S(1)}, u32[]{:S(2)}, u32[]{:S(2)}) collective-permute-start(bf16[8,4,640]{2,1,0:T(4,128)(2,1)S(1)} %get-tuple-element.64), channel_id=1, source_target_pairs={{0,16},{8,24},{16,0},{24,8},{1,17},{9,25},{17,1},{25,9},{2,18},{10... | collective-permute-start | bytes 122888 | tf_op jit(solution)/shard_map/ppermute | solution.py:382
  17.3 5.8 %collective-permute-start.6 = (bf16[8,4,640]{2,1,0:T(4,128)(2,1)S(1)}, bf16[8,4,640]{2,1,0:T(4,128)(2,1)S(1)}, u32[]{:S(2)}, u32[]{:S(2)}) collective-permute-start(bf16[8,4,640]{2,1,0:T(4,128)(2,1)S(1)} %get-tuple-element.65), channel_id=1, source_target_pairs={{0,24},{8,16},{16,8},{24,0},{1,25},{9,17},{17,9},{25,1},{2,26},{10... | collective-permute-start | bytes 122888 | tf_op jit(solution)/shard_map/ppermute | solution.py:382
  23.1 16.5 %copy-start.1 = (f32[96,1024]{1,0:T(8,128)S(1)}, f32[96,1024]{1,0:T(8,128)}, u32[]{:S(2)}) copy-start(f32[96,1024]{1,0:T(8,128)} %constant.10.clone.base_ref) | copy-start | bytes 1179652
  34.2 1.8 %collective-permute-start.7 = (f32[3,16,2048]{2,1,0:T(8,128)S(1)}, f32[3,16,2048]{2,1,0:T(8,128)S(1)}, u32[]{:S(2)}, u32[]{:S(2)}) collective-permute-start(f32[3,16,2048]{2,1,0:T(8,128)S(1)} %get-tuple-element.67), channel_id=1, source_target_pairs={{0,1},{1,0},{2,3},{3,2},{4,5},{5,4},{6,7},{7,6},{8,9},{9,8},{10,11... | collective-permute-start | bytes 1179656 | tf_op jit(solution)/shard_map/ppermute | solution.py:382
  36.0 10.6 %copy-start = (f32[96,1024]{1,0:T(8,128)S(1)}, f32[96,1024]{1,0:T(8,128)}, u32[]{:S(2)}) copy-start(f32[96,1024]{1,0:T(8,128)} %constant.11.clone.base_ref) | copy-start | bytes 1179652
  36.1 4.9 %collective-permute-start.8 = (bf16[3,4,2048]{2,1,0:T(4,128)(2,1)S(1)}, bf16[3,4,2048]{2,1,0:T(4,128)(2,1)S(1)}, u32[]{:S(2)}, u32[]{:S(2)}) collective-permute-start(bf16[3,4,2048]{2,1,0:T(4,128)(2,1)S(1)} %get-tuple-element.74), channel_id=1, source_target_pairs={{0,2},{1,3},{2,0},{3,1},{4,6},{5,7},{6,4},{7,5},{8,10},{9,11},{10,... | collective-permute-start | bytes 147464 | tf_op jit(solution)/shard_map/ppermute | solution.py:382
  36.7 4.6 %collective-permute-start.9 = (bf16[3,4,2048]{2,1,0:T(4,128)(2,1)S(1)}, bf16[3,4,2048]{2,1,0:T(4,128)(2,1)S(1)}, u32[]{:S(2)}, u32[]{:S(2)}) collective-permute-start(bf16[3,4,2048]{2,1,0:T(4,128)(2,1)S(1)} %get-tuple-element.75), channel_id=1, source_target_pairs={{0,4},{1,5},{2,6},{3,7},{4,0},{5,1},{6,2},{7,3},{8,12},{9,13},{10,... | collective-permute-start | bytes 147464 | tf_op jit(solution)/shard_map/ppermute | solution.py:382
  37.2 5.0 %collective-permute-start.10 = (bf16[3,4,2048]{2,1,0:T(4,128)(2,1)S(1)}, bf16[3,4,2048]{2,1,0:T(4,128)(2,1)S(1)}, u32[]{:S(2)}, u32[]{:S(2)}) collective-permute-start(bf16[3,4,2048]{2,1,0:T(4,128)(2,1)S(1)} %get-tuple-element.76), channel_id=1, source_target_pairs={{0,6},{1,7},{2,4},{3,5},{4,2},{5,3},{6,0},{7,1},{8,14},{9,15},{10,... | collective-permute-start | bytes 147464 | tf_op jit(solution)/shard_map/ppermute | solution.py:382
  42.2 5.8 %collective-permute-start.11 = (f32[3,1,2048]{2,1,0:T(1,128)S(1)}, f32[3,1,2048]{2,1,0:T(1,128)S(1)}, u32[]{:S(2)}, u32[]{:S(2)}) collective-permute-start(f32[3,1,2048]{2,1,0:T(1,128)S(1)} %get-tuple-element.83), channel_id=1, source_target_pairs={{0,8},{8,0},{16,24},{24,16},{1,9},{9,1},{17,25},{25,17},{2,10},{10... | collective-permute-start | bytes 73736 | tf_op jit(solution)/shard_map/ppermute | solution.py:382
  42.3 5.7 %collective-permute-start.12 = (f32[3,1,2048]{2,1,0:T(1,128)S(1)}, f32[3,1,2048]{2,1,0:T(1,128)S(1)}, u32[]{:S(2)}, u32[]{:S(2)}) collective-permute-start(f32[3,1,2048]{2,1,0:T(1,128)S(1)} %get-tuple-element.84), channel_id=1, source_target_pairs={{0,16},{8,24},{16,0},{24,8},{1,17},{9,25},{17,1},{25,9},{2,18},{10... | collective-permute-start | bytes 73736 | tf_op jit(solution)/shard_map/ppermute | solution.py:382
  43.3 5.6 %collective-permute-start.13 = (f32[3,1,2048]{2,1,0:T(1,128)S(1)}, f32[3,1,2048]{2,1,0:T(1,128)S(1)}, u32[]{:S(2)}, u32[]{:S(2)}) collective-permute-start(f32[3,1,2048]{2,1,0:T(1,128)S(1)} %get-tuple-element.85), channel_id=1, source_target_pairs={{0,24},{8,16},{16,8},{24,0},{1,25},{9,17},{17,9},{25,1},{2,26},{10... | collective-permute-start | bytes 73736 | tf_op jit(solution)/shard_map/ppermute | solution.py:382

commit v4 on v3

--- a/solution.py
+++ b/solution.py
@@ -75,20 +75,16 @@
     return place
 
 
-def pack_kernel(stages, capacity, *refs):
-    sources, refs = refs[:4], refs[4:]
-    first = stages[0][1]
-    out_refs = refs[:first]
-    scr, own_ref, pts_ref, mom_ref, slip_ref, sems = refs[first:]
+def pack_kernel(*refs):
+    sources = refs[:4]
+    out_ref, scr, own_ref, pts_ref, mom_ref, slip_ref, sems = refs[4:]
     copies = [
         pltpu.make_async_copy(src, dst, sems.at[i])
         for i, (src, dst) in enumerate(zip(sources, (own_ref, pts_ref, mom_ref, slip_ref)))
     ]
     for copy in copies:
         copy.start()
-    devices = math.prod(radix for _, radix, _, _ in stages)
-    n_worker = lax.axis_size("worker")
-    me = lax.axis_index("server") * n_worker + lax.axis_index("worker")
+    devices, capacity, _ = out_ref.shape
     slots = devices * capacity
     rup_w, sub = pts_ref.shape
     asked = rup_w * sub
@@ -112,9 +108,7 @@
     onehot = (iota((devices, asked), 0).astype(F32) == dev).astype(F32)
     before = nn(onehot.astype(BF16), earlier)
     rank = jnp.sum(before * onehot, axis=0, keepdims=True)
-    away = dev.astype(jnp.int32) ^ me
-    chunk = ordered(stages, {"worker": away % n_worker, "server": away // n_worker})
-    target = chunk.astype(F32) * capacity + rank
+    target = dev * capacity + rank
     pick = (iota((slots, asked), 0).astype(F32) == target).astype(F32)
     pick16 = pick.astype(BF16)
     mom = jnp.concatenate(
@@ -132,48 +126,31 @@
     scr[:, n_slip:] = nt(pick16, expanded.astype(BF16))
     slip = slip_ref[...].astype(F32).reshape(asked, n_slip).astype(BF16)
     scr[:, :n_slip] = nn(pick16, slip)
-    part = out_refs[0].shape[0]
     for d in range(devices):
-        out_refs[d // part][d % part] = scr[d * capacity : (d + 1) * capacity, :].astype(BF16)
-
-
-def pass_kernel(seen, count, *refs):
-    radix = len(refs) - count
-    in_refs, out_refs = refs[:count], refs[count:]
-    rest = in_refs[0].shape[0] // (seen * radix)
-    for o in range(seen):
-        for k in range(radix):
-            for j in range(rest):
-                for i in range(count):
-                    at = (o * count + i) * rest + j
-                    out_refs[k][at] = in_refs[i][(o * radix + k) * rest + j]
-
-
-def owner_kernel(stages, sgt_ref, even_ref, odd_ref, *refs):
+        out_ref[d] = scr[d * capacity : (d + 1) * capacity, :].astype(BF16)
+
+
+def owner_kernel(stages, rec_ref, sgt_ref, even_ref, odd_ref, *refs):
     first = stages[0][1]
-    last = stages[-1][1]
-    rec_refs = refs[:last]
-    out_refs = refs[last : last + first]
-    rec_s, x_s, sgt_s, sems = refs[last + first :]
-    part, capacity, width = rec_refs[0].shape
-    devices = last * part
+    out_refs = refs[:first]
+    rec_s, x_s, sgt_s, tab_s, sems = refs[first:]
+    devices, capacity, width = rec_ref.shape
     slots = devices * capacity
     n_time = sgt_ref.shape[2]
     half = n_time // 2
     quarter = half // 2
     n_slip = width - 128
     wide = 512
-    steps = n_time // wide
-
-    def rows_copy(c, n):
-        at = (slice(6 * c, 6 * c + 6), slice(None), slice(n * wide, (n + 1) * wide))
-        return pltpu.make_async_copy(sgt_ref.at[at], sgt_s.at[at], sems.at[c * steps + n])
-
+    copies = []
     for c in range(3):
-        for n in range(steps):
-            rows_copy(c, n).start()
+        at = slice(6 * c, 6 * c + 6)
+        copies.append(pltpu.make_async_copy(sgt_ref.at[at], sgt_s.at[at], sems.at[c]))
+    for q, ref in enumerate((even_ref, odd_ref)):
+        copies.append(pltpu.make_async_copy(ref, tab_s.at[q], sems.at[3 + q]))
+    for copy in copies:
+        copy.start()
     for d in range(devices):
-        rec_s[d * capacity : (d + 1) * capacity, :] = rec_refs[d // part][d % part].astype(F32)
+        rec_s[d * capacity : (d + 1) * capacity, :] = rec_ref[d].astype(F32)
     tail = rec_s[:, n_slip:]
     row = tail[:, ROW_LANE : ROW_LANE + 1]
     here = iota((slots, PTS), 1).astype(F32) == row
@@ -188,48 +165,41 @@
         axis=0,
     )
     for c in range(3):
-        for n in range(steps):
-            rows_copy(c, n).wait()
-            rows = sgt_s[6 * c : 6 * c + 6, :, n * wide : (n + 1) * wide].reshape(6 * PTS, wide)
-            out = nn(left, rows)
-            h, at = divmod(n * wide, half)
-            x_s[c, h * slots : (h + 1) * slots, at : at + wide] = (out[:slots] + out[slots:]).astype(BF16)
+        copies[c].wait()
+        for at in range(0, half, wide):
+            ends = []
+            for start in (at, half + at):
+                rows = sgt_s[6 * c : 6 * c + 6, :, start : start + wide].reshape(6 * PTS, wide)
+                out = nn(left, rows)
+                ends.append(out[:slots] + out[slots:])
+            x_s[c, 0, :, at : at + wide] = (ends[0] + ends[1]).astype(BF16)
+            x_s[c, 1, :, at : at + wide] = (ends[0] - ends[1]).astype(BF16)
 
     ruptures = math.prod(radix for _, radix, _, _ in stages)
     shape = (ruptures, slots)
     rup = nt((iota((8, 128), 1) == RUP_LANE).astype(F32).astype(BF16), tail.astype(BF16))[:1].astype(jnp.int32)
-    chunk = iota((1, slots), 1) // capacity
-    apart = {"worker": jnp.zeros_like(chunk), "server": rup ^ lax.axis_index("server")}
-    for axis, radix, shift, _ in stages[-2::-1]:
-        if axis == "worker":
-            apart[axis] = apart[axis] | ((chunk % radix) << shift)
-        chunk = chunk // radix
+    worker = (iota((1, slots), 1) // capacity) % lax.axis_size("worker")
+    apart = {"worker": worker ^ lax.axis_index("worker"), "server": rup ^ lax.axis_index("server")}
     where_to = ordered(stages, apart)
     seg = (iota(shape, 0) == where_to).astype(F32).astype(BF16)
+    seg = jnp.concatenate([seg, seg], axis=1)
     slip = rec_s[:, :n_slip].astype(BF16)
     part = ruptures // first
     for q in range(2):
         re = slice(q * quarter, (q + 1) * quarter)
         im = slice(half + q * quarter, half + (q + 1) * quarter)
-        tab_ref = (even_ref, odd_ref)[q]
-        slip_re = nn(slip, tab_ref[:n_slip, :quarter])
-        slip_im = nn(slip, tab_ref[:n_slip, quarter:])
+        copies[3 + q].wait()
+        slip_re = nn(slip, tab_s[q, :n_slip, :quarter])
+        slip_im = nn(slip, tab_s[q, :n_slip, quarter:])
         for c in range(3):
-            x = x_s[c]
-            u_re = nn(x, tab_ref[:, :quarter])
-            u_im = nn(x, tab_ref[:, quarter:])
-            if q == 0:
-                t_re = u_re[:slots] + u_re[slots:]
-                t_im = u_im[:slots] + u_im[slots:]
-            else:
-                t_re = u_re[:slots] - u_re[slots:]
-                t_im = u_im[:slots] - u_im[slots:]
+            x = x_s[c, q]
+            t_re = nn(x, tab_s[q, :, :quarter])
+            t_im = nn(x, tab_s[q, :, quarter:])
             for cols, prod in (
                 (re, slip_re * t_re - slip_im * t_im),
                 (im, slip_re * t_im + slip_im * t_re),
             ):
-                hi, lo = hilo(prod)
-                total = nn(seg, hi) + nn(seg, lo)
+                total = nn(seg, jnp.concatenate(hilo(prod), axis=0))
                 for k in range(first):
                     ref = out_refs[k]
                     ref[c, :, cols] = total[k * part : (k + 1) * part].astype(ref.dtype)
@@ -359,6 +329,10 @@
     return pl.BlockSpec(memory_space=pltpu.HBM)
 
 
+def in_hbm(x):
+    return pltpu.with_memory_space_constraint(x, pltpu.HBM)
+
+
 def params(mib):
     return pltpu.CompilerParams(vmem_limit_bytes=mib << 20)
 
@@ -380,7 +354,7 @@
     axis, radix, shift, size = stage
     return [
         lax.ppermute(parts[k], axis, [(i, i ^ (k << shift)) for i in range(size)])
-        for k in range(1, radix)
+        for k in range(radix - 1, 0, -1)
     ]
 
 
@@ -417,15 +391,11 @@
         name="forward_table",
     )
 
-    def record_shapes(i):
-        chunk = (devices // stages[i][1], capacity, width)
-        return [jax.ShapeDtypeStruct(chunk, BF16)] * stages[i][1]
-
-    records = pl.pallas_call(
-        functools.partial(pack_kernel, stages, capacity),
-        out_shape=record_shapes(0),
+    record = pl.pallas_call(
+        pack_kernel,
+        out_shape=jax.ShapeDtypeStruct((devices, capacity, width), BF16),
         in_specs=[hbm()] * 4,
-        out_specs=[vmem()] * stages[0][1],
+        out_specs=vmem(),
         scratch_shapes=[
             pltpu.VMEM((slots, width), F32),
             pltpu.VMEM((ownership.shape[0] // 128, 128), jnp.int32),
@@ -438,7 +408,7 @@
         name="pack",
     )(
         *[
-            pltpu.with_memory_space_constraint(x, pltpu.HBM)
+            in_hbm(x)
             for x in (
                 ownership.reshape(-1, 128),
                 sub_points[0],
@@ -447,27 +417,8 @@
             )
         ]
     )
-    seen = 1
-    bases = forward_bases(n_time)
-    forwards = []
-    for i in range(len(stages)):
-        arrived = send(records, stages[i])
-        own = records[0]
-        if i >= len(stages) - 2:
-            own, table = beside(forward, bases[len(forwards)], own)
-            forwards += table
-        records = [own, *arrived]
-        if i + 1 < len(stages):
-            count = len(records)
-            records = pl.pallas_call(
-                functools.partial(pass_kernel, seen, count),
-                out_shape=record_shapes(i + 1),
-                in_specs=[vmem()] * count,
-                out_specs=[vmem()] * stages[i + 1][1],
-                compiler_params=params(2),
-                name=f"pass_{i}",
-            )(*records)
-            seen *= count
+    record = lax.all_to_all(record, ("server", "worker"), split_axis=0, concat_axis=0, tiled=True)
+    forwards = [in_hbm(forward(jnp.asarray(base))[0]) for base in forward_bases(n_time)]
 
     inverse = pl.pallas_call(
         inverse_table_kernel,
@@ -498,18 +449,19 @@
     parts = pl.pallas_call(
         functools.partial(owner_kernel, stages),
         out_shape=part_shapes(0),
-        in_specs=[hbm()] + [vmem()] * (2 + stages[-1][1]),
+        in_specs=[vmem()] + [hbm()] * 3,
         out_specs=[vmem()] * stages[0][1],
         scratch_shapes=[
             pltpu.VMEM((slots, width), F32),
-            pltpu.VMEM((3, 2 * slots, half), BF16),
+            pltpu.VMEM((3, 2, slots, half), BF16),
             pltpu.VMEM((18, PTS, n_time), BF16),
-            pltpu.SemaphoreType.DMA((12,)),
+            pltpu.VMEM((2, half, half), BF16),
+            pltpu.SemaphoreType.DMA((5,)),
         ],
-        compiler_params=params(32),
+        compiler_params=params(36),
         cost_estimate=pl.CostEstimate(flops=10**10, bytes_accessed=2 * 10**7, transcendentals=0),
         name="owner",
-    )(pltpu.with_memory_space_constraint(jnp.transpose(sgt, (1, 0, 2)), pltpu.HBM), *forwards, *records)
+    )(record, in_hbm(jnp.transpose(sgt, (1, 0, 2))), *forwards)
     arrived = send(parts, stages[0])
     for i in range(1, len(stages)):
         radix = stages[i][1]

time: 51.8 us -> 45.4 us (0.88)
  waiting for transfers between devices: 12.2 us -> 6.36 us
  local copies, waits for them, and re-layouts: 0.97 us -> 3.59 us
  starting transfers between devices: 17.5 us -> 15.8 us
  Pallas kernels: 20.2 us -> 18.8 us
    ppermute x14 -> x7, starting transfers between devices: 17.5 us -> 8.48 us  [send(): lax.ppermute(parts[k], axis, [(i, i ^ k << shift) for i in range(size)])]
    ppermute x14 -> x7, waiting for transfers between devices: 12.2 us -> 3.24 us  [send(): lax.ppermute(parts[k], axis, [(i, i ^ k << shift) for i in range(size)])]
    all_to_all x0 -> x1, starting transfers between devices: none -> 7.3 us  [shards(): lax.all_to_all(record, ('server', 'worker'), split_axis=0, concat_axis=0,...]
    all_to_all x0 -> x1, waiting for transfers between devices: none -> 3.11 us  [shards(): lax.all_to_all(record, ('server', 'worker'), split_axis=0, concat_axis=0,...]
    unnamed x8 -> x12, local copies, waits for them, and re-layouts: 0.97 us -> 3.59 us
    pallas_call x3, Pallas kernels: 1.64 us -> 4.12 us  [the longest x1 2.27 us: shards(): pl.pallas_call(pack_kernel, out_shape=jax.ShapeDtypeStruct((devices, capa...]
    pallas_call x1, Pallas kernels: 11.1 us -> 8.97 us  [shards(): pl.pallas_call(functools.partial(owner_kernel, stages), out_shape=part_sh...]
    pallas_call x4 -> x2, Pallas kernels: 4.52 us -> 2.68 us  [beside(): own, *made = lax.optimization_barrier((own, *kernel(base)))]
  transfers between devices with their start and end apart: 14 -> 8, of which waited for: 9 -> 7; matrix products, arithmetic and copies ran while one was open for 0% -> 0% of each run, Pallas kernels for 9% -> 10%
where the time goes in v4:
time: 45.4 us; the launch traced here: 45.2 us
  Pallas kernels  18.8 us (41%)
  starting transfers between devices  15.8 us (35%)
  waiting for transfers between devices  6.36 us (14%)
  local copies, waits for them, and re-layouts  3.59 us (8%)
  between operations  0.75 us (2%)
    pallas_call x1, Pallas kernels, shards(): pl.pallas_call(functools.partial(owner_kernel, stages), out_shape=part_sh...  8.97 us
    ppermute x7, starting transfers between devices, send(): lax.ppermute(parts[k], axis, [(i, i ^ k << shift) for i in range(size)])  8.48 us
    all_to_all x1, starting transfers between devices, shards(): lax.all_to_all(record, ('server', 'worker'), split_axis=0, concat_axis=0,...  7.3 us
    unnamed x12, local copies, waits for them, and re-layouts  3.59 us
    ppermute x7, waiting for transfers between devices, send(): lax.ppermute(parts[k], axis, [(i, i ^ k << shift) for i in range(size)])  3.24 us
    all_to_all x1, waiting for transfers between devices, shards(): lax.all_to_all(record, ('server', 'worker'), split_axis=0, concat_axis=0,...  3.11 us
    pallas_call x1, Pallas kernels, shards(): pl.pallas_call(functools.partial(final_kernel, count), out_shape=[jax.Sha...  2.8 us
    pallas_call x2, Pallas kernels, beside(): own, *made = lax.optimization_barrier((own, *kernel(base)))  2.68 us
  transfers between devices with their start and end apart: 8, of which 7 were waited for; matrix products, arithmetic and copies ran while one was open for 0% of the time, Pallas kernels for 10%

profile of v4, /device:TPU:0, one launch (start us, length us, event | category | flops | bytes accessed | tf_op | source)
XLA Modules:
  0.0 45.2 jit_solution(6079215786722271221)
XLA Ops:
  0.6 0.0 copy-start.3
  0.6 2.3 %pack.1 = bf16[32,4,640]{2,1,0:T(4,128)(2,1)} custom-call(s32[32,128]{1,0:T(8,128)} %bitcast.14, s32[4,24]{1,0:T(4,128)} %bitcast.16, f32[6,4,24]{2,1,0:T(4,128)} %bitcast.15, bf16[4,24,512]{2,1,0:T(8,128)(2,1)} %bitcast.13), custom_call_target="tpu_custom_call" | custom-call | tf_op jit(solution)/shard_map/pack/pallas_call | solution.py:394
  2.9 7.3 %all-to-all-start = ((bf16[32,4,640]{2,1,0:T(4,128)(2,1)}), bf16[32,4,640]{2,1,0:T(4,128)(2,1)S(1)}, u32[]{:S(2)}, u32[]{:S(2)}) async-start(bf16[32,4,640]{2,1,0:T(4,128)(2,1)} %pack.1), calls=%async_computation | async-start | bytes 327680 | tf_op jit(solution)/shard_map/all_to_all | solution.py:420
  10.2 0.0 copy-start.2
  10.2 0.9 %copy-done.2 = f32[128,512]{1,0:T(8,128)S(1)} copy-done((f32[128,512]{1,0:T(8,128)S(1)}, f32[128,512]{1,0:T(8,128)}, u32[]{:S(2)}) %copy-start.2) | copy-done | bytes 262168
  11.2 0.9 %forward_table.2.even_ref = bf16[1024,1024]{1,0:T(8,128)(2,1)S(1)} custom-call(f32[128,512]{1,0:T(8,128)S(1)} %copy-done.2), custom_call_target="tpu_custom_call" | custom-call | flops 1000000000 | bytes 10000000 | tf_op jit(solution)/shard_map/forward_table/pallas_call | solution.py:421
  12.1 0.0 copy-start.4
  12.1 1.3 %copy-done.4 = bf16[1024,1024]{1,0:T(8,128)(2,1)} copy-done((bf16[1024,1024]{1,0:T(8,128)(2,1)}, bf16[1024,1024]{1,0:T(8,128)(2,1)S(1)}, u32[]{:S(2)}) %copy-start.4) | copy-done | bytes 2097176
  13.5 0.0 copy-done.3
  13.5 0.9 %forward_table.3.odd_ref = bf16[1024,1024]{1,0:T(8,128)(2,1)S(1)} custom-call(f32[128,512]{1,0:T(8,128)S(1)} %copy-done.3), custom_call_target="tpu_custom_call" | custom-call | flops 1000000000 | bytes 10000000 | tf_op jit(solution)/shard_map/forward_table/pallas_call | solution.py:421
  14.4 0.0 copy-start.5
  14.4 1.3 %copy-done.5 = bf16[1024,1024]{1,0:T(8,128)(2,1)} copy-done((bf16[1024,1024]{1,0:T(8,128)(2,1)}, bf16[1024,1024]{1,0:T(8,128)(2,1)S(1)}, u32[]{:S(2)}) %copy-start.5) | copy-done | bytes 2097176
  15.7 3.1 %all-to-all-done.rec_ref = bf16[32,4,640]{2,1,0:T(4,128)(2,1)S(1)} async-done(((bf16[32,4,640]{2,1,0:T(4,128)(2,1)}), bf16[32,4,640]{2,1,0:T(4,128)(2,1)S(1)}, u32[]{:S(2)}, u32[]{:S(2)}) %all-to-all-start) | async-done | bytes 163872 | tf_op jit(solution)/shard_map/all_to_all | solution.py:420
  18.8 0.0 copy-start.1
  18.8 9.0 %owner.1 = (f32[3,16,2048]{2,1,0:T(8,128)S(1)}, f32[3,16,2048]{2,1,0:T(8,128)S(1)}) custom-call(bf16[32,4,640]{2,1,0:T(4,128)(2,1)S(1)} %all-to-all-done.rec_ref, bf16[18,128,2048]{2,1,0:T(8,128)(2,1)} %bitcast.17, bf16[1024,1024]{1,0:T(8,128)(2,1)} %copy-done.4, bf16[1024,1024]{1,0:T(8,128)(2,1)} %copy-done.5), custom_call_target="tpu_custom_call" | custom-call | flops 10000000000 | bytes 20000000 | tf_op jit(solution)/shard_map/owner/pallas_call | solution.py:449
  27.8 0.5 %collective-permute-start = (f32[3,16,2048]{2,1,0:T(8,128)S(1)}, f32[3,16,2048]{2,1,0:T(8,128)S(1)}, u32[]{:S(2)}, u32[]{:S(2)}) collective-permute-start(f32[3,16,2048]{2,1,0:T(8,128)S(1)} %get-tuple-element.31), channel_id=1, source_target_pairs={{0,1},{1,0},{2,3},{3,2},{4,5},{5,4},{6,7},{7,6},{8,9},{9,8},{10,11... | collective-permute-start | bytes 1179656 | tf_op jit(solution)/shard_map/ppermute | solution.py:356
  28.2 0.1 gain.1
  28.4 1.2 %collective-permute-done.refs_1_ = f32[3,16,2048]{2,1,0:T(8,128)S(1)} collective-permute-done((f32[3,16,2048]{2,1,0:T(8,128)S(1)}, f32[3,16,2048]{2,1,0:T(8,128)S(1)}, u32[]{:S(2)}, u32[]{:S(2)}) %collective-permute-start) | collective-permute-done | bytes 393248 | tf_op jit(solution)/shard_map/ppermute | solution.py:356
  29.6 0.0 copy-start
  29.6 1.1 %collective-permute-start.1 = (bf16[3,4,2048]{2,1,0:T(4,128)(2,1)S(1)}, bf16[3,4,2048]{2,1,0:T(4,128)(2,1)S(1)}, u32[]{:S(2)}, u32[]{:S(2)}) collective-permute-start(bf16[3,4,2048]{2,1,0:T(4,128)(2,1)S(1)} %get-tuple-element.38), channel_id=1, source_target_pairs={{0,6},{1,7},{2,4},{3,5},{4,2},{5,3},{6,0},{7,1},{8,14},{9,15},{10,... | collective-permute-start | bytes 147464 | tf_op jit(solution)/shard_map/ppermute | solution.py:356
  30.7 1.0 %collective-permute-start.2 = (bf16[3,4,2048]{2,1,0:T(4,128)(2,1)S(1)}, bf16[3,4,2048]{2,1,0:T(4,128)(2,1)S(1)}, u32[]{:S(2)}, u32[]{:S(2)}) collective-permute-start(bf16[3,4,2048]{2,1,0:T(4,128)(2,1)S(1)} %get-tuple-element.39), channel_id=1, source_target_pairs={{0,4},{1,5},{2,6},{3,7},{4,0},{5,1},{6,2},{7,3},{8,12},{9,13},{10,... | collective-permute-start | bytes 147464 | tf_op jit(solution)/shard_map/ppermute | solution.py:356
  31.8 1.5 %collective-permute-start.3 = (bf16[3,4,2048]{2,1,0:T(4,128)(2,1)S(1)}, bf16[3,4,2048]{2,1,0:T(4,128)(2,1)S(1)}, u32[]{:S(2)}, u32[]{:S(2)}) collective-permute-start(bf16[3,4,2048]{2,1,0:T(4,128)(2,1)S(1)} %get-tuple-element.40), channel_id=1, source_target_pairs={{0,2},{1,3},{2,0},{3,1},{4,6},{5,7},{6,4},{7,5},{8,10},{9,11},{10,... | collective-permute-start | bytes 147464 | tf_op jit(solution)/shard_map/ppermute | solution.py:356
  33.2 0.0 copy-done.1
  33.2 1.3 %inverse_table.2 = (bf16[1024,1024]{1,0:T(8,128)(2,1)S(1)}, bf16[1024,1024]{1,0:T(8,128)(2,1)S(1)}) custom-call(f32[96,1024]{1,0:T(8,128)S(1)} %copy-done.1), custom_call_target="tpu_custom_call" | custom-call | flops 1000000000 | bytes 10000000 | tf_op jit(solution)/shard_map/inverse_table/pallas_call | solution.py:363
  34.6 0.5 %collective-permute-done.1.refs_1_ = bf16[3,4,2048]{2,1,0:T(4,128)(2,1)S(1)} collective-permute-done((bf16[3,4,2048]{2,1,0:T(4,128)(2,1)S(1)}, bf16[3,4,2048]{2,1,0:T(4,128)(2,1)S(1)}, u32[]{:S(2)}, u32[]{:S(2)}) %collective-permute-start.1) | collective-permute-done | bytes 49184 | tf_op jit(solution)/shard_map/ppermute | solution.py:356
  35.1 0.2 collective-permute-done.2.refs_2_
  35.3 0.6 %collective-permute-done.3.refs_3_ = bf16[3,4,2048]{2,1,0:T(4,128)(2,1)S(1)} collective-permute-done((bf16[3,4,2048]{2,1,0:T(4,128)(2,1)S(1)}, bf16[3,4,2048]{2,1,0:T(4,128)(2,1)S(1)}, u32[]{:S(2)}, u32[]{:S(2)}) %collective-permute-start.3) | collective-permute-done | bytes 49184 | tf_op jit(solution)/shard_map/ppermute | solution.py:356
  35.9 1.5 %collective-permute-start.4 = (f32[3,1,2048]{2,1,0:T(1,128)S(1)}, f32[3,1,2048]{2,1,0:T(1,128)S(1)}, u32[]{:S(2)}, u32[]{:S(2)}) collective-permute-start(f32[3,1,2048]{2,1,0:T(1,128)S(1)} %get-tuple-element.47), channel_id=1, source_target_pairs={{0,24},{8,16},{16,8},{24,0},{1,25},{9,17},{17,9},{25,1},{2,26},{10... | collective-permute-start | bytes 73736 | tf_op jit(solution)/shard_map/ppermute | solution.py:356
  37.4 0.4 collective-permute-start.5
  37.8 2.5 %collective-permute-start.6 = (f32[3,1,2048]{2,1,0:T(1,128)S(1)}, f32[3,1,2048]{2,1,0:T(1,128)S(1)}, u32[]{:S(2)}, u32[]{:S(2)}) collective-permute-start(f32[3,1,2048]{2,1,0:T(1,128)S(1)} %get-tuple-element.49), channel_id=1, source_target_pairs={{0,8},{8,0},{16,24},{24,16},{1,9},{9,1},{17,25},{25,17},{2,10},{10... | collective-permute-start | bytes 73736 | tf_op jit(solution)/shard_map/ppermute | solution.py:356
  40.3 0.0 copy-done
  40.4 1.3 %inverse_table.3 = (bf16[1024,1024]{1,0:T(8,128)(2,1)S(1)}, bf16[1024,1024]{1,0:T(8,128)(2,1)S(1)}) custom-call(f32[96,1024]{1,0:T(8,128)S(1)} %copy-done), custom_call_target="tpu_custom_call" | custom-call | flops 1000000000 | bytes 10000000 | tf_op jit(solution)/shard_map/inverse_table/pallas_call | solution.py:363
  41.7 0.1 collective-permute-done.4.refs_1_
  41.8 0.6 %collective-permute-done.5.refs_2_ = f32[3,1,2048]{2,1,0:T(1,128)S(1)} collective-permute-done((f32[3,1,2048]{2,1,0:T(1,128)S(1)}, f32[3,1,2048]{2,1,0:T(1,128)S(1)}, u32[]{:S(2)}, u32[]{:S(2)}) %collective-permute-start.5) | collective-permute-done | bytes 24608 | tf_op jit(solution)/shard_map/ppermute | solution.py:356
  42.4 0.0 collective-permute-done.6.refs_3_
  42.4 2.8 %finish.1 = (f32[3,1,2048]{2,1,0:T(1,128)}, f32[3,1,44]{2,1,0:T(1,128)}) custom-call(f32[3,1,2048]{2,1,0:T(1,128)S(1)} %get-tuple-element.46.refs_0_, f32[3,1,2048]{2,1,0:T(1,128)S(1)} %collective-permute-done.4.refs_1_, f32[3,1,2048]{2,1,0:T(1,128)S(1)} %collective-permute-done.5.refs_2_, f32[3,1,2048]{2,1,0:T(1,128)S(1)} %collective-permute-done.6.refs_3_, ...), custom_call_target="tpu_custom_call" | custom-call | tf_op jit(solution)/shard_map/finish/pallas_call | solution.py:482
  (2 shorter events, 0.1 us)
Async XLA Ops:
  0.6 12.8 %copy-start.3 = (f32[128,512]{1,0:T(8,128)S(1)}, f32[128,512]{1,0:T(8,128)}, u32[]{:S(2)}) copy-start(f32[128,512]{1,0:T(8,128)} %constant.9.clone.base_ref) | copy-start | bytes 786436
  2.9 15.9 %all-to-all-start = ((bf16[32,4,640]{2,1,0:T(4,128)(2,1)}), bf16[32,4,640]{2,1,0:T(4,128)(2,1)S(1)}, u32[]{:S(2)}, u32[]{:S(2)}) async-start(bf16[32,4,640]{2,1,0:T(4,128)(2,1)} %pack.1), calls=%async_computation | async-start | bytes 327680 | tf_op jit(solution)/shard_map/all_to_all | solution.py:420
  10.2 1.0 %copy-start.2 = (f32[128,512]{1,0:T(8,128)S(1)}, f32[128,512]{1,0:T(8,128)}, u32[]{:S(2)}) copy-start(f32[128,512]{1,0:T(8,128)} %constant.8.clone.base_ref) | copy-start | bytes 786436
  12.1 1.3 %copy-start.4 = (bf16[1024,1024]{1,0:T(8,128)(2,1)}, bf16[1024,1024]{1,0:T(8,128)(2,1)S(1)}, u32[]{:S(2)}) copy-start(bf16[1024,1024]{1,0:T(8,128)(2,1)S(1)} %forward_table.2.even_ref) | copy-start | bytes 6291460
  14.4 1.3 %copy-start.5 = (bf16[1024,1024]{1,0:T(8,128)(2,1)}, bf16[1024,1024]{1,0:T(8,128)(2,1)S(1)}, u32[]{:S(2)}) copy-start(bf16[1024,1024]{1,0:T(8,128)(2,1)S(1)} %forward_table.3.odd_ref) | copy-start | bytes 6291460
  18.8 14.4 %copy-start.1 = (f32[96,1024]{1,0:T(8,128)S(1)}, f32[96,1024]{1,0:T(8,128)}, u32[]{:S(2)}) copy-start(f32[96,1024]{1,0:T(8,128)} %constant.10.clone.base_ref) | copy-start | bytes 1179652
  27.8 1.8 %collective-permute-start = (f32[3,16,2048]{2,1,0:T(8,128)S(1)}, f32[3,16,2048]{2,1,0:T(8,128)S(1)}, u32[]{:S(2)}, u32[]{:S(2)}) collective-permute-start(f32[3,16,2048]{2,1,0:T(8,128)S(1)} %get-tuple-element.31), channel_id=1, source_target_pairs={{0,1},{1,0},{2,3},{3,2},{4,5},{5,4},{6,7},{7,6},{8,9},{9,8},{10,11... | collective-permute-start | bytes 1179656 | tf_op jit(solution)/shard_map/ppermute | solution.py:356
  29.6 10.7 %copy-start = (f32[96,1024]{1,0:T(8,128)S(1)}, f32[96,1024]{1,0:T(8,128)}, u32[]{:S(2)}) copy-start(f32[96,1024]{1,0:T(8,128)} %constant.11.clone.base_ref) | copy-start | bytes 1179652
  29.6 5.4 %collective-permute-start.1 = (bf16[3,4,2048]{2,1,0:T(4,128)(2,1)S(1)}, bf16[3,4,2048]{2,1,0:T(4,128)(2,1)S(1)}, u32[]{:S(2)}, u32[]{:S(2)}) collective-permute-start(bf16[3,4,2048]{2,1,0:T(4,128)(2,1)S(1)} %get-tuple-element.38), channel_id=1, source_target_pairs={{0,6},{1,7},{2,4},{3,5},{4,2},{5,3},{6,0},{7,1},{8,14},{9,15},{10,... | collective-permute-start | bytes 147464 | tf_op jit(solution)/shard_map/ppermute | solution.py:356
  30.7 4.6 %collective-permute-start.2 = (bf16[3,4,2048]{2,1,0:T(4,128)(2,1)S(1)}, bf16[3,4,2048]{2,1,0:T(4,128)(2,1)S(1)}, u32[]{:S(2)}, u32[]{:S(2)}) collective-permute-start(bf16[3,4,2048]{2,1,0:T(4,128)(2,1)S(1)} %get-tuple-element.39), channel_id=1, source_target_pairs={{0,4},{1,5},{2,6},{3,7},{4,0},{5,1},{6,2},{7,3},{8,12},{9,13},{10,... | collective-permute-start | bytes 147464 | tf_op jit(solution)/shard_map/ppermute | solution.py:356
  31.8 4.1 %collective-permute-start.3 = (bf16[3,4,2048]{2,1,0:T(4,128)(2,1)S(1)}, bf16[3,4,2048]{2,1,0:T(4,128)(2,1)S(1)}, u32[]{:S(2)}, u32[]{:S(2)}) collective-permute-start(bf16[3,4,2048]{2,1,0:T(4,128)(2,1)S(1)} %get-tuple-element.40), channel_id=1, source_target_pairs={{0,2},{1,3},{2,0},{3,1},{4,6},{5,7},{6,4},{7,5},{8,10},{9,11},{10,... | collective-permute-start | bytes 147464 | tf_op jit(solution)/shard_map/ppermute | solution.py:356
  35.9 5.9 %collective-permute-start.4 = (f32[3,1,2048]{2,1,0:T(1,128)S(1)}, f32[3,1,2048]{2,1,0:T(1,128)S(1)}, u32[]{:S(2)}, u32[]{:S(2)}) collective-permute-start(f32[3,1,2048]{2,1,0:T(1,128)S(1)} %get-tuple-element.47), channel_id=1, source_target_pairs={{0,24},{8,16},{16,8},{24,0},{1,25},{9,17},{17,9},{25,1},{2,26},{10... | collective-permute-start | bytes 73736 | tf_op jit(solution)/shard_map/ppermute | solution.py:356
  37.4 5.0 %collective-permute-start.5 = (f32[3,1,2048]{2,1,0:T(1,128)S(1)}, f32[3,1,2048]{2,1,0:T(1,128)S(1)}, u32[]{:S(2)}, u32[]{:S(2)}) collective-permute-start(f32[3,1,2048]{2,1,0:T(1,128)S(1)} %get-tuple-element.48), channel_id=1, source_target_pairs={{0,16},{8,24},{16,0},{24,8},{1,17},{9,25},{17,1},{25,9},{2,18},{10... | collective-permute-start | bytes 73736 | tf_op jit(solution)/shard_map/ppermute | solution.py:356
  37.8 4.6 %collective-permute-start.6 = (f32[3,1,2048]{2,1,0:T(1,128)S(1)}, f32[3,1,2048]{2,1,0:T(1,128)S(1)}, u32[]{:S(2)}, u32[]{:S(2)}) collective-permute-start(f32[3,1,2048]{2,1,0:T(1,128)S(1)} %get-tuple-element.49), channel_id=1, source_target_pairs={{0,8},{8,0},{16,24},{24,16},{1,9},{9,1},{17,25},{25,17},{2,10},{10... | collective-permute-start | bytes 73736 | tf_op jit(solution)/shard_map/ppermute | solution.py:356

commit v5 on v4

--- a/solution.py
+++ b/solution.py
@@ -14,6 +14,7 @@
 ROWS = 48
 STEP = 32
 PTS = 128
+DFT_WIDE = 512
 ROW_LANE = 64
 RUP_LANE = 96
 F32 = jnp.float32
@@ -130,10 +131,32 @@
         out_ref[d] = scr[d * capacity : (d + 1) * capacity, :].astype(BF16)
 
 
-def owner_kernel(stages, rec_ref, sgt_ref, even_ref, odd_ref, *refs):
+def forward_table(base_ref, tab_ref):
+    half, width = tab_ref.shape
+    quarter = width // 2
+    count = half // STEP
+    wide = 256
+    for lc in range(quarter // wide):
+        sl = slice(lc * wide, (lc + 1) * wide)
+        sl2 = slice(quarter + lc * wide, quarter + (lc + 1) * wide)
+        cb = base_ref[2 * count : 2 * count + STEP, sl]
+        sb = base_ref[2 * count + STEP :, sl]
+
+        def table(a, carry):
+            ca = base_ref[pl.ds(a, 1), sl]
+            sa = base_ref[pl.ds(count + a, 1), sl]
+            at = pl.ds(pl.multiple_of(a * STEP, STEP), STEP)
+            tab_ref[at, sl] = (ca * cb - sa * sb).astype(BF16)
+            tab_ref[at, sl2] = (-(sa * cb + ca * sb)).astype(BF16)
+            return carry
+
+        lax.fori_loop(0, count, table, 0, unroll=4)
+
+
+def owner_kernel(stages, rec_ref, sgt_ref, base_ref, *refs):
     first = stages[0][1]
     out_refs = refs[:first]
-    rec_s, x_s, sgt_s, tab_s, sems = refs[first:]
+    rec_s, x_s, sgt_s, base_s, tab_s, sems = refs[first:]
     devices, capacity, width = rec_ref.shape
     slots = devices * capacity
     n_time = sgt_ref.shape[2]
@@ -141,14 +164,13 @@
     quarter = half // 2
     n_slip = width - 128
     wide = 512
+    base_copy = pltpu.make_async_copy(base_ref, base_s, sems.at[3])
+    base_copy.start()
     copies = []
     for c in range(3):
         at = slice(6 * c, 6 * c + 6)
         copies.append(pltpu.make_async_copy(sgt_ref.at[at], sgt_s.at[at], sems.at[c]))
-    for q, ref in enumerate((even_ref, odd_ref)):
-        copies.append(pltpu.make_async_copy(ref, tab_s.at[q], sems.at[3 + q]))
-    for copy in copies:
-        copy.start()
+        copies[c].start()
     for d in range(devices):
         rec_s[d * capacity : (d + 1) * capacity, :] = rec_ref[d].astype(F32)
     tail = rec_s[:, n_slip:]
@@ -164,7 +186,10 @@
         ],
         axis=0,
     )
+    base_copy.wait()
     for c in range(3):
+        if c < 2:
+            forward_table(base_s.at[c], tab_s.at[c])
         copies[c].wait()
         for at in range(0, half, wide):
             ends = []
@@ -172,8 +197,8 @@
                 rows = sgt_s[6 * c : 6 * c + 6, :, start : start + wide].reshape(6 * PTS, wide)
                 out = nn(left, rows)
                 ends.append(out[:slots] + out[slots:])
-            x_s[c, 0, :, at : at + wide] = (ends[0] + ends[1]).astype(BF16)
-            x_s[c, 1, :, at : at + wide] = (ends[0] - ends[1]).astype(BF16)
+            x_s[0, c * slots : (c + 1) * slots, at : at + wide] = (ends[0] + ends[1]).astype(BF16)
+            x_s[1, c * slots : (c + 1) * slots, at : at + wide] = (ends[0] - ends[1]).astype(BF16)
 
     ruptures = math.prod(radix for _, radix, _, _ in stages)
     shape = (ruptures, slots)
@@ -186,23 +211,25 @@
     slip = rec_s[:, :n_slip].astype(BF16)
     part = ruptures // first
     for q in range(2):
-        re = slice(q * quarter, (q + 1) * quarter)
-        im = slice(half + q * quarter, half + (q + 1) * quarter)
-        copies[3 + q].wait()
-        slip_re = nn(slip, tab_s[q, :n_slip, :quarter])
-        slip_im = nn(slip, tab_s[q, :n_slip, quarter:])
-        for c in range(3):
-            x = x_s[c, q]
-            t_re = nn(x, tab_s[q, :, :quarter])
-            t_im = nn(x, tab_s[q, :, quarter:])
-            for cols, prod in (
-                (re, slip_re * t_re - slip_im * t_im),
-                (im, slip_re * t_im + slip_im * t_re),
-            ):
-                total = nn(seg, jnp.concatenate(hilo(prod), axis=0))
-                for k in range(first):
-                    ref = out_refs[k]
-                    ref[c, :, cols] = total[k * part : (k + 1) * part].astype(ref.dtype)
+        for at in range(0, quarter, DFT_WIDE):
+            cols = slice(at, at + DFT_WIDE)
+            cols_im = slice(quarter + at, quarter + at + DFT_WIDE)
+            slip_re = nn(slip, tab_s[q, :n_slip, cols])
+            slip_im = nn(slip, tab_s[q, :n_slip, cols_im])
+            all_re = nn(x_s[q], tab_s[q, :, cols])
+            all_im = nn(x_s[q], tab_s[q, :, cols_im])
+            for c in range(3):
+                t_re = all_re[c * slots : (c + 1) * slots]
+                t_im = all_im[c * slots : (c + 1) * slots]
+                for base, prod in (
+                    (0, slip_re * t_re - slip_im * t_im),
+                    (half, slip_re * t_im + slip_im * t_re),
+                ):
+                    start = base + q * quarter + at
+                    total = nn(seg, jnp.concatenate(hilo(prod), axis=0))
+                    for k in range(first):
+                        ref = out_refs[k]
+                        ref[c, :, start : start + DFT_WIDE] = total[k * part : (k + 1) * part].astype(ref.dtype)
 
 
 def sum_kernel(radix, *refs):
@@ -215,28 +242,6 @@
             total = total + ref[c].astype(F32)
         for k in range(radix):
             out_refs[k][c] = total[k * part : (k + 1) * part].astype(out_refs[k].dtype)
-
-
-def forward_table_kernel(base_ref, tab_ref):
-    half = tab_ref.shape[0]
-    quarter = half // 2
-    count = half // STEP
-    wide = 256
-    for lc in range(quarter // wide):
-        sl = slice(lc * wide, (lc + 1) * wide)
-        sl2 = slice(quarter + lc * wide, quarter + (lc + 1) * wide)
-        cb = base_ref[2 * count : 2 * count + STEP, sl]
-        sb = base_ref[2 * count + STEP :, sl]
-
-        def table(a, carry):
-            ca = base_ref[pl.ds(a, 1), sl]
-            sa = base_ref[pl.ds(count + a, 1), sl]
-            at = pl.ds(pl.multiple_of(a * STEP, STEP), STEP)
-            tab_ref[at, sl] = (ca * cb - sa * sb).astype(BF16)
-            tab_ref[at, sl2] = (-(sa * cb + ca * sb)).astype(BF16)
-            return carry
-
-        lax.fori_loop(0, count, table, 0)
 
 
 def inverse_table_kernel(base_ref, hi_ref, lo_ref):
@@ -381,16 +386,6 @@
     stages = exchange_plan(n_worker, n_server)
     assert rup_w == n_server and sgt.shape[0] == PTS and slots % 16 == 0
 
-    forward = pl.pallas_call(
-        forward_table_kernel,
-        out_shape=[jax.ShapeDtypeStruct((half, half), BF16)],
-        in_specs=[vmem()],
-        out_specs=[vmem()],
-        compiler_params=params(4),
-        cost_estimate=pl.CostEstimate(flops=10**9, bytes_accessed=10**7, transcendentals=0),
-        name="forward_table",
-    )
-
     record = pl.pallas_call(
         pack_kernel,
         out_shape=jax.ShapeDtypeStruct((devices, capacity, width), BF16),
@@ -418,7 +413,7 @@
         ]
     )
     record = lax.all_to_all(record, ("server", "worker"), split_axis=0, concat_axis=0, tiled=True)
-    forwards = [in_hbm(forward(jnp.asarray(base))[0]) for base in forward_bases(n_time)]
+    base = jnp.asarray(np.stack(forward_bases(n_time)))
 
     inverse = pl.pallas_call(
         inverse_table_kernel,
@@ -449,19 +444,20 @@
     parts = pl.pallas_call(
         functools.partial(owner_kernel, stages),
         out_shape=part_shapes(0),
-        in_specs=[vmem()] + [hbm()] * 3,
+        in_specs=[vmem()] + [hbm()] * 2,
         out_specs=[vmem()] * stages[0][1],
         scratch_shapes=[
             pltpu.VMEM((slots, width), F32),
-            pltpu.VMEM((3, 2, slots, half), BF16),
+            pltpu.VMEM((2, 3 * slots, half), BF16),
             pltpu.VMEM((18, PTS, n_time), BF16),
+            pltpu.VMEM(base.shape, F32),
             pltpu.VMEM((2, half, half), BF16),
-            pltpu.SemaphoreType.DMA((5,)),
+            pltpu.SemaphoreType.DMA((4,)),
         ],
         compiler_params=params(36),
         cost_estimate=pl.CostEstimate(flops=10**10, bytes_accessed=2 * 10**7, transcendentals=0),
         name="owner",
-    )(record, in_hbm(jnp.transpose(sgt, (1, 0, 2))), *forwards)
+    )(record, in_hbm(jnp.transpose(sgt, (1, 0, 2))), in_hbm(base))
     arrived = send(parts, stages[0])
     for i in range(1, len(stages)):
         radix = stages[i][1]

time: 45.4 us -> 44.2 us (0.974)
  blocking collectives: 0 us -> 15.7 us
  starting transfers between devices: 15.8 us -> 8.48 us
  local copies, waits for them, and re-layouts: 3.59 us -> 0.01 us
  waiting for transfers between devices: 6.36 us -> 3.2 us
  Pallas kernels: 18.8 us -> 15.9 us
    all_to_all x0 -> x1, blocking collectives: none -> 15.7 us  [shards(): lax.all_to_all(record, ('server', 'worker'), split_axis=0, concat_axis=0,...]
    all_to_all x1 -> x0, starting transfers between devices: 7.3 us -> none  [shards(): lax.all_to_all(record, ('server', 'worker'), split_axis=0, concat_axis=0,...]
    unnamed x12 -> x4, local copies, waits for them, and re-layouts: 3.59 us -> 0.01 us
    all_to_all x1 -> x0, waiting for transfers between devices: 3.11 us -> none  [shards(): lax.all_to_all(record, ('server', 'worker'), split_axis=0, concat_axis=0,...]
    pallas_call x2 -> x0, Pallas kernels: 1.85 us -> none  [shards(): forward(jnp.asarray(base))[0]]
    pallas_call x1, Pallas kernels: 2.27 us -> 1.56 us  [shards(): pl.pallas_call(pack_kernel, out_shape=jax.ShapeDtypeStruct((devices, capa...]
  transfers between devices with their start and end apart: 8 -> 7, of which waited for: 7 -> 6; matrix products, arithmetic and copies ran while one was open for 0% -> 0% of each run, Pallas kernels for 10% -> 6%
where the time goes in v5:
time: 44.2 us; the launch traced here: 43.9 us
  Pallas kernels  15.9 us (36%)
  blocking collectives  15.7 us (36%)
  starting transfers between devices  8.48 us (19%)
  waiting for transfers between devices  3.2 us (7%)
  between operations  0.7 us (2%)
    all_to_all x1, blocking collectives, shards(): lax.all_to_all(record, ('server', 'worker'), split_axis=0, concat_axis=0,...  15.7 us
    pallas_call x1, Pallas kernels, shards(): pl.pallas_call(functools.partial(owner_kernel, stages), out_shape=part_sh...  8.63 us
    ppermute x7, starting transfers between devices, send(): lax.ppermute(parts[k], axis, [(i, i ^ k << shift) for i in range(size)])  8.48 us
    ppermute x7, waiting for transfers between devices, send(): lax.ppermute(parts[k], axis, [(i, i ^ k << shift) for i in range(size)])  3.2 us
    pallas_call x1, Pallas kernels, shards(): pl.pallas_call(functools.partial(final_kernel, count), out_shape=[jax.Sha...  2.8 us
    pallas_call x2, Pallas kernels, beside(): own, *made = lax.optimization_barrier((own, *kernel(base)))  2.68 us
    pallas_call x1, Pallas kernels, shards(): pl.pallas_call(pack_kernel, out_shape=jax.ShapeDtypeStruct((devices, capa...  1.56 us
  transfers between devices with their start and end apart: 7, of which 6 were waited for; matrix products, arithmetic and copies ran while one was open for 0% of the time, Pallas kernels for 6%

profile of v5, /device:TPU:0, one launch (start us, length us, event | category | flops | bytes accessed | tf_op | source)
XLA Modules:
  0.0 43.9 jit_solution(8815377740177454843)
XLA Ops:
  0.6 1.6 %pack.1 = bf16[32,4,640]{2,1,0:T(4,128)(2,1)S(1)} custom-call(s32[32,128]{1,0:T(8,128)} %bitcast.14, s32[4,24]{1,0:T(4,128)} %bitcast.16, f32[6,4,24]{2,1,0:T(4,128)} %bitcast.15, bf16[4,24,512]{2,1,0:T(8,128)(2,1)} %bitcast.13), custom_call_target="tpu_custom_call" | custom-call | tf_op jit(solution)/shard_map/pack/pallas_call | solution.py:389
  2.2 15.7 %all_to_all.5.rec_ref = bf16[32,4,640]{2,1,0:T(4,128)(2,1)S(1)} all-to-all(bf16[32,4,640]{2,1,0:T(4,128)(2,1)S(1)} %pack.1), channel_id=1, replica_groups=mesh['server'=4,'worker'=8] {'server','worker'}, dimensions={0} | all-to-all | bytes 327680 | tf_op jit(solution)/shard_map/all_to_all | solution.py:415
  17.9 0.0 copy-start.1
  17.9 8.6 %owner.1 = (f32[3,16,2048]{2,1,0:T(8,128)S(1)}, f32[3,16,2048]{2,1,0:T(8,128)S(1)}) custom-call(bf16[32,4,640]{2,1,0:T(4,128)(2,1)S(1)} %all_to_all.5.rec_ref, bf16[18,128,2048]{2,1,0:T(8,128)(2,1)} %bitcast.17, f32[2,128,512]{2,1,0:T(8,128)} %constant.6.clone.base_ref), custom_call_target="tpu_custom_call" | custom-call | flops 10000000000 | bytes 20000000 | tf_op jit(solution)/shard_map/owner/pallas_call | solution.py:444
  26.5 0.5 %collective-permute-start = (f32[3,16,2048]{2,1,0:T(8,128)S(1)}, f32[3,16,2048]{2,1,0:T(8,128)S(1)}, u32[]{:S(2)}, u32[]{:S(2)}) collective-permute-start(f32[3,16,2048]{2,1,0:T(8,128)S(1)} %get-tuple-element.31), channel_id=1, source_target_pairs={{0,1},{1,0},{2,3},{3,2},{4,5},{5,4},{6,7},{7,6},{8,9},{9,8},{10,11... | collective-permute-start | bytes 1179656 | tf_op jit(solution)/shard_map/ppermute | solution.py:361
  27.0 0.1 gain.1
  27.1 1.2 %collective-permute-done.refs_1_ = f32[3,16,2048]{2,1,0:T(8,128)S(1)} collective-permute-done((f32[3,16,2048]{2,1,0:T(8,128)S(1)}, f32[3,16,2048]{2,1,0:T(8,128)S(1)}, u32[]{:S(2)}, u32[]{:S(2)}) %collective-permute-start) | collective-permute-done | bytes 393248 | tf_op jit(solution)/shard_map/ppermute | solution.py:361
  28.4 0.0 copy-start
  28.4 1.1 %collective-permute-start.1 = (bf16[3,4,2048]{2,1,0:T(4,128)(2,1)S(1)}, bf16[3,4,2048]{2,1,0:T(4,128)(2,1)S(1)}, u32[]{:S(2)}, u32[]{:S(2)}) collective-permute-start(bf16[3,4,2048]{2,1,0:T(4,128)(2,1)S(1)} %get-tuple-element.38), channel_id=1, source_target_pairs={{0,6},{1,7},{2,4},{3,5},{4,2},{5,3},{6,0},{7,1},{8,14},{9,15},{10,... | collective-permute-start | bytes 147464 | tf_op jit(solution)/shard_map/ppermute | solution.py:361
  29.4 1.1 %collective-permute-start.2 = (bf16[3,4,2048]{2,1,0:T(4,128)(2,1)S(1)}, bf16[3,4,2048]{2,1,0:T(4,128)(2,1)S(1)}, u32[]{:S(2)}, u32[]{:S(2)}) collective-permute-start(bf16[3,4,2048]{2,1,0:T(4,128)(2,1)S(1)} %get-tuple-element.39), channel_id=1, source_target_pairs={{0,4},{1,5},{2,6},{3,7},{4,0},{5,1},{6,2},{7,3},{8,12},{9,13},{10,... | collective-permute-start | bytes 147464 | tf_op jit(solution)/shard_map/ppermute | solution.py:361
  30.5 1.4 %collective-permute-start.3 = (bf16[3,4,2048]{2,1,0:T(4,128)(2,1)S(1)}, bf16[3,4,2048]{2,1,0:T(4,128)(2,1)S(1)}, u32[]{:S(2)}, u32[]{:S(2)}) collective-permute-start(bf16[3,4,2048]{2,1,0:T(4,128)(2,1)S(1)} %get-tuple-element.40), channel_id=1, source_target_pairs={{0,2},{1,3},{2,0},{3,1},{4,6},{5,7},{6,4},{7,5},{8,10},{9,11},{10,... | collective-permute-start | bytes 147464 | tf_op jit(solution)/shard_map/ppermute | solution.py:361
  32.0 0.0 copy-done.1
  32.0 1.3 %inverse_table.2 = (bf16[1024,1024]{1,0:T(8,128)(2,1)S(1)}, bf16[1024,1024]{1,0:T(8,128)(2,1)S(1)}) custom-call(f32[96,1024]{1,0:T(8,128)S(1)} %copy-done.1), custom_call_target="tpu_custom_call" | custom-call | flops 1000000000 | bytes 10000000 | tf_op jit(solution)/shard_map/inverse_table/pallas_call | solution.py:368
  33.3 0.5 %collective-permute-done.1.refs_1_ = bf16[3,4,2048]{2,1,0:T(4,128)(2,1)S(1)} collective-permute-done((bf16[3,4,2048]{2,1,0:T(4,128)(2,1)S(1)}, bf16[3,4,2048]{2,1,0:T(4,128)(2,1)S(1)}, u32[]{:S(2)}, u32[]{:S(2)}) %collective-permute-start.1) | collective-permute-done | bytes 49184 | tf_op jit(solution)/shard_map/ppermute | solution.py:361
  33.8 0.2 collective-permute-done.2.refs_2_
  34.0 0.6 %collective-permute-done.3.refs_3_ = bf16[3,4,2048]{2,1,0:T(4,128)(2,1)S(1)} collective-permute-done((bf16[3,4,2048]{2,1,0:T(4,128)(2,1)S(1)}, bf16[3,4,2048]{2,1,0:T(4,128)(2,1)S(1)}, u32[]{:S(2)}, u32[]{:S(2)}) %collective-permute-start.3) | collective-permute-done | bytes 49184 | tf_op jit(solution)/shard_map/ppermute | solution.py:361
  34.6 1.5 %collective-permute-start.4 = (f32[3,1,2048]{2,1,0:T(1,128)S(1)}, f32[3,1,2048]{2,1,0:T(1,128)S(1)}, u32[]{:S(2)}, u32[]{:S(2)}) collective-permute-start(f32[3,1,2048]{2,1,0:T(1,128)S(1)} %get-tuple-element.47), channel_id=1, source_target_pairs={{0,24},{8,16},{16,8},{24,0},{1,25},{9,17},{17,9},{25,1},{2,26},{10... | collective-permute-start | bytes 73736 | tf_op jit(solution)/shard_map/ppermute | solution.py:361
  36.1 0.4 collective-permute-start.5
  36.5 2.5 %collective-permute-start.6 = (f32[3,1,2048]{2,1,0:T(1,128)S(1)}, f32[3,1,2048]{2,1,0:T(1,128)S(1)}, u32[]{:S(2)}, u32[]{:S(2)}) collective-permute-start(f32[3,1,2048]{2,1,0:T(1,128)S(1)} %get-tuple-element.49), channel_id=1, source_target_pairs={{0,8},{8,0},{16,24},{24,16},{1,9},{9,1},{17,25},{25,17},{2,10},{10... | collective-permute-start | bytes 73736 | tf_op jit(solution)/shard_map/ppermute | solution.py:361
  39.1 0.0 copy-done
  39.1 1.3 %inverse_table.3 = (bf16[1024,1024]{1,0:T(8,128)(2,1)S(1)}, bf16[1024,1024]{1,0:T(8,128)(2,1)S(1)}) custom-call(f32[96,1024]{1,0:T(8,128)S(1)} %copy-done), custom_call_target="tpu_custom_call" | custom-call | flops 1000000000 | bytes 10000000 | tf_op jit(solution)/shard_map/inverse_table/pallas_call | solution.py:368
  40.4 0.0 collective-permute-done.4.refs_1_
  40.4 0.4 collective-permute-done.5.refs_2_
  40.9 0.2 collective-permute-done.6.refs_3_
  41.1 2.8 %finish.1 = (f32[3,1,2048]{2,1,0:T(1,128)}, f32[3,1,44]{2,1,0:T(1,128)}) custom-call(f32[3,1,2048]{2,1,0:T(1,128)S(1)} %get-tuple-element.46.refs_0_, f32[3,1,2048]{2,1,0:T(1,128)S(1)} %collective-permute-done.4.refs_1_, f32[3,1,2048]{2,1,0:T(1,128)S(1)} %collective-permute-done.5.refs_2_, f32[3,1,2048]{2,1,0:T(1,128)S(1)} %collective-permute-done.6.refs_3_, ...), custom_call_target="tpu_custom_call" | custom-call | tf_op jit(solution)/shard_map/finish/pallas_call | solution.py:478
  (2 shorter events, 0.1 us)
Async XLA Ops:
  17.9 14.1 %copy-start.1 = (f32[96,1024]{1,0:T(8,128)S(1)}, f32[96,1024]{1,0:T(8,128)}, u32[]{:S(2)}) copy-start(f32[96,1024]{1,0:T(8,128)} %constant.7.clone.base_ref) | copy-start | bytes 1179652
  26.5 1.8 %collective-permute-start = (f32[3,16,2048]{2,1,0:T(8,128)S(1)}, f32[3,16,2048]{2,1,0:T(8,128)S(1)}, u32[]{:S(2)}, u32[]{:S(2)}) collective-permute-start(f32[3,16,2048]{2,1,0:T(8,128)S(1)} %get-tuple-element.31), channel_id=1, source_target_pairs={{0,1},{1,0},{2,3},{3,2},{4,5},{5,4},{6,7},{7,6},{8,9},{9,8},{10,11... | collective-permute-start | bytes 1179656 | tf_op jit(solution)/shard_map/ppermute | solution.py:361
  28.4 10.7 %copy-start = (f32[96,1024]{1,0:T(8,128)S(1)}, f32[96,1024]{1,0:T(8,128)}, u32[]{:S(2)}) copy-start(f32[96,1024]{1,0:T(8,128)} %constant.8.clone.base_ref) | copy-start | bytes 1179652
  28.4 5.4 %collective-permute-start.1 = (bf16[3,4,2048]{2,1,0:T(4,128)(2,1)S(1)}, bf16[3,4,2048]{2,1,0:T(4,128)(2,1)S(1)}, u32[]{:S(2)}, u32[]{:S(2)}) collective-permute-start(bf16[3,4,2048]{2,1,0:T(4,128)(2,1)S(1)} %get-tuple-element.38), channel_id=1, source_target_pairs={{0,6},{1,7},{2,4},{3,5},{4,2},{5,3},{6,0},{7,1},{8,14},{9,15},{10,... | collective-permute-start | bytes 147464 | tf_op jit(solution)/shard_map/ppermute | solution.py:361
  29.4 4.6 %collective-permute-start.2 = (bf16[3,4,2048]{2,1,0:T(4,128)(2,1)S(1)}, bf16[3,4,2048]{2,1,0:T(4,128)(2,1)S(1)}, u32[]{:S(2)}, u32[]{:S(2)}) collective-permute-start(bf16[3,4,2048]{2,1,0:T(4,128)(2,1)S(1)} %get-tuple-element.39), channel_id=1, source_target_pairs={{0,4},{1,5},{2,6},{3,7},{4,0},{5,1},{6,2},{7,3},{8,12},{9,13},{10,... | collective-permute-start | bytes 147464 | tf_op jit(solution)/shard_map/ppermute | solution.py:361
  30.5 4.1 %collective-permute-start.3 = (bf16[3,4,2048]{2,1,0:T(4,128)(2,1)S(1)}, bf16[3,4,2048]{2,1,0:T(4,128)(2,1)S(1)}, u32[]{:S(2)}, u32[]{:S(2)}) collective-permute-start(bf16[3,4,2048]{2,1,0:T(4,128)(2,1)S(1)} %get-tuple-element.40), channel_id=1, source_target_pairs={{0,2},{1,3},{2,0},{3,1},{4,6},{5,7},{6,4},{7,5},{8,10},{9,11},{10,... | collective-permute-start | bytes 147464 | tf_op jit(solution)/shard_map/ppermute | solution.py:361
  34.6 5.8 %collective-permute-start.4 = (f32[3,1,2048]{2,1,0:T(1,128)S(1)}, f32[3,1,2048]{2,1,0:T(1,128)S(1)}, u32[]{:S(2)}, u32[]{:S(2)}) collective-permute-start(f32[3,1,2048]{2,1,0:T(1,128)S(1)} %get-tuple-element.47), channel_id=1, source_target_pairs={{0,24},{8,16},{16,8},{24,0},{1,25},{9,17},{17,9},{25,1},{2,26},{10... | collective-permute-start | bytes 73736 | tf_op jit(solution)/shard_map/ppermute | solution.py:361
  36.1 4.8 %collective-permute-start.5 = (f32[3,1,2048]{2,1,0:T(1,128)S(1)}, f32[3,1,2048]{2,1,0:T(1,128)S(1)}, u32[]{:S(2)}, u32[]{:S(2)}) collective-permute-start(f32[3,1,2048]{2,1,0:T(1,128)S(1)} %get-tuple-element.48), channel_id=1, source_target_pairs={{0,16},{8,24},{16,0},{24,8},{1,17},{9,25},{17,1},{25,9},{2,18},{10... | collective-permute-start | bytes 73736 | tf_op jit(solution)/shard_map/ppermute | solution.py:361
  36.5 4.6 %collective-permute-start.6 = (f32[3,1,2048]{2,1,0:T(1,128)S(1)}, f32[3,1,2048]{2,1,0:T(1,128)S(1)}, u32[]{:S(2)}, u32[]{:S(2)}) collective-permute-start(f32[3,1,2048]{2,1,0:T(1,128)S(1)} %get-tuple-element.49), channel_id=1, source_target_pairs={{0,8},{8,0},{16,24},{24,16},{1,9},{9,1},{17,25},{25,17},{2,10},{10... | collective-permute-start | bytes 73736 | tf_op jit(solution)/shard_map/ppermute | solution.py:361

commit v6 on v5

--- a/solution.py
+++ b/solution.py
@@ -14,7 +14,7 @@
 ROWS = 48
 STEP = 32
 PTS = 128
-DFT_WIDE = 512
+RESIDUES = (0, 2, 1, 3)
 ROW_LANE = 64
 RUP_LANE = 96
 F32 = jnp.float32
@@ -42,31 +42,26 @@
     return (2.0 * math.pi / n_time) * (product % n_time)
 
 
-def forward_bases(n_time):
-    half = n_time // 2
-    quarter = half // 2
-    bases = []
-    for odd in range(2):
-        freq = 2 * np.arange(quarter) + odd
-        coarse = angle(np.arange(half // STEP)[:, None] * STEP * freq[None, :], n_time)
-        fine = angle(np.arange(STEP)[:, None] * freq[None, :], n_time)
-        bases.append(
-            np.concatenate([f(x) for x in (coarse, fine) for f in (np.cos, np.sin)]).astype(np.float32)
-        )
-    return bases
+def cos_sin(*angles):
+    return np.concatenate([f(x) for x in angles for f in (np.cos, np.sin)]).astype(np.float32)
+
+
+def forward_base(n_time):
+    index = np.arange(n_time // 8)
+    freq = np.concatenate([4 * index + residue for residue in RESIDUES])
+    coarse = angle(np.arange(n_time // 4 // STEP)[:, None] * STEP * freq[None, :], n_time)
+    fine = angle(np.arange(STEP)[:, None] * freq[None, :], n_time)
+    return cos_sin(coarse, fine)
 
 
 def inverse_bases(n_time):
-    half = n_time // 2
-    quarter = half // 2
-    time = np.arange(half)
-    coarse = angle(np.arange(quarter // STEP)[:, None] * 2 * STEP * time[None, :], n_time)
-    even = angle(np.arange(STEP)[:, None] * 2 * time[None, :], n_time)
-    odd = angle((np.arange(STEP)[:, None] * 2 + 1) * time[None, :], n_time)
-    return [
-        np.concatenate([f(x) for x in (coarse, fine) for f in (np.cos, np.sin)]).astype(np.float32)
-        for fine in (even, odd)
+    time = np.arange(n_time // 4)
+    coarse = angle(np.arange(n_time // 8 // STEP)[:, None] * 4 * STEP * time[None, :], n_time)
+    fine = [
+        angle((np.arange(STEP)[:, None] * 4 + residue) * time[None, :], n_time)
+        for residue in RESIDUES
     ]
+    return [cos_sin(coarse, *fine[:2]), cos_sin(coarse, *fine[2:])]
 
 
 def ordered(stages, apart):
@@ -131,39 +126,37 @@
         out_ref[d] = scr[d * capacity : (d + 1) * capacity, :].astype(BF16)
 
 
-def forward_table(base_ref, tab_ref):
-    half, width = tab_ref.shape
-    quarter = width // 2
-    count = half // STEP
-    wide = 256
-    for lc in range(quarter // wide):
-        sl = slice(lc * wide, (lc + 1) * wide)
-        sl2 = slice(quarter + lc * wide, quarter + (lc + 1) * wide)
-        cb = base_ref[2 * count : 2 * count + STEP, sl]
-        sb = base_ref[2 * count + STEP :, sl]
-
-        def table(a, carry):
-            ca = base_ref[pl.ds(a, 1), sl]
-            sa = base_ref[pl.ds(count + a, 1), sl]
-            at = pl.ds(pl.multiple_of(a * STEP, STEP), STEP)
-            tab_ref[at, sl] = (ca * cb - sa * sb).astype(BF16)
-            tab_ref[at, sl2] = (-(sa * cb + ca * sb)).astype(BF16)
-            return carry
-
-        lax.fori_loop(0, count, table, 0, unroll=4)
+def forward_table(base_ref, tab_ref, block):
+    count = tab_ref.shape[0] // STEP
+    wide = tab_ref.shape[1] // 8
+    sl = slice(block * wide, (block + 1) * wide)
+    cols = slice(2 * block * wide, (2 * block + 1) * wide)
+    cols_im = slice((2 * block + 1) * wide, (2 * block + 2) * wide)
+    cb = base_ref[2 * count : 2 * count + STEP, sl]
+    sb = base_ref[2 * count + STEP :, sl]
+
+    def table(a, carry):
+        ca = base_ref[pl.ds(a, 1), sl]
+        sa = base_ref[pl.ds(count + a, 1), sl]
+        at = pl.ds(pl.multiple_of(a * STEP, STEP), STEP)
+        tab_ref[at, cols] = (ca * cb - sa * sb).astype(BF16)
+        tab_ref[at, cols_im] = (-(sa * cb + ca * sb)).astype(BF16)
+        return carry
+
+    lax.fori_loop(0, count, table, 0, unroll=4)
 
 
 def owner_kernel(stages, rec_ref, sgt_ref, base_ref, *refs):
     first = stages[0][1]
     out_refs = refs[:first]
-    rec_s, x_s, sgt_s, base_s, tab_s, sems = refs[first:]
+    rec_s, x_s, p_s, slip_s, sgt_s, base_s, tab_s, sems = refs[first:]
     devices, capacity, width = rec_ref.shape
     slots = devices * capacity
     n_time = sgt_ref.shape[2]
     half = n_time // 2
-    quarter = half // 2
+    wide = n_time // 4
+    block_wide = n_time // 8
     n_slip = width - 128
-    wide = 512
     base_copy = pltpu.make_async_copy(base_ref, base_s, sems.at[3])
     base_copy.start()
     copies = []
@@ -187,19 +180,12 @@
         axis=0,
     )
     base_copy.wait()
-    for c in range(3):
-        if c < 2:
-            forward_table(base_s.at[c], tab_s.at[c])
-        copies[c].wait()
-        for at in range(0, half, wide):
-            ends = []
-            for start in (at, half + at):
-                rows = sgt_s[6 * c : 6 * c + 6, :, start : start + wide].reshape(6 * PTS, wide)
-                out = nn(left, rows)
-                ends.append(out[:slots] + out[slots:])
-            x_s[0, c * slots : (c + 1) * slots, at : at + wide] = (ends[0] + ends[1]).astype(BF16)
-            x_s[1, c * slots : (c + 1) * slots, at : at + wide] = (ends[0] - ends[1]).astype(BF16)
-
+    for block in range(4):
+        forward_table(base_s, tab_s, block)
+    slip = rec_s[:, :n_slip].astype(BF16)
+    for block in range(4):
+        cols = slice(2 * block * block_wide, 2 * (block + 1) * block_wide)
+        slip_s[:, cols] = nn(slip, tab_s[:, cols])
     ruptures = math.prod(radix for _, radix, _, _ in stages)
     shape = (ruptures, slots)
     rup = nt((iota((8, 128), 1) == RUP_LANE).astype(F32).astype(BF16), tail.astype(BF16))[:1].astype(jnp.int32)
@@ -208,28 +194,51 @@
     where_to = ordered(stages, apart)
     seg = (iota(shape, 0) == where_to).astype(F32).astype(BF16)
     seg = jnp.concatenate([seg, seg], axis=1)
-    slip = rec_s[:, :n_slip].astype(BF16)
     part = ruptures // first
-    for q in range(2):
-        for at in range(0, quarter, DFT_WIDE):
-            cols = slice(at, at + DFT_WIDE)
-            cols_im = slice(quarter + at, quarter + at + DFT_WIDE)
-            slip_re = nn(slip, tab_s[q, :n_slip, cols])
-            slip_im = nn(slip, tab_s[q, :n_slip, cols_im])
-            all_re = nn(x_s[q], tab_s[q, :, cols])
-            all_im = nn(x_s[q], tab_s[q, :, cols_im])
-            for c in range(3):
-                t_re = all_re[c * slots : (c + 1) * slots]
-                t_im = all_im[c * slots : (c + 1) * slots]
-                for base, prod in (
-                    (0, slip_re * t_re - slip_im * t_im),
-                    (half, slip_re * t_im + slip_im * t_re),
-                ):
-                    start = base + q * quarter + at
-                    total = nn(seg, jnp.concatenate(hilo(prod), axis=0))
-                    for k in range(first):
-                        ref = out_refs[k]
-                        ref[c, :, start : start + DFT_WIDE] = total[k * part : (k + 1) * part].astype(ref.dtype)
+    for c in range(3):
+        copies[c].wait()
+        x = []
+        for k in range(4):
+            rows = sgt_s[6 * c : 6 * c + 6, :, k * wide : (k + 1) * wide].reshape(6 * PTS, wide)
+            out = nn(left, rows)
+            x.append(out[:slots] + out[slots:])
+        plus = (x[0] + x[2], x[1] + x[3])
+        x_s[c, :slots, :] = (plus[0] + plus[1]).astype(BF16)
+        x_s[c, slots : 2 * slots, :] = (plus[0] - plus[1]).astype(BF16)
+        x_s[c, 2 * slots : 3 * slots, :] = (x[0] - x[2]).astype(BF16)
+        x_s[c, 3 * slots :, :] = (x[1] - x[3]).astype(BF16)
+        for block in range(4):
+            first_row, last_row = ((0, 1), (1, 2), (2, 4), (2, 4))[block]
+            middle = (2 * block + 1) * block_wide
+            cols = slice(middle - block_wide, middle)
+            cols_im = slice(middle, middle + block_wide)
+            product = nn(
+                x_s[c, first_row * slots : last_row * slots, :],
+                tab_s[:, middle - block_wide : middle + block_wide],
+            )
+            t_re = product[:slots, :block_wide]
+            t_im = product[:slots, block_wide:]
+            if block == 2:
+                t_re, t_im = t_re + product[slots:, block_wide:], t_im - product[slots:, :block_wide]
+            elif block == 3:
+                t_re, t_im = t_re - product[slots:, block_wide:], t_im + product[slots:, :block_wide]
+            slip_re = slip_s[:, cols]
+            slip_im = slip_s[:, cols_im]
+            hi, lo = hilo(slip_re * t_re - slip_im * t_im)
+            p_s[:slots, cols] = hi
+            p_s[slots:, cols] = lo
+            hi, lo = hilo(slip_re * t_im + slip_im * t_re)
+            p_s[:slots, cols_im] = hi
+            p_s[slots:, cols_im] = lo
+        total = nn(seg, p_s[...])
+        for block in range(4):
+            for k in range(first):
+                ref = out_refs[k]
+                for p in range(2):
+                    at = slice(p * half + block * block_wide, p * half + (block + 1) * block_wide)
+                    ref[c, :, at] = total[
+                        k * part : (k + 1) * part, (2 * block + p) * block_wide : (2 * block + p + 1) * block_wide
+                    ].astype(ref.dtype)
 
 
 def sum_kernel(radix, *refs):
@@ -245,38 +254,40 @@
 
 
 def inverse_table_kernel(base_ref, hi_ref, lo_ref):
-    half = hi_ref.shape[0]
-    quarter = half // 2
-    count = quarter // STEP
+    block_wide = hi_ref.shape[0] // 4
+    count = block_wide // STEP
     wide = 256
-    for lc in range(half // wide):
-        sl = slice(lc * wide, (lc + 1) * wide)
-        cf = base_ref[2 * count : 2 * count + STEP, sl]
-        sf = base_ref[2 * count + STEP :, sl]
-
-        def table(a, carry):
-            ca = base_ref[pl.ds(a, 1), sl]
-            sa = base_ref[pl.ds(count + a, 1), sl]
-            for base, value in ((0, ca * cf - sa * sf), (quarter, -(sa * cf + ca * sf))):
-                at = pl.ds(pl.multiple_of(base + a * STEP, STEP), STEP)
-                hi, lo = hilo(value)
-                hi_ref[at, sl] = hi
-                lo_ref[at, sl] = lo
-            return carry
-
-        lax.fori_loop(0, count, table, 0)
+    for p in range(2):
+        fine = 2 * count + 2 * p * STEP
+        for lc in range(hi_ref.shape[1] // wide):
+            sl = slice(lc * wide, (lc + 1) * wide)
+            cf = base_ref[fine : fine + STEP, sl]
+            sf = base_ref[fine + STEP : fine + 2 * STEP, sl]
+
+            def table(a, carry):
+                ca = base_ref[pl.ds(a, 1), sl]
+                sa = base_ref[pl.ds(count + a, 1), sl]
+                for base, value in ((0, ca * cf - sa * sf), (block_wide, -(sa * cf + ca * sf))):
+                    at = pl.ds(pl.multiple_of(2 * p * block_wide + base + a * STEP, STEP), STEP)
+                    hi, lo = hilo(value)
+                    hi_ref[at, sl] = hi
+                    lo_ref[at, sl] = lo
+                return carry
+
+            lax.fori_loop(0, count, table, 0)
 
 
 def gain_kernel(gr_ref, gi_ref):
     half = gr_ref.shape[1]
-    quarter = half // 2
+    block_wide = half // 4
     n_time = 2 * half
     shape = gr_ref.shape
     low = math.log(4.0 / n_time)
     high = math.log(0.25)
     period = iota(shape, 0)
     slot = iota(shape, 1)
-    freq = jnp.where(slot < quarter, 2 * slot, 2 * (slot - quarter) + 1)
+    block = slot // block_wide
+    freq = 4 * (slot % block_wide) + jnp.where(block < 2, 2 * block, 2 * block - 3)
     omega_freq = freq.astype(F32) * (2.0 * math.pi / n_time)
     omega_osc = 2.0 * math.pi * jnp.exp(low + (high - low) * period.astype(F32) / (PERIODS - 1))
     den_real = omega_osc * omega_osc - omega_freq * omega_freq
@@ -291,7 +302,8 @@
     spec_refs = refs[:count]
     *tables, gr_ref, gi_ref, seis_ref, peak_ref = refs[count:]
     half = gr_ref.shape[1]
-    quarter = half // 2
+    block_wide = half // 4
+    wide = half // 2
     spec = []
     for c in range(3):
         total = spec_refs[0][c]
@@ -300,27 +312,50 @@
         spec.append(total)
     gr = gr_ref[...]
     gi = gi_ref[...]
-    sums = []
-    for q in range(2):
-        cols = slice(q * quarter, (q + 1) * quarter)
-        cols_im = slice(half + q * quarter, half + (q + 1) * quarter)
-        lefts = []
-        for c in range(3):
-            re = spec[c][:, cols]
-            im = spec[c][:, cols_im]
-            g_re = gr[:, cols]
-            g_im = gi[:, cols]
-            lefts.append(jnp.concatenate([re * g_re + im * g_im, im * g_re - re * g_im], axis=1))
-        hi, lo = hilo(jnp.concatenate(lefts, axis=0))
-        hi_ref, lo_ref = tables[2 * q : 2 * q + 2]
-        first = nn(jnp.concatenate([hi, lo], axis=0), hi_ref[...])
-        sums.append(first[: 3 * ROWS] + first[3 * ROWS :] + nn(hi, lo_ref[...]))
-    even, odd = sums
-    peak = jnp.max(jnp.abs(even) + jnp.abs(odd), axis=1, keepdims=True)
+
+    def accel(block):
+        cols = slice(block * block_wide, (block + 1) * block_wide)
+        cols_im = slice(half + block * block_wide, half + (block + 1) * block_wide)
+        g_re = gr[:, cols]
+        g_im = gi[:, cols]
+        re = jnp.concatenate([s[:, cols] * g_re + s[:, cols_im] * g_im for s in spec], axis=0)
+        im = jnp.concatenate([s[:, cols_im] * g_re - s[:, cols] * g_im for s in spec], axis=0)
+        return re, im
+
+    def product(left, hi_tab, lo_tab):
+        count = left.shape[0]
+        hi, lo = hilo(left)
+        both = nn(jnp.concatenate([hi, lo], axis=0), hi_tab)
+        return both[:count] + both[count:] + nn(hi, lo_tab)
+
+    even_hi, even_lo, odd_hi, odd_lo = tables
+    pair = [
+        product(
+            jnp.concatenate(accel(block), axis=1),
+            even_hi[block * wide : (block + 1) * wide, :],
+            even_lo[block * wide : (block + 1) * wide, :],
+        )
+        for block in range(2)
+    ]
+    re_c, im_c = accel(2)
+    re_d, im_d = accel(3)
+    straight = jnp.concatenate([re_c, im_c, re_d, im_d], axis=1)
+    turned = jnp.concatenate([-im_c, re_c, im_d, -re_d], axis=1)
+    odd = product(jnp.concatenate([straight, turned], axis=0), odd_hi[...], odd_lo[...])
+    evens = (pair[0] + pair[1], pair[0] - pair[1])
+    odds = (odd[: 3 * ROWS], odd[3 * ROWS :])
+    peak = jnp.max(
+        jnp.maximum(jnp.abs(evens[0]) + jnp.abs(odds[0]), jnp.abs(evens[1]) + jnp.abs(odds[1])),
+        axis=1,
+        keepdims=True,
+    )
     for c in range(3):
         row = c * ROWS + PERIODS
-        seis_ref[c, :, :half] = even[row : row + 1] + odd[row : row + 1]
-        seis_ref[c, :, half:] = even[row : row + 1] - odd[row : row + 1]
+        for k in range(2):
+            e = evens[k][row : row + 1]
+            o = odds[k][row : row + 1]
+            seis_ref[c, :, k * wide : (k + 1) * wide] = e + o
+            seis_ref[c, :, half + k * wide : half + (k + 1) * wide] = e - o
         column = jnp.broadcast_to(peak[c * ROWS : (c + 1) * ROWS], (ROWS, 128))
         column = jnp.concatenate([column, jnp.zeros((128 - ROWS, 128), F32)], axis=0)
         peak_ref[c] = column.T[:1, :PERIODS]
@@ -384,7 +419,7 @@
     slots = devices * capacity
     width = n_slip + 128
     stages = exchange_plan(n_worker, n_server)
-    assert rup_w == n_server and sgt.shape[0] == PTS and slots % 16 == 0
+    assert rup_w == n_server and sgt.shape[0] == PTS and slots % 16 == 0 and 4 * n_slip == n_time
 
     record = pl.pallas_call(
         pack_kernel,
@@ -413,11 +448,11 @@
         ]
     )
     record = lax.all_to_all(record, ("server", "worker"), split_axis=0, concat_axis=0, tiled=True)
-    base = jnp.asarray(np.stack(forward_bases(n_time)))
+    base = jnp.asarray(forward_base(n_time))
 
     inverse = pl.pallas_call(
         inverse_table_kernel,
-        out_shape=[jax.ShapeDtypeStruct((half, half), BF16)] * 2,
+        out_shape=[jax.ShapeDtypeStruct((half, half // 2), BF16)] * 2,
         in_specs=[vmem()],
         out_specs=[vmem()] * 2,
         compiler_params=params(8),
@@ -448,10 +483,12 @@
         out_specs=[vmem()] * stages[0][1],
         scratch_shapes=[
             pltpu.VMEM((slots, width), F32),
-            pltpu.VMEM((2, 3 * slots, half), BF16),
+            pltpu.VMEM((3, 4 * slots, n_slip), BF16),
+            pltpu.VMEM((2 * slots, n_time), BF16),
+            pltpu.VMEM((slots, n_time), F32),
             pltpu.VMEM((18, PTS, n_time), BF16),
             pltpu.VMEM(base.shape, F32),
-            pltpu.VMEM((2, half, half), BF16),
+            pltpu.VMEM((half // 2, n_time), BF16),
             pltpu.SemaphoreType.DMA((4,)),
         ],
         compiler_params=params(36),

time: 44.2 us -> 42.6 us (0.964)
  Pallas kernels: 15.9 us -> 13 us
  waiting for transfers between devices: 3.2 us -> 4.53 us
    pallas_call x2, Pallas kernels: 2.68 us -> 1.34 us  [beside(): own, *made = lax.optimization_barrier((own, *kernel(base)))]
    ppermute x7, waiting for transfers between devices: 3.2 us -> 4.53 us  [send(): lax.ppermute(parts[k], axis, [(i, i ^ k << shift) for i in range(size)])]
    pallas_call x1, Pallas kernels: 8.63 us -> 7.65 us  [shards(): pl.pallas_call(functools.partial(owner_kernel, stages), out_shape=part_sh...]
    pallas_call x1, Pallas kernels: 2.8 us -> 2.27 us  [shards(): pl.pallas_call(functools.partial(final_kernel, count), out_shape=[jax.Sha...]
  transfers between devices with their start and end apart: 7 -> 7, of which waited for: 6 -> 7; matrix products, arithmetic and copies ran while one was open for 0% -> 0% of each run, Pallas kernels for 6% -> 3%
where the time goes in v6:
time: 42.6 us; the launch traced here: 42.4 us
  blocking collectives  15.7 us (37%)
  Pallas kernels  13 us (31%)
  starting transfers between devices  8.46 us (20%)
  waiting for transfers between devices  4.53 us (11%)
  between operations  0.68 us (2%)
    all_to_all x1, blocking collectives, shards(): lax.all_to_all(record, ('server', 'worker'), split_axis=0, concat_axis=0,...  15.7 us
    ppermute x7, starting transfers between devices, send(): lax.ppermute(parts[k], axis, [(i, i ^ k << shift) for i in range(size)])  8.46 us
    pallas_call x1, Pallas kernels, shards(): pl.pallas_call(functools.partial(owner_kernel, stages), out_shape=part_sh...  7.65 us
    ppermute x7, waiting for transfers between devices, send(): lax.ppermute(parts[k], axis, [(i, i ^ k << shift) for i in range(size)])  4.53 us
    pallas_call x1, Pallas kernels, shards(): pl.pallas_call(functools.partial(final_kernel, count), out_shape=[jax.Sha...  2.27 us
    pallas_call x1, Pallas kernels, shards(): pl.pallas_call(pack_kernel, out_shape=jax.ShapeDtypeStruct((devices, capa...  1.56 us
    pallas_call x2, Pallas kernels, beside(): own, *made = lax.optimization_barrier((own, *kernel(base)))  1.34 us
  transfers between devices with their start and end apart: 7, of which 7 were waited for; matrix products, arithmetic and copies ran while one was open for 0% of the time, Pallas kernels for 3%

profile of v6, /device:TPU:0, one launch (start us, length us, event | category | flops | bytes accessed | tf_op | source)
XLA Modules:
  0.0 42.4 jit_solution(12554323251056112747)
XLA Ops:
  0.6 1.6 %pack.1 = bf16[32,4,640]{2,1,0:T(4,128)(2,1)S(1)} custom-call(s32[32,128]{1,0:T(8,128)} %bitcast.14, s32[4,24]{1,0:T(4,128)} %bitcast.16, f32[6,4,24]{2,1,0:T(4,128)} %bitcast.15, bf16[4,24,512]{2,1,0:T(8,128)(2,1)} %bitcast.13), custom_call_target="tpu_custom_call" | custom-call | tf_op jit(solution)/shard_map/pack/pallas_call | solution.py:424
  2.2 15.7 %all_to_all.5.rec_ref = bf16[32,4,640]{2,1,0:T(4,128)(2,1)S(1)} all-to-all(bf16[32,4,640]{2,1,0:T(4,128)(2,1)S(1)} %pack.1), channel_id=1, replica_groups=mesh['server'=4,'worker'=8] {'server','worker'}, dimensions={0} | all-to-all | bytes 327680 | tf_op jit(solution)/shard_map/all_to_all | solution.py:450
  17.9 0.0 copy-start.1
  17.9 0.0 copy-start
  17.9 7.7 %owner.1 = (f32[3,16,2048]{2,1,0:T(8,128)S(1)}, f32[3,16,2048]{2,1,0:T(8,128)S(1)}) custom-call(bf16[32,4,640]{2,1,0:T(4,128)(2,1)S(1)} %all_to_all.5.rec_ref, bf16[18,128,2048]{2,1,0:T(8,128)(2,1)} %bitcast.17, f32[96,1024]{1,0:T(8,128)} %constant.6.clone.base_ref), custom_call_target="tpu_custom_call" | custom-call | flops 10000000000 | bytes 20000000 | tf_op jit(solution)/shard_map/owner/pallas_call | solution.py:479
  25.5 0.4 %collective-permute-start = (f32[3,16,2048]{2,1,0:T(8,128)S(1)}, f32[3,16,2048]{2,1,0:T(8,128)S(1)}, u32[]{:S(2)}, u32[]{:S(2)}) collective-permute-start(f32[3,16,2048]{2,1,0:T(8,128)S(1)} %get-tuple-element.31), channel_id=1, source_target_pairs={{0,1},{1,0},{2,3},{3,2},{4,5},{5,4},{6,7},{7,6},{8,9},{9,8},{10,11... | collective-permute-start | bytes 1179656 | tf_op jit(solution)/shard_map/ppermute | solution.py:396
  26.0 0.1 gain.1
  26.1 1.2 %collective-permute-done.refs_1_ = f32[3,16,2048]{2,1,0:T(8,128)S(1)} collective-permute-done((f32[3,16,2048]{2,1,0:T(8,128)S(1)}, f32[3,16,2048]{2,1,0:T(8,128)S(1)}, u32[]{:S(2)}, u32[]{:S(2)}) %collective-permute-start) | collective-permute-done | bytes 393248 | tf_op jit(solution)/shard_map/ppermute | solution.py:396
  27.4 1.1 %collective-permute-start.1 = (bf16[3,4,2048]{2,1,0:T(4,128)(2,1)S(1)}, bf16[3,4,2048]{2,1,0:T(4,128)(2,1)S(1)}, u32[]{:S(2)}, u32[]{:S(2)}) collective-permute-start(bf16[3,4,2048]{2,1,0:T(4,128)(2,1)S(1)} %get-tuple-element.38), channel_id=1, source_target_pairs={{0,6},{1,7},{2,4},{3,5},{4,2},{5,3},{6,0},{7,1},{8,14},{9,15},{10,... | collective-permute-start | bytes 147464 | tf_op jit(solution)/shard_map/ppermute | solution.py:396
  28.4 1.1 %collective-permute-start.2 = (bf16[3,4,2048]{2,1,0:T(4,128)(2,1)S(1)}, bf16[3,4,2048]{2,1,0:T(4,128)(2,1)S(1)}, u32[]{:S(2)}, u32[]{:S(2)}) collective-permute-start(bf16[3,4,2048]{2,1,0:T(4,128)(2,1)S(1)} %get-tuple-element.39), channel_id=1, source_target_pairs={{0,4},{1,5},{2,6},{3,7},{4,0},{5,1},{6,2},{7,3},{8,12},{9,13},{10,... | collective-permute-start | bytes 147464 | tf_op jit(solution)/shard_map/ppermute | solution.py:396
  29.5 1.5 %collective-permute-start.3 = (bf16[3,4,2048]{2,1,0:T(4,128)(2,1)S(1)}, bf16[3,4,2048]{2,1,0:T(4,128)(2,1)S(1)}, u32[]{:S(2)}, u32[]{:S(2)}) collective-permute-start(bf16[3,4,2048]{2,1,0:T(4,128)(2,1)S(1)} %get-tuple-element.40), channel_id=1, source_target_pairs={{0,2},{1,3},{2,0},{3,1},{4,6},{5,7},{6,4},{7,5},{8,10},{9,11},{10,... | collective-permute-start | bytes 147464 | tf_op jit(solution)/shard_map/ppermute | solution.py:396
  31.0 0.0 copy-done.1
  31.0 0.7 %inverse_table.2 = (bf16[1024,512]{1,0:T(8,128)(2,1)S(1)}, bf16[1024,512]{1,0:T(8,128)(2,1)S(1)}) custom-call(f32[144,512]{1,0:T(8,128)S(1)} %copy-done.1), custom_call_target="tpu_custom_call" | custom-call | flops 1000000000 | bytes 10000000 | tf_op jit(solution)/shard_map/inverse_table/pallas_call | solution.py:403
  31.6 1.2 %collective-permute-done.1.refs_1_ = bf16[3,4,2048]{2,1,0:T(4,128)(2,1)S(1)} collective-permute-done((bf16[3,4,2048]{2,1,0:T(4,128)(2,1)S(1)}, bf16[3,4,2048]{2,1,0:T(4,128)(2,1)S(1)}, u32[]{:S(2)}, u32[]{:S(2)}) %collective-permute-start.1) | collective-permute-done | bytes 49184 | tf_op jit(solution)/shard_map/ppermute | solution.py:396
  32.8 0.2 collective-permute-done.2.refs_2_
  33.0 0.6 %collective-permute-done.3.refs_3_ = bf16[3,4,2048]{2,1,0:T(4,128)(2,1)S(1)} collective-permute-done((bf16[3,4,2048]{2,1,0:T(4,128)(2,1)S(1)}, bf16[3,4,2048]{2,1,0:T(4,128)(2,1)S(1)}, u32[]{:S(2)}, u32[]{:S(2)}) %collective-permute-start.3) | collective-permute-done | bytes 49184 | tf_op jit(solution)/shard_map/ppermute | solution.py:396
  33.6 1.5 %collective-permute-start.4 = (f32[3,1,2048]{2,1,0:T(1,128)S(1)}, f32[3,1,2048]{2,1,0:T(1,128)S(1)}, u32[]{:S(2)}, u32[]{:S(2)}) collective-permute-start(f32[3,1,2048]{2,1,0:T(1,128)S(1)} %get-tuple-element.47), channel_id=1, source_target_pairs={{0,24},{8,16},{16,8},{24,0},{1,25},{9,17},{17,9},{25,1},{2,26},{10... | collective-permute-start | bytes 73736 | tf_op jit(solution)/shard_map/ppermute | solution.py:396
  35.1 0.4 %collective-permute-start.5 = (f32[3,1,2048]{2,1,0:T(1,128)S(1)}, f32[3,1,2048]{2,1,0:T(1,128)S(1)}, u32[]{:S(2)}, u32[]{:S(2)}) collective-permute-start(f32[3,1,2048]{2,1,0:T(1,128)S(1)} %get-tuple-element.48), channel_id=1, source_target_pairs={{0,16},{8,24},{16,0},{24,8},{1,17},{9,25},{17,1},{25,9},{2,18},{10... | collective-permute-start | bytes 73736 | tf_op jit(solution)/shard_map/ppermute | solution.py:396
  35.5 2.5 %collective-permute-start.6 = (f32[3,1,2048]{2,1,0:T(1,128)S(1)}, f32[3,1,2048]{2,1,0:T(1,128)S(1)}, u32[]{:S(2)}, u32[]{:S(2)}) collective-permute-start(f32[3,1,2048]{2,1,0:T(1,128)S(1)} %get-tuple-element.49), channel_id=1, source_target_pairs={{0,8},{8,0},{16,24},{24,16},{1,9},{9,1},{17,25},{25,17},{2,10},{10... | collective-permute-start | bytes 73736 | tf_op jit(solution)/shard_map/ppermute | solution.py:396
  38.1 0.0 copy-done
  38.1 0.7 %inverse_table.3 = (bf16[1024,512]{1,0:T(8,128)(2,1)S(1)}, bf16[1024,512]{1,0:T(8,128)(2,1)S(1)}) custom-call(f32[144,512]{1,0:T(8,128)S(1)} %copy-done), custom_call_target="tpu_custom_call" | custom-call | flops 1000000000 | bytes 10000000 | tf_op jit(solution)/shard_map/inverse_table/pallas_call | solution.py:403
  38.8 0.6 %collective-permute-done.4.refs_1_ = f32[3,1,2048]{2,1,0:T(1,128)S(1)} collective-permute-done((f32[3,1,2048]{2,1,0:T(1,128)S(1)}, f32[3,1,2048]{2,1,0:T(1,128)S(1)}, u32[]{:S(2)}, u32[]{:S(2)}) %collective-permute-start.4) | collective-permute-done | bytes 24608 | tf_op jit(solution)/shard_map/ppermute | solution.py:396
  39.3 0.5 %collective-permute-done.5.refs_2_ = f32[3,1,2048]{2,1,0:T(1,128)S(1)} collective-permute-done((f32[3,1,2048]{2,1,0:T(1,128)S(1)}, f32[3,1,2048]{2,1,0:T(1,128)S(1)}, u32[]{:S(2)}, u32[]{:S(2)}) %collective-permute-start.5) | collective-permute-done | bytes 24608 | tf_op jit(solution)/shard_map/ppermute | solution.py:396
  39.9 0.2 collective-permute-done.6.refs_3_
  40.1 2.3 %finish.1 = (f32[3,1,2048]{2,1,0:T(1,128)}, f32[3,1,44]{2,1,0:T(1,128)}) custom-call(f32[3,1,2048]{2,1,0:T(1,128)S(1)} %get-tuple-element.46.refs_0_, f32[3,1,2048]{2,1,0:T(1,128)S(1)} %collective-permute-done.4.refs_1_, f32[3,1,2048]{2,1,0:T(1,128)S(1)} %collective-permute-done.5.refs_2_, f32[3,1,2048]{2,1,0:T(1,128)S(1)} %collective-permute-done.6.refs_3_, ...), custom_call_target="tpu_custom_call" | custom-call | tf_op jit(solution)/shard_map/finish/pallas_call | solution.py:515
  (2 shorter events, 0.1 us)
Async XLA Ops:
  17.9 13.1 %copy-start.1 = (f32[144,512]{1,0:T(8,128)S(1)}, f32[144,512]{1,0:T(8,128)}, u32[]{:S(2)}) copy-start(f32[144,512]{1,0:T(8,128)} %constant.7.clone.base_ref) | copy-start | bytes 884740
  17.9 20.2 %copy-start = (f32[144,512]{1,0:T(8,128)S(1)}, f32[144,512]{1,0:T(8,128)}, u32[]{:S(2)}) copy-start(f32[144,512]{1,0:T(8,128)} %constant.8.clone.base_ref) | copy-start | bytes 884740
  25.5 1.8 %collective-permute-start = (f32[3,16,2048]{2,1,0:T(8,128)S(1)}, f32[3,16,2048]{2,1,0:T(8,128)S(1)}, u32[]{:S(2)}, u32[]{:S(2)}) collective-permute-start(f32[3,16,2048]{2,1,0:T(8,128)S(1)} %get-tuple-element.31), channel_id=1, source_target_pairs={{0,1},{1,0},{2,3},{3,2},{4,5},{5,4},{6,7},{7,6},{8,9},{9,8},{10,11... | collective-permute-start | bytes 1179656 | tf_op jit(solution)/shard_map/ppermute | solution.py:396
  27.4 5.4 %collective-permute-start.1 = (bf16[3,4,2048]{2,1,0:T(4,128)(2,1)S(1)}, bf16[3,4,2048]{2,1,0:T(4,128)(2,1)S(1)}, u32[]{:S(2)}, u32[]{:S(2)}) collective-permute-start(bf16[3,4,2048]{2,1,0:T(4,128)(2,1)S(1)} %get-tuple-element.38), channel_id=1, source_target_pairs={{0,6},{1,7},{2,4},{3,5},{4,2},{5,3},{6,0},{7,1},{8,14},{9,15},{10,... | collective-permute-start | bytes 147464 | tf_op jit(solution)/shard_map/ppermute | solution.py:396
  28.4 4.6 %collective-permute-start.2 = (bf16[3,4,2048]{2,1,0:T(4,128)(2,1)S(1)}, bf16[3,4,2048]{2,1,0:T(4,128)(2,1)S(1)}, u32[]{:S(2)}, u32[]{:S(2)}) collective-permute-start(bf16[3,4,2048]{2,1,0:T(4,128)(2,1)S(1)} %get-tuple-element.39), channel_id=1, source_target_pairs={{0,4},{1,5},{2,6},{3,7},{4,0},{5,1},{6,2},{7,3},{8,12},{9,13},{10,... | collective-permute-start | bytes 147464 | tf_op jit(solution)/shard_map/ppermute | solution.py:396
  29.5 4.1 %collective-permute-start.3 = (bf16[3,4,2048]{2,1,0:T(4,128)(2,1)S(1)}, bf16[3,4,2048]{2,1,0:T(4,128)(2,1)S(1)}, u32[]{:S(2)}, u32[]{:S(2)}) collective-permute-start(bf16[3,4,2048]{2,1,0:T(4,128)(2,1)S(1)} %get-tuple-element.40), channel_id=1, source_target_pairs={{0,2},{1,3},{2,0},{3,1},{4,6},{5,7},{6,4},{7,5},{8,10},{9,11},{10,... | collective-permute-start | bytes 147464 | tf_op jit(solution)/shard_map/ppermute | solution.py:396
  33.6 5.7 %collective-permute-start.4 = (f32[3,1,2048]{2,1,0:T(1,128)S(1)}, f32[3,1,2048]{2,1,0:T(1,128)S(1)}, u32[]{:S(2)}, u32[]{:S(2)}) collective-permute-start(f32[3,1,2048]{2,1,0:T(1,128)S(1)} %get-tuple-element.47), channel_id=1, source_target_pairs={{0,24},{8,16},{16,8},{24,0},{1,25},{9,17},{17,9},{25,1},{2,26},{10... | collective-permute-start | bytes 73736 | tf_op jit(solution)/shard_map/ppermute | solution.py:396
  35.1 4.7 %collective-permute-start.5 = (f32[3,1,2048]{2,1,0:T(1,128)S(1)}, f32[3,1,2048]{2,1,0:T(1,128)S(1)}, u32[]{:S(2)}, u32[]{:S(2)}) collective-permute-start(f32[3,1,2048]{2,1,0:T(1,128)S(1)} %get-tuple-element.48), channel_id=1, source_target_pairs={{0,16},{8,24},{16,0},{24,8},{1,17},{9,25},{17,1},{25,9},{2,18},{10... | collective-permute-start | bytes 73736 | tf_op jit(solution)/shard_map/ppermute | solution.py:396
  35.5 4.6 %collective-permute-start.6 = (f32[3,1,2048]{2,1,0:T(1,128)S(1)}, f32[3,1,2048]{2,1,0:T(1,128)S(1)}, u32[]{:S(2)}, u32[]{:S(2)}) collective-permute-start(f32[3,1,2048]{2,1,0:T(1,128)S(1)} %get-tuple-element.49), channel_id=1, source_target_pairs={{0,8},{8,0},{16,24},{24,16},{1,9},{9,1},{17,25},{25,17},{2,10},{10... | collective-permute-start | bytes 73736 | tf_op jit(solution)/shard_map/ppermute | solution.py:396

commit v7 on v6

--- a/solution.py
+++ b/solution.py
@@ -14,6 +14,7 @@
 ROWS = 48
 STEP = 32
 PTS = 128
+EARLY = 3
 RESIDUES = (0, 2, 1, 3)
 ROW_LANE = 64
 RUP_LANE = 96
@@ -72,11 +73,11 @@
 
 
 def pack_kernel(*refs):
-    sources = refs[:4]
-    out_ref, scr, own_ref, pts_ref, mom_ref, slip_ref, sems = refs[4:]
+    sources = (*refs[:5], refs[5].at[:EARLY])
+    out_ref, kept_ref, rows_ref, scr, own_ref, pts_ref, mom_ref, slip_ref, sems = refs[6:]
     copies = [
         pltpu.make_async_copy(src, dst, sems.at[i])
-        for i, (src, dst) in enumerate(zip(sources, (own_ref, pts_ref, mom_ref, slip_ref)))
+        for i, (src, dst) in enumerate(zip(sources, (own_ref, pts_ref, mom_ref, slip_ref, kept_ref, rows_ref)))
     ]
     for copy in copies:
         copy.start()
@@ -90,7 +91,7 @@
     comp = iota((128, 6), 1)
     spread_hi = (spread == comp).astype(F32).astype(BF16)
     spread_lo = (spread == comp + 6).astype(F32).astype(BF16)
-    for copy in copies:
+    for copy in copies[:4]:
         copy.wait()
     own = own_ref[...]
     blocks = own.shape[0]
@@ -124,6 +125,8 @@
     scr[:, :n_slip] = nn(pick16, slip)
     for d in range(devices):
         out_ref[d] = scr[d * capacity : (d + 1) * capacity, :].astype(BF16)
+    for copy in copies[4:]:
+        copy.wait()
 
 
 def forward_table(base_ref, tab_ref, block):
@@ -146,10 +149,10 @@
     lax.fori_loop(0, count, table, 0, unroll=4)
 
 
-def owner_kernel(stages, rec_ref, sgt_ref, base_ref, *refs):
+def owner_kernel(stages, rec_ref, sgt_ref, base_ref, rows_ref, *refs):
     first = stages[0][1]
     out_refs = refs[:first]
-    rec_s, x_s, p_s, slip_s, sgt_s, base_s, tab_s, sems = refs[first:]
+    rec_s, x_s, p_s, slip_s, sgt_s, tab_s, sems = refs[first:]
     devices, capacity, width = rec_ref.shape
     slots = devices * capacity
     n_time = sgt_ref.shape[2]
@@ -157,11 +160,9 @@
     wide = n_time // 4
     block_wide = n_time // 8
     n_slip = width - 128
-    base_copy = pltpu.make_async_copy(base_ref, base_s, sems.at[3])
-    base_copy.start()
     copies = []
     for c in range(3):
-        at = slice(6 * c, 6 * c + 6)
+        at = slice(6 * c if c else EARLY, 6 * c + 6)
         copies.append(pltpu.make_async_copy(sgt_ref.at[at], sgt_s.at[at], sems.at[c]))
         copies[c].start()
     for d in range(devices):
@@ -179,9 +180,8 @@
         ],
         axis=0,
     )
-    base_copy.wait()
     for block in range(4):
-        forward_table(base_s, tab_s, block)
+        forward_table(base_ref, tab_s, block)
     slip = rec_s[:, :n_slip].astype(BF16)
     for block in range(4):
         cols = slice(2 * block * block_wide, 2 * (block + 1) * block_wide)
@@ -199,7 +199,10 @@
         copies[c].wait()
         x = []
         for k in range(4):
-            rows = sgt_s[6 * c : 6 * c + 6, :, k * wide : (k + 1) * wide].reshape(6 * PTS, wide)
+            cols = slice(k * wide, (k + 1) * wide)
+            rows = sgt_s[6 * c if c else EARLY : 6 * c + 6, :, cols].reshape(-1, wide)
+            if c == 0:
+                rows = jnp.concatenate([rows_ref[:, :, cols].reshape(-1, wide), rows], axis=0)
             out = nn(left, rows)
             x.append(out[:slots] + out[slots:])
         plus = (x[0] + x[2], x[1] + x[3])
@@ -421,20 +424,26 @@
     stages = exchange_plan(n_worker, n_server)
     assert rup_w == n_server and sgt.shape[0] == PTS and slots % 16 == 0 and 4 * n_slip == n_time
 
-    record = pl.pallas_call(
+    base = jnp.asarray(forward_base(n_time))
+    sgt = in_hbm(jnp.transpose(sgt, (1, 0, 2)))
+    record, base, rows = pl.pallas_call(
         pack_kernel,
-        out_shape=jax.ShapeDtypeStruct((devices, capacity, width), BF16),
-        in_specs=[hbm()] * 4,
-        out_specs=vmem(),
+        out_shape=[
+            jax.ShapeDtypeStruct((devices, capacity, width), BF16),
+            jax.ShapeDtypeStruct(base.shape, F32),
+            jax.ShapeDtypeStruct((EARLY, PTS, n_time), BF16),
+        ],
+        in_specs=[hbm()] * 6,
+        out_specs=[vmem()] * 3,
         scratch_shapes=[
             pltpu.VMEM((slots, width), F32),
             pltpu.VMEM((ownership.shape[0] // 128, 128), jnp.int32),
             pltpu.VMEM((rup_w, sub_dev), jnp.int32),
             pltpu.VMEM((6, rup_w, sub_dev), F32),
             pltpu.VMEM((rup_w, sub_dev, n_slip), BF16),
-            pltpu.SemaphoreType.DMA((4,)),
+            pltpu.SemaphoreType.DMA((6,)),
         ],
-        compiler_params=params(12),
+        compiler_params=params(16),
         name="pack",
     )(
         *[
@@ -444,11 +453,12 @@
                 sub_points[0],
                 jnp.transpose(moments[0], (1, 0, 2)),
                 slip[0],
+                base,
+                sgt,
             )
         ]
     )
     record = lax.all_to_all(record, ("server", "worker"), split_axis=0, concat_axis=0, tiled=True)
-    base = jnp.asarray(forward_base(n_time))
 
     inverse = pl.pallas_call(
         inverse_table_kernel,
@@ -479,7 +489,7 @@
     parts = pl.pallas_call(
         functools.partial(owner_kernel, stages),
         out_shape=part_shapes(0),
-        in_specs=[vmem()] + [hbm()] * 2,
+        in_specs=[vmem(), hbm(), vmem(), vmem()],
         out_specs=[vmem()] * stages[0][1],
         scratch_shapes=[
             pltpu.VMEM((slots, width), F32),
@@ -487,14 +497,13 @@
             pltpu.VMEM((2 * slots, n_time), BF16),
             pltpu.VMEM((slots, n_time), F32),
             pltpu.VMEM((18, PTS, n_time), BF16),
-            pltpu.VMEM(base.shape, F32),
             pltpu.VMEM((half // 2, n_time), BF16),
             pltpu.SemaphoreType.DMA((4,)),
         ],
         compiler_params=params(36),
         cost_estimate=pl.CostEstimate(flops=10**10, bytes_accessed=2 * 10**7, transcendentals=0),
         name="owner",
-    )(record, in_hbm(jnp.transpose(sgt, (1, 0, 2))), in_hbm(base))
+    )(record, sgt, base, rows)
     arrived = send(parts, stages[0])
     for i in range(1, len(stages)):
         radix = stages[i][1]

time: 42.6 us -> 42 us (0.986)
  Pallas kernels: 13 us -> 12.3 us
    pallas_call x1, Pallas kernels: 7.65 us -> 6.85 us  [shards(): pl.pallas_call(functools.partial(owner_kernel, stages), out_shape=part_sh...]
where the time goes in v7:
time: 42 us; the launch traced here: 41.7 us
  blocking collectives  15.7 us (37%)
  Pallas kernels  12.3 us (29%)
  starting transfers between devices  8.47 us (20%)
  waiting for transfers between devices  4.54 us (11%)
  between operations  0.68 us (2%)
    all_to_all x1, blocking collectives, shards(): lax.all_to_all(record, ('server', 'worker'), split_axis=0, concat_axis=0,...  15.7 us
    ppermute x7, starting transfers between devices, send(): lax.ppermute(parts[k], axis, [(i, i ^ k << shift) for i in range(size)])  8.47 us
    pallas_call x1, Pallas kernels, shards(): pl.pallas_call(functools.partial(owner_kernel, stages), out_shape=part_sh...  6.85 us
    ppermute x7, waiting for transfers between devices, send(): lax.ppermute(parts[k], axis, [(i, i ^ k << shift) for i in range(size)])  4.54 us
    pallas_call x1, Pallas kernels, shards(): pl.pallas_call(functools.partial(final_kernel, count), out_shape=[jax.Sha...  2.26 us
    pallas_call x1, Pallas kernels, shards(): pl.pallas_call(pack_kernel, out_shape=[jax.ShapeDtypeStruct((devices, cap...  1.69 us
    pallas_call x2, Pallas kernels, beside(): own, *made = lax.optimization_barrier((own, *kernel(base)))  1.34 us
  transfers between devices with their start and end apart: 7, of which 7 were waited for; matrix products, arithmetic and copies ran while one was open for 0% of the time, Pallas kernels for 3%

profile of v7, /device:TPU:0, one launch (start us, length us, event | category | flops | bytes accessed | tf_op | source)
XLA Modules:
  0.0 41.7 jit_solution(5550833072318647384)
XLA Ops:
  0.6 1.7 %pack.1 = (bf16[32,4,640]{2,1,0:T(4,128)(2,1)S(1)}, f32[96,1024]{1,0:T(8,128)S(1)}, bf16[3,128,2048]{2,1,0:T(8,128)(2,1)S(1)}) custom-call(s32[32,128]{1,0:T(8,128)} %bitcast.16, s32[4,24]{1,0:T(4,128)} %bitcast.18, f32[6,4,24]{2,1,0:T(4,128)} %bitcast.17, bf16[4,24,512]{2,1,0:T(8,128)(2,1)} %bitcast.15, f32[96,1024]{1,0:T(8,128)} %constant.6.clone.refs_4_, ...), custom_call_target="tpu_custom_call" | custom-call | tf_op jit(solution)/shard_map/pack/pallas_call | solution.py:429
  2.3 15.7 %all_to_all.5.rec_ref = bf16[32,4,640]{2,1,0:T(4,128)(2,1)S(1)} all-to-all(bf16[32,4,640]{2,1,0:T(4,128)(2,1)S(1)} %get-tuple-element.33), channel_id=1, replica_groups=mesh['server'=4,'worker'=8] {'server','worker'}, dimensions={0} | all-to-all | bytes 327680 | tf_op jit(solution)/shard_map/all_to_all | solution.py:461
  18.0 0.0 copy-start.1
  18.0 0.0 copy-start
  18.0 6.8 %owner.1 = (f32[3,16,2048]{2,1,0:T(8,128)S(1)}, f32[3,16,2048]{2,1,0:T(8,128)S(1)}) custom-call(bf16[32,4,640]{2,1,0:T(4,128)(2,1)S(1)} %all_to_all.5.rec_ref, bf16[18,128,2048]{2,1,0:T(8,128)(2,1)} %bitcast.14, f32[96,1024]{1,0:T(8,128)S(1)} %get-tuple-element.34.base_ref, bf16[3,128,2048]{2,1,0:T(8,128)(2,1)S(1)} %get-tuple-element.35.rows_ref), custom_call_target="tpu_custom_call" | custom-call | flops 10000000000 | bytes 20000000 | tf_op jit(solution)/shard_map/owner/pallas_call | solution.py:489
  24.9 0.4 %collective-permute-start = (f32[3,16,2048]{2,1,0:T(8,128)S(1)}, f32[3,16,2048]{2,1,0:T(8,128)S(1)}, u32[]{:S(2)}, u32[]{:S(2)}) collective-permute-start(f32[3,16,2048]{2,1,0:T(8,128)S(1)} %get-tuple-element.37), channel_id=1, source_target_pairs={{0,1},{1,0},{2,3},{3,2},{4,5},{5,4},{6,7},{7,6},{8,9},{9,8},{10,11... | collective-permute-start | bytes 1179656 | tf_op jit(solution)/shard_map/ppermute | solution.py:399
  25.3 0.1 gain.1
  25.4 1.2 %collective-permute-done.refs_1_ = f32[3,16,2048]{2,1,0:T(8,128)S(1)} collective-permute-done((f32[3,16,2048]{2,1,0:T(8,128)S(1)}, f32[3,16,2048]{2,1,0:T(8,128)S(1)}, u32[]{:S(2)}, u32[]{:S(2)}) %collective-permute-start) | collective-permute-done | bytes 393248 | tf_op jit(solution)/shard_map/ppermute | solution.py:399
  26.7 1.1 %collective-permute-start.1 = (bf16[3,4,2048]{2,1,0:T(4,128)(2,1)S(1)}, bf16[3,4,2048]{2,1,0:T(4,128)(2,1)S(1)}, u32[]{:S(2)}, u32[]{:S(2)}) collective-permute-start(bf16[3,4,2048]{2,1,0:T(4,128)(2,1)S(1)} %get-tuple-element.44), channel_id=1, source_target_pairs={{0,6},{1,7},{2,4},{3,5},{4,2},{5,3},{6,0},{7,1},{8,14},{9,15},{10,... | collective-permute-start | bytes 147464 | tf_op jit(solution)/shard_map/ppermute | solution.py:399
  27.8 1.0 %collective-permute-start.2 = (bf16[3,4,2048]{2,1,0:T(4,128)(2,1)S(1)}, bf16[3,4,2048]{2,1,0:T(4,128)(2,1)S(1)}, u32[]{:S(2)}, u32[]{:S(2)}) collective-permute-start(bf16[3,4,2048]{2,1,0:T(4,128)(2,1)S(1)} %get-tuple-element.45), channel_id=1, source_target_pairs={{0,4},{1,5},{2,6},{3,7},{4,0},{5,1},{6,2},{7,3},{8,12},{9,13},{10,... | collective-permute-start | bytes 147464 | tf_op jit(solution)/shard_map/ppermute | solution.py:399
  28.8 1.5 %collective-permute-start.3 = (bf16[3,4,2048]{2,1,0:T(4,128)(2,1)S(1)}, bf16[3,4,2048]{2,1,0:T(4,128)(2,1)S(1)}, u32[]{:S(2)}, u32[]{:S(2)}) collective-permute-start(bf16[3,4,2048]{2,1,0:T(4,128)(2,1)S(1)} %get-tuple-element.46), channel_id=1, source_target_pairs={{0,2},{1,3},{2,0},{3,1},{4,6},{5,7},{6,4},{7,5},{8,10},{9,11},{10,... | collective-permute-start | bytes 147464 | tf_op jit(solution)/shard_map/ppermute | solution.py:399
  30.3 0.0 copy-done.1
  30.3 0.7 %inverse_table.2 = (bf16[1024,512]{1,0:T(8,128)(2,1)S(1)}, bf16[1024,512]{1,0:T(8,128)(2,1)S(1)}) custom-call(f32[144,512]{1,0:T(8,128)S(1)} %copy-done.1), custom_call_target="tpu_custom_call" | custom-call | flops 1000000000 | bytes 10000000 | tf_op jit(solution)/shard_map/inverse_table/pallas_call | solution.py:406
  31.0 1.2 %collective-permute-done.1.refs_1_ = bf16[3,4,2048]{2,1,0:T(4,128)(2,1)S(1)} collective-permute-done((bf16[3,4,2048]{2,1,0:T(4,128)(2,1)S(1)}, bf16[3,4,2048]{2,1,0:T(4,128)(2,1)S(1)}, u32[]{:S(2)}, u32[]{:S(2)}) %collective-permute-start.1) | collective-permute-done | bytes 49184 | tf_op jit(solution)/shard_map/ppermute | solution.py:399
  32.1 0.2 collective-permute-done.2.refs_2_
  32.3 0.6 %collective-permute-done.3.refs_3_ = bf16[3,4,2048]{2,1,0:T(4,128)(2,1)S(1)} collective-permute-done((bf16[3,4,2048]{2,1,0:T(4,128)(2,1)S(1)}, bf16[3,4,2048]{2,1,0:T(4,128)(2,1)S(1)}, u32[]{:S(2)}, u32[]{:S(2)}) %collective-permute-start.3) | collective-permute-done | bytes 49184 | tf_op jit(solution)/shard_map/ppermute | solution.py:399
  33.0 1.5 %collective-permute-start.4 = (f32[3,1,2048]{2,1,0:T(1,128)S(1)}, f32[3,1,2048]{2,1,0:T(1,128)S(1)}, u32[]{:S(2)}, u32[]{:S(2)}) collective-permute-start(f32[3,1,2048]{2,1,0:T(1,128)S(1)} %get-tuple-element.53), channel_id=1, source_target_pairs={{0,24},{8,16},{16,8},{24,0},{1,25},{9,17},{17,9},{25,1},{2,26},{10... | collective-permute-start | bytes 73736 | tf_op jit(solution)/shard_map/ppermute | solution.py:399
  34.4 0.4 %collective-permute-start.5 = (f32[3,1,2048]{2,1,0:T(1,128)S(1)}, f32[3,1,2048]{2,1,0:T(1,128)S(1)}, u32[]{:S(2)}, u32[]{:S(2)}) collective-permute-start(f32[3,1,2048]{2,1,0:T(1,128)S(1)} %get-tuple-element.54), channel_id=1, source_target_pairs={{0,16},{8,24},{16,0},{24,8},{1,17},{9,25},{17,1},{25,9},{2,18},{10... | collective-permute-start | bytes 73736 | tf_op jit(solution)/shard_map/ppermute | solution.py:399
  34.9 2.5 %collective-permute-start.6 = (f32[3,1,2048]{2,1,0:T(1,128)S(1)}, f32[3,1,2048]{2,1,0:T(1,128)S(1)}, u32[]{:S(2)}, u32[]{:S(2)}) collective-permute-start(f32[3,1,2048]{2,1,0:T(1,128)S(1)} %get-tuple-element.55), channel_id=1, source_target_pairs={{0,8},{8,0},{16,24},{24,16},{1,9},{9,1},{17,25},{25,17},{2,10},{10... | collective-permute-start | bytes 73736 | tf_op jit(solution)/shard_map/ppermute | solution.py:399
  37.4 0.0 copy-done
  37.4 0.7 %inverse_table.3 = (bf16[1024,512]{1,0:T(8,128)(2,1)S(1)}, bf16[1024,512]{1,0:T(8,128)(2,1)S(1)}) custom-call(f32[144,512]{1,0:T(8,128)S(1)} %copy-done), custom_call_target="tpu_custom_call" | custom-call | flops 1000000000 | bytes 10000000 | tf_op jit(solution)/shard_map/inverse_table/pallas_call | solution.py:406
  38.1 0.6 %collective-permute-done.4.refs_1_ = f32[3,1,2048]{2,1,0:T(1,128)S(1)} collective-permute-done((f32[3,1,2048]{2,1,0:T(1,128)S(1)}, f32[3,1,2048]{2,1,0:T(1,128)S(1)}, u32[]{:S(2)}, u32[]{:S(2)}) %collective-permute-start.4) | collective-permute-done | bytes 24608 | tf_op jit(solution)/shard_map/ppermute | solution.py:399
  38.6 0.5 %collective-permute-done.5.refs_2_ = f32[3,1,2048]{2,1,0:T(1,128)S(1)} collective-permute-done((f32[3,1,2048]{2,1,0:T(1,128)S(1)}, f32[3,1,2048]{2,1,0:T(1,128)S(1)}, u32[]{:S(2)}, u32[]{:S(2)}) %collective-permute-start.5) | collective-permute-done | bytes 24608 | tf_op jit(solution)/shard_map/ppermute | solution.py:399
  39.2 0.2 collective-permute-done.6.refs_3_
  39.4 2.3 %finish.1 = (f32[3,1,2048]{2,1,0:T(1,128)}, f32[3,1,44]{2,1,0:T(1,128)}) custom-call(f32[3,1,2048]{2,1,0:T(1,128)S(1)} %get-tuple-element.52.refs_0_, f32[3,1,2048]{2,1,0:T(1,128)S(1)} %collective-permute-done.4.refs_1_, f32[3,1,2048]{2,1,0:T(1,128)S(1)} %collective-permute-done.5.refs_2_, f32[3,1,2048]{2,1,0:T(1,128)S(1)} %collective-permute-done.6.refs_3_, ...), custom_call_target="tpu_custom_call" | custom-call | tf_op jit(solution)/shard_map/finish/pallas_call | solution.py:524
  (2 shorter events, 0.1 us)
Async XLA Ops:
  18.0 12.3 %copy-start.1 = (f32[144,512]{1,0:T(8,128)S(1)}, f32[144,512]{1,0:T(8,128)}, u32[]{:S(2)}) copy-start(f32[144,512]{1,0:T(8,128)} %constant.7.clone.base_ref) | copy-start | bytes 884740
  18.0 19.4 %copy-start = (f32[144,512]{1,0:T(8,128)S(1)}, f32[144,512]{1,0:T(8,128)}, u32[]{:S(2)}) copy-start(f32[144,512]{1,0:T(8,128)} %constant.8.clone.base_ref) | copy-start | bytes 884740
  24.9 1.8 %collective-permute-start = (f32[3,16,2048]{2,1,0:T(8,128)S(1)}, f32[3,16,2048]{2,1,0:T(8,128)S(1)}, u32[]{:S(2)}, u32[]{:S(2)}) collective-permute-start(f32[3,16,2048]{2,1,0:T(8,128)S(1)} %get-tuple-element.37), channel_id=1, source_target_pairs={{0,1},{1,0},{2,3},{3,2},{4,5},{5,4},{6,7},{7,6},{8,9},{9,8},{10,11... | collective-permute-start | bytes 1179656 | tf_op jit(solution)/shard_map/ppermute | solution.py:399
  26.7 5.4 %collective-permute-start.1 = (bf16[3,4,2048]{2,1,0:T(4,128)(2,1)S(1)}, bf16[3,4,2048]{2,1,0:T(4,128)(2,1)S(1)}, u32[]{:S(2)}, u32[]{:S(2)}) collective-permute-start(bf16[3,4,2048]{2,1,0:T(4,128)(2,1)S(1)} %get-tuple-element.44), channel_id=1, source_target_pairs={{0,6},{1,7},{2,4},{3,5},{4,2},{5,3},{6,0},{7,1},{8,14},{9,15},{10,... | collective-permute-start | bytes 147464 | tf_op jit(solution)/shard_map/ppermute | solution.py:399
  27.8 4.6 %collective-permute-start.2 = (bf16[3,4,2048]{2,1,0:T(4,128)(2,1)S(1)}, bf16[3,4,2048]{2,1,0:T(4,128)(2,1)S(1)}, u32[]{:S(2)}, u32[]{:S(2)}) collective-permute-start(bf16[3,4,2048]{2,1,0:T(4,128)(2,1)S(1)} %get-tuple-element.45), channel_id=1, source_target_pairs={{0,4},{1,5},{2,6},{3,7},{4,0},{5,1},{6,2},{7,3},{8,12},{9,13},{10,... | collective-permute-start | bytes 147464 | tf_op jit(solution)/shard_map/ppermute | solution.py:399
  28.8 4.1 %collective-permute-start.3 = (bf16[3,4,2048]{2,1,0:T(4,128)(2,1)S(1)}, bf16[3,4,2048]{2,1,0:T(4,128)(2,1)S(1)}, u32[]{:S(2)}, u32[]{:S(2)}) collective-permute-start(bf16[3,4,2048]{2,1,0:T(4,128)(2,1)S(1)} %get-tuple-element.46), channel_id=1, source_target_pairs={{0,2},{1,3},{2,0},{3,1},{4,6},{5,7},{6,4},{7,5},{8,10},{9,11},{10,... | collective-permute-start | bytes 147464 | tf_op jit(solution)/shard_map/ppermute | solution.py:399
  33.0 5.7 %collective-permute-start.4 = (f32[3,1,2048]{2,1,0:T(1,128)S(1)}, f32[3,1,2048]{2,1,0:T(1,128)S(1)}, u32[]{:S(2)}, u32[]{:S(2)}) collective-permute-start(f32[3,1,2048]{2,1,0:T(1,128)S(1)} %get-tuple-element.53), channel_id=1, source_target_pairs={{0,24},{8,16},{16,8},{24,0},{1,25},{9,17},{17,9},{25,1},{2,26},{10... | collective-permute-start | bytes 73736 | tf_op jit(solution)/shard_map/ppermute | solution.py:399
  34.4 4.8 %collective-permute-start.5 = (f32[3,1,2048]{2,1,0:T(1,128)S(1)}, f32[3,1,2048]{2,1,0:T(1,128)S(1)}, u32[]{:S(2)}, u32[]{:S(2)}) collective-permute-start(f32[3,1,2048]{2,1,0:T(1,128)S(1)} %get-tuple-element.54), channel_id=1, source_target_pairs={{0,16},{8,24},{16,0},{24,8},{1,17},{9,25},{17,1},{25,9},{2,18},{10... | collective-permute-start | bytes 73736 | tf_op jit(solution)/shard_map/ppermute | solution.py:399
  34.9 4.6 %collective-permute-start.6 = (f32[3,1,2048]{2,1,0:T(1,128)S(1)}, f32[3,1,2048]{2,1,0:T(1,128)S(1)}, u32[]{:S(2)}, u32[]{:S(2)}) collective-permute-start(f32[3,1,2048]{2,1,0:T(1,128)S(1)} %get-tuple-element.55), channel_id=1, source_target_pairs={{0,8},{8,0},{16,24},{24,16},{1,9},{9,1},{17,25},{25,17},{2,10},{10... | collective-permute-start | bytes 73736 | tf_op jit(solution)/shard_map/ppermute | solution.py:399

commit v8 on v7

--- a/solution.py
+++ b/solution.py
@@ -256,13 +256,13 @@
             out_refs[k][c] = total[k * part : (k + 1) * part].astype(out_refs[k].dtype)
 
 
-def inverse_table_kernel(base_ref, hi_ref, lo_ref):
-    block_wide = hi_ref.shape[0] // 4
+def inverse_table_kernel(base_ref, tab_ref):
+    block_wide = tab_ref.shape[0] // 4
     count = block_wide // STEP
     wide = 256
     for p in range(2):
         fine = 2 * count + 2 * p * STEP
-        for lc in range(hi_ref.shape[1] // wide):
+        for lc in range(tab_ref.shape[1] // wide):
             sl = slice(lc * wide, (lc + 1) * wide)
             cf = base_ref[fine : fine + STEP, sl]
             sf = base_ref[fine + STEP : fine + 2 * STEP, sl]
@@ -272,9 +272,7 @@
                 sa = base_ref[pl.ds(count + a, 1), sl]
                 for base, value in ((0, ca * cf - sa * sf), (block_wide, -(sa * cf + ca * sf))):
                     at = pl.ds(pl.multiple_of(2 * p * block_wide + base + a * STEP, STEP), STEP)
-                    hi, lo = hilo(value)
-                    hi_ref[at, sl] = hi
-                    lo_ref[at, sl] = lo
+                    tab_ref[at, sl] = value.astype(BF16)
                 return carry
 
             lax.fori_loop(0, count, table, 0)
@@ -325,18 +323,16 @@
         im = jnp.concatenate([s[:, cols_im] * g_re - s[:, cols] * g_im for s in spec], axis=0)
         return re, im
 
-    def product(left, hi_tab, lo_tab):
+    def product(left, table):
         count = left.shape[0]
-        hi, lo = hilo(left)
-        both = nn(jnp.concatenate([hi, lo], axis=0), hi_tab)
-        return both[:count] + both[count:] + nn(hi, lo_tab)
-
-    even_hi, even_lo, odd_hi, odd_lo = tables
+        both = nn(jnp.concatenate(hilo(left), axis=0), table)
+        return both[:count] + both[count:]
+
+    even_ref, odd_ref = tables
     pair = [
         product(
             jnp.concatenate(accel(block), axis=1),
-            even_hi[block * wide : (block + 1) * wide, :],
-            even_lo[block * wide : (block + 1) * wide, :],
+            even_ref[block * wide : (block + 1) * wide, :],
         )
         for block in range(2)
     ]
@@ -344,7 +340,7 @@
     re_d, im_d = accel(3)
     straight = jnp.concatenate([re_c, im_c, re_d, im_d], axis=1)
     turned = jnp.concatenate([-im_c, re_c, im_d, -re_d], axis=1)
-    odd = product(jnp.concatenate([straight, turned], axis=0), odd_hi[...], odd_lo[...])
+    odd = product(jnp.concatenate([straight, turned], axis=0), odd_ref[...])
     evens = (pair[0] + pair[1], pair[0] - pair[1])
     odds = (odd[: 3 * ROWS], odd[3 * ROWS :])
     peak = jnp.max(
@@ -462,9 +458,9 @@
 
     inverse = pl.pallas_call(
         inverse_table_kernel,
-        out_shape=[jax.ShapeDtypeStruct((half, half // 2), BF16)] * 2,
+        out_shape=[jax.ShapeDtypeStruct((half, half // 2), BF16)],
         in_specs=[vmem()],
-        out_specs=[vmem()] * 2,
+        out_specs=[vmem()],
         compiler_params=params(8),
         cost_estimate=pl.CostEstimate(flops=10**9, bytes_accessed=10**7, transcendentals=0),
         name="inverse_table",
@@ -517,7 +513,7 @@
         )(parts[0], *arrived)
         arrived = send(parts, stages[i])
         if i >= len(stages) - 2:
-            own, pair = beside(inverse, bases[len(tables) // 2], parts[0])
+            own, pair = beside(inverse, bases[len(tables)], parts[0])
             parts = [own]
             tables += pair
     count = 1 + len(arrived)
@@ -527,7 +523,7 @@
             jax.ShapeDtypeStruct((3, 1, n_time), F32),
             jax.ShapeDtypeStruct((3, 1, PERIODS), F32),
         ],
-        in_specs=[vmem()] * (count + 6),
+        in_specs=[vmem()] * (count + 4),
         out_specs=[vmem()] * 2,
         compiler_params=params(20),
         name="finish",

time: 42 us -> 41.5 us (0.988)
  Pallas kernels: 12.3 us -> 11.5 us
    pallas_call x1, Pallas kernels: 2.26 us -> 1.82 us  [shards(): pl.pallas_call(functools.partial(final_kernel, count), out_shape=[jax.Sha...]
where the time goes in v8:
time: 41.5 us; the launch traced here: 41.3 us
  blocking collectives  15.7 us (38%)
  Pallas kernels  11.5 us (28%)
  starting transfers between devices  8.47 us (20%)
  waiting for transfers between devices  4.94 us (12%)
  between operations  0.68 us (2%)
    all_to_all x1, blocking collectives, shards(): lax.all_to_all(record, ('server', 'worker'), split_axis=0, concat_axis=0,...  15.7 us
    ppermute x7, starting transfers between devices, send(): lax.ppermute(parts[k], axis, [(i, i ^ k << shift) for i in range(size)])  8.47 us
    pallas_call x1, Pallas kernels, shards(): pl.pallas_call(functools.partial(owner_kernel, stages), out_shape=part_sh...  6.85 us
    ppermute x7, waiting for transfers between devices, send(): lax.ppermute(parts[k], axis, [(i, i ^ k << shift) for i in range(size)])  4.94 us
    pallas_call x1, Pallas kernels, shards(): pl.pallas_call(functools.partial(final_kernel, count), out_shape=[jax.Sha...  1.82 us
    pallas_call x1, Pallas kernels, shards(): pl.pallas_call(pack_kernel, out_shape=[jax.ShapeDtypeStruct((devices, cap...  1.69 us
    pallas_call x2, Pallas kernels, beside(): own, *made = lax.optimization_barrier((own, *kernel(base)))  0.93 us
  transfers between devices with their start and end apart: 7, of which 7 were waited for; matrix products, arithmetic and copies ran while one was open for 0% of the time, Pallas kernels for 3%

profile of v8, /device:TPU:0, one launch (start us, length us, event | category | flops | bytes accessed | tf_op | source)
XLA Modules:
  0.0 41.3 jit_solution(11193975603072209158)
XLA Ops:
  0.6 1.7 %pack.1 = (bf16[32,4,640]{2,1,0:T(4,128)(2,1)S(1)}, f32[96,1024]{1,0:T(8,128)S(1)}, bf16[3,128,2048]{2,1,0:T(8,128)(2,1)S(1)}) custom-call(s32[32,128]{1,0:T(8,128)} %bitcast.16, s32[4,24]{1,0:T(4,128)} %bitcast.18, f32[6,4,24]{2,1,0:T(4,128)} %bitcast.17, bf16[4,24,512]{2,1,0:T(8,128)(2,1)} %bitcast.15, f32[96,1024]{1,0:T(8,128)} %constant.6.clone.refs_4_, ...), custom_call_target="tpu_custom_call" | custom-call | tf_op jit(solution)/shard_map/pack/pallas_call | solution.py:425
  2.3 15.7 %all_to_all.5.rec_ref = bf16[32,4,640]{2,1,0:T(4,128)(2,1)S(1)} all-to-all(bf16[32,4,640]{2,1,0:T(4,128)(2,1)S(1)} %get-tuple-element.27), channel_id=1, replica_groups=mesh['server'=4,'worker'=8] {'server','worker'}, dimensions={0} | all-to-all | bytes 327680 | tf_op jit(solution)/shard_map/all_to_all | solution.py:457
  18.0 0.0 copy-start.1
  18.0 0.0 copy-start
  18.0 6.8 %owner.1 = (f32[3,16,2048]{2,1,0:T(8,128)S(1)}, f32[3,16,2048]{2,1,0:T(8,128)S(1)}) custom-call(bf16[32,4,640]{2,1,0:T(4,128)(2,1)S(1)} %all_to_all.5.rec_ref, bf16[18,128,2048]{2,1,0:T(8,128)(2,1)} %bitcast.14, f32[96,1024]{1,0:T(8,128)S(1)} %get-tuple-element.28.base_ref, bf16[3,128,2048]{2,1,0:T(8,128)(2,1)S(1)} %get-tuple-element.29.rows_ref), custom_call_target="tpu_custom_call" | custom-call | flops 10000000000 | bytes 20000000 | tf_op jit(solution)/shard_map/owner/pallas_call | solution.py:485
  24.9 0.4 %collective-permute-start = (f32[3,16,2048]{2,1,0:T(8,128)S(1)}, f32[3,16,2048]{2,1,0:T(8,128)S(1)}, u32[]{:S(2)}, u32[]{:S(2)}) collective-permute-start(f32[3,16,2048]{2,1,0:T(8,128)S(1)} %get-tuple-element.31), channel_id=1, source_target_pairs={{0,1},{1,0},{2,3},{3,2},{4,5},{5,4},{6,7},{7,6},{8,9},{9,8},{10,11... | collective-permute-start | bytes 1179656 | tf_op jit(solution)/shard_map/ppermute | solution.py:395
  25.3 0.1 gain.1
  25.4 1.2 %collective-permute-done.refs_1_ = f32[3,16,2048]{2,1,0:T(8,128)S(1)} collective-permute-done((f32[3,16,2048]{2,1,0:T(8,128)S(1)}, f32[3,16,2048]{2,1,0:T(8,128)S(1)}, u32[]{:S(2)}, u32[]{:S(2)}) %collective-permute-start) | collective-permute-done | bytes 393248 | tf_op jit(solution)/shard_map/ppermute | solution.py:395
  26.7 1.1 %collective-permute-start.1 = (bf16[3,4,2048]{2,1,0:T(4,128)(2,1)S(1)}, bf16[3,4,2048]{2,1,0:T(4,128)(2,1)S(1)}, u32[]{:S(2)}, u32[]{:S(2)}) collective-permute-start(bf16[3,4,2048]{2,1,0:T(4,128)(2,1)S(1)} %get-tuple-element.36), channel_id=1, source_target_pairs={{0,6},{1,7},{2,4},{3,5},{4,2},{5,3},{6,0},{7,1},{8,14},{9,15},{10,... | collective-permute-start | bytes 147464 | tf_op jit(solution)/shard_map/ppermute | solution.py:395
  27.8 1.0 %collective-permute-start.2 = (bf16[3,4,2048]{2,1,0:T(4,128)(2,1)S(1)}, bf16[3,4,2048]{2,1,0:T(4,128)(2,1)S(1)}, u32[]{:S(2)}, u32[]{:S(2)}) collective-permute-start(bf16[3,4,2048]{2,1,0:T(4,128)(2,1)S(1)} %get-tuple-element.37), channel_id=1, source_target_pairs={{0,4},{1,5},{2,6},{3,7},{4,0},{5,1},{6,2},{7,3},{8,12},{9,13},{10,... | collective-permute-start | bytes 147464 | tf_op jit(solution)/shard_map/ppermute | solution.py:395
  28.8 1.5 %collective-permute-start.3 = (bf16[3,4,2048]{2,1,0:T(4,128)(2,1)S(1)}, bf16[3,4,2048]{2,1,0:T(4,128)(2,1)S(1)}, u32[]{:S(2)}, u32[]{:S(2)}) collective-permute-start(bf16[3,4,2048]{2,1,0:T(4,128)(2,1)S(1)} %get-tuple-element.38), channel_id=1, source_target_pairs={{0,2},{1,3},{2,0},{3,1},{4,6},{5,7},{6,4},{7,5},{8,10},{9,11},{10,... | collective-permute-start | bytes 147464 | tf_op jit(solution)/shard_map/ppermute | solution.py:395
  30.3 0.0 copy-done.1
  30.3 0.5 %inverse_table.2.refs_4_ = bf16[1024,512]{1,0:T(8,128)(2,1)S(1)} custom-call(f32[144,512]{1,0:T(8,128)S(1)} %copy-done.1), custom_call_target="tpu_custom_call" | custom-call | flops 1000000000 | bytes 10000000 | tf_op jit(solution)/shard_map/inverse_table/pallas_call | solution.py:402
  30.8 1.4 %collective-permute-done.1.refs_1_ = bf16[3,4,2048]{2,1,0:T(4,128)(2,1)S(1)} collective-permute-done((bf16[3,4,2048]{2,1,0:T(4,128)(2,1)S(1)}, bf16[3,4,2048]{2,1,0:T(4,128)(2,1)S(1)}, u32[]{:S(2)}, u32[]{:S(2)}) %collective-permute-start.1) | collective-permute-done | bytes 49184 | tf_op jit(solution)/shard_map/ppermute | solution.py:395
  32.1 0.2 collective-permute-done.2.refs_2_
  32.3 0.6 %collective-permute-done.3.refs_3_ = bf16[3,4,2048]{2,1,0:T(4,128)(2,1)S(1)} collective-permute-done((bf16[3,4,2048]{2,1,0:T(4,128)(2,1)S(1)}, bf16[3,4,2048]{2,1,0:T(4,128)(2,1)S(1)}, u32[]{:S(2)}, u32[]{:S(2)}) %collective-permute-start.3) | collective-permute-done | bytes 49184 | tf_op jit(solution)/shard_map/ppermute | solution.py:395
  33.0 1.5 %collective-permute-start.4 = (f32[3,1,2048]{2,1,0:T(1,128)S(1)}, f32[3,1,2048]{2,1,0:T(1,128)S(1)}, u32[]{:S(2)}, u32[]{:S(2)}) collective-permute-start(f32[3,1,2048]{2,1,0:T(1,128)S(1)} %get-tuple-element.43), channel_id=1, source_target_pairs={{0,24},{8,16},{16,8},{24,0},{1,25},{9,17},{17,9},{25,1},{2,26},{10... | collective-permute-start | bytes 73736 | tf_op jit(solution)/shard_map/ppermute | solution.py:395
  34.4 0.4 %collective-permute-start.5 = (f32[3,1,2048]{2,1,0:T(1,128)S(1)}, f32[3,1,2048]{2,1,0:T(1,128)S(1)}, u32[]{:S(2)}, u32[]{:S(2)}) collective-permute-start(f32[3,1,2048]{2,1,0:T(1,128)S(1)} %get-tuple-element.44), channel_id=1, source_target_pairs={{0,16},{8,24},{16,0},{24,8},{1,17},{9,25},{17,1},{25,9},{2,18},{10... | collective-permute-start | bytes 73736 | tf_op jit(solution)/shard_map/ppermute | solution.py:395
  34.9 2.5 %collective-permute-start.6 = (f32[3,1,2048]{2,1,0:T(1,128)S(1)}, f32[3,1,2048]{2,1,0:T(1,128)S(1)}, u32[]{:S(2)}, u32[]{:S(2)}) collective-permute-start(f32[3,1,2048]{2,1,0:T(1,128)S(1)} %get-tuple-element.45), channel_id=1, source_target_pairs={{0,8},{8,0},{16,24},{24,16},{1,9},{9,1},{17,25},{25,17},{2,10},{10... | collective-permute-start | bytes 73736 | tf_op jit(solution)/shard_map/ppermute | solution.py:395
  37.4 0.0 copy-done
  37.4 0.5 %inverse_table.3.refs_5_ = bf16[1024,512]{1,0:T(8,128)(2,1)S(1)} custom-call(f32[144,512]{1,0:T(8,128)S(1)} %copy-done), custom_call_target="tpu_custom_call" | custom-call | flops 1000000000 | bytes 10000000 | tf_op jit(solution)/shard_map/inverse_table/pallas_call | solution.py:402
  37.9 0.8 %collective-permute-done.4.refs_1_ = f32[3,1,2048]{2,1,0:T(1,128)S(1)} collective-permute-done((f32[3,1,2048]{2,1,0:T(1,128)S(1)}, f32[3,1,2048]{2,1,0:T(1,128)S(1)}, u32[]{:S(2)}, u32[]{:S(2)}) %collective-permute-start.4) | collective-permute-done | bytes 24608 | tf_op jit(solution)/shard_map/ppermute | solution.py:395
  38.6 0.5 %collective-permute-done.5.refs_2_ = f32[3,1,2048]{2,1,0:T(1,128)S(1)} collective-permute-done((f32[3,1,2048]{2,1,0:T(1,128)S(1)}, f32[3,1,2048]{2,1,0:T(1,128)S(1)}, u32[]{:S(2)}, u32[]{:S(2)}) %collective-permute-start.5) | collective-permute-done | bytes 24608 | tf_op jit(solution)/shard_map/ppermute | solution.py:395
  39.2 0.2 collective-permute-done.6.refs_3_
  39.4 1.8 %finish.1 = (f32[3,1,2048]{2,1,0:T(1,128)}, f32[3,1,44]{2,1,0:T(1,128)}) custom-call(f32[3,1,2048]{2,1,0:T(1,128)S(1)} %get-tuple-element.42.refs_0_, f32[3,1,2048]{2,1,0:T(1,128)S(1)} %collective-permute-done.4.refs_1_, f32[3,1,2048]{2,1,0:T(1,128)S(1)} %collective-permute-done.5.refs_2_, f32[3,1,2048]{2,1,0:T(1,128)S(1)} %collective-permute-done.6.refs_3_, ...), custom_call_target="tpu_custom_call" | custom-call | tf_op jit(solution)/shard_map/finish/pallas_call | solution.py:520
  (2 shorter events, 0.1 us)
Async XLA Ops:
  18.0 12.3 %copy-start.1 = (f32[144,512]{1,0:T(8,128)S(1)}, f32[144,512]{1,0:T(8,128)}, u32[]{:S(2)}) copy-start(f32[144,512]{1,0:T(8,128)} %constant.7.clone.base_ref) | copy-start | bytes 884740
  18.0 19.4 %copy-start = (f32[144,512]{1,0:T(8,128)S(1)}, f32[144,512]{1,0:T(8,128)}, u32[]{:S(2)}) copy-start(f32[144,512]{1,0:T(8,128)} %constant.8.clone.base_ref) | copy-start | bytes 884740
  24.9 1.8 %collective-permute-start = (f32[3,16,2048]{2,1,0:T(8,128)S(1)}, f32[3,16,2048]{2,1,0:T(8,128)S(1)}, u32[]{:S(2)}, u32[]{:S(2)}) collective-permute-start(f32[3,16,2048]{2,1,0:T(8,128)S(1)} %get-tuple-element.31), channel_id=1, source_target_pairs={{0,1},{1,0},{2,3},{3,2},{4,5},{5,4},{6,7},{7,6},{8,9},{9,8},{10,11... | collective-permute-start | bytes 1179656 | tf_op jit(solution)/shard_map/ppermute | solution.py:395
  26.7 5.4 %collective-permute-start.1 = (bf16[3,4,2048]{2,1,0:T(4,128)(2,1)S(1)}, bf16[3,4,2048]{2,1,0:T(4,128)(2,1)S(1)}, u32[]{:S(2)}, u32[]{:S(2)}) collective-permute-start(bf16[3,4,2048]{2,1,0:T(4,128)(2,1)S(1)} %get-tuple-element.36), channel_id=1, source_target_pairs={{0,6},{1,7},{2,4},{3,5},{4,2},{5,3},{6,0},{7,1},{8,14},{9,15},{10,... | collective-permute-start | bytes 147464 | tf_op jit(solution)/shard_map/ppermute | solution.py:395
  27.8 4.6 %collective-permute-start.2 = (bf16[3,4,2048]{2,1,0:T(4,128)(2,1)S(1)}, bf16[3,4,2048]{2,1,0:T(4,128)(2,1)S(1)}, u32[]{:S(2)}, u32[]{:S(2)}) collective-permute-start(bf16[3,4,2048]{2,1,0:T(4,128)(2,1)S(1)} %get-tuple-element.37), channel_id=1, source_target_pairs={{0,4},{1,5},{2,6},{3,7},{4,0},{5,1},{6,2},{7,3},{8,12},{9,13},{10,... | collective-permute-start | bytes 147464 | tf_op jit(solution)/shard_map/ppermute | solution.py:395
  28.8 4.1 %collective-permute-start.3 = (bf16[3,4,2048]{2,1,0:T(4,128)(2,1)S(1)}, bf16[3,4,2048]{2,1,0:T(4,128)(2,1)S(1)}, u32[]{:S(2)}, u32[]{:S(2)}) collective-permute-start(bf16[3,4,2048]{2,1,0:T(4,128)(2,1)S(1)} %get-tuple-element.38), channel_id=1, source_target_pairs={{0,2},{1,3},{2,0},{3,1},{4,6},{5,7},{6,4},{7,5},{8,10},{9,11},{10,... | collective-permute-start | bytes 147464 | tf_op jit(solution)/shard_map/ppermute | solution.py:395
  33.0 5.7 %collective-permute-start.4 = (f32[3,1,2048]{2,1,0:T(1,128)S(1)}, f32[3,1,2048]{2,1,0:T(1,128)S(1)}, u32[]{:S(2)}, u32[]{:S(2)}) collective-permute-start(f32[3,1,2048]{2,1,0:T(1,128)S(1)} %get-tuple-element.43), channel_id=1, source_target_pairs={{0,24},{8,16},{16,8},{24,0},{1,25},{9,17},{17,9},{25,1},{2,26},{10... | collective-permute-start | bytes 73736 | tf_op jit(solution)/shard_map/ppermute | solution.py:395
  34.4 4.8 %collective-permute-start.5 = (f32[3,1,2048]{2,1,0:T(1,128)S(1)}, f32[3,1,2048]{2,1,0:T(1,128)S(1)}, u32[]{:S(2)}, u32[]{:S(2)}) collective-permute-start(f32[3,1,2048]{2,1,0:T(1,128)S(1)} %get-tuple-element.44), channel_id=1, source_target_pairs={{0,16},{8,24},{16,0},{24,8},{1,17},{9,25},{17,1},{25,9},{2,18},{10... | collective-permute-start | bytes 73736 | tf_op jit(solution)/shard_map/ppermute | solution.py:395
  34.9 4.6 %collective-permute-start.6 = (f32[3,1,2048]{2,1,0:T(1,128)S(1)}, f32[3,1,2048]{2,1,0:T(1,128)S(1)}, u32[]{:S(2)}, u32[]{:S(2)}) collective-permute-start(f32[3,1,2048]{2,1,0:T(1,128)S(1)} %get-tuple-element.45), channel_id=1, source_target_pairs={{0,8},{8,0},{16,24},{24,16},{1,9},{9,1},{17,25},{25,17},{2,10},{10... | collective-permute-start | bytes 73736 | tf_op jit(solution)/shard_map/ppermute | solution.py:395

commit v9 on v8

--- a/solution.py
+++ b/solution.py
@@ -404,7 +404,7 @@
 
 
 def sent_type(stages, i):
-    return F32 if i == 0 or i == len(stages) - 1 else BF16
+    return F32 if i == len(stages) - 1 else BF16
 
 
 def shards(n_server, n_worker, sgt, ownership, sub_points, moments, slip):

time: 41.5 us -> 41.3 us (level)
  no operation moved by 1% of the time
where the time goes in v9:
time: 41.3 us; the launch traced here: 41 us
  blocking collectives  15.7 us (38%)
  Pallas kernels  11.5 us (28%)
  starting transfers between devices  8.47 us (21%)
  waiting for transfers between devices  4.66 us (11%)
  between operations  0.68 us (2%)
    all_to_all x1, blocking collectives, shards(): lax.all_to_all(record, ('server', 'worker'), split_axis=0, concat_axis=0,...  15.7 us
    ppermute x7, starting transfers between devices, send(): lax.ppermute(parts[k], axis, [(i, i ^ k << shift) for i in range(size)])  8.47 us
    pallas_call x1, Pallas kernels, shards(): pl.pallas_call(functools.partial(owner_kernel, stages), out_shape=part_sh...  6.85 us
    ppermute x7, waiting for transfers between devices, send(): lax.ppermute(parts[k], axis, [(i, i ^ k << shift) for i in range(size)])  4.66 us
    pallas_call x1, Pallas kernels, shards(): pl.pallas_call(functools.partial(final_kernel, count), out_shape=[jax.Sha...  1.82 us
    pallas_call x1, Pallas kernels, shards(): pl.pallas_call(pack_kernel, out_shape=[jax.ShapeDtypeStruct((devices, cap...  1.69 us
    pallas_call x2, Pallas kernels, beside(): own, *made = lax.optimization_barrier((own, *kernel(base)))  0.93 us
  transfers between devices with their start and end apart: 7, of which 7 were waited for; matrix products, arithmetic and copies ran while one was open for 0% of the time, Pallas kernels for 3%

profile of v9, /device:TPU:0, one launch (start us, length us, event | category | flops | bytes accessed | tf_op | source)
XLA Modules:
  0.0 41.0 jit_solution(16504614307213682405)
XLA Ops:
  0.6 1.7 %pack.1 = (bf16[32,4,640]{2,1,0:T(4,128)(2,1)S(1)}, f32[96,1024]{1,0:T(8,128)S(1)}, bf16[3,128,2048]{2,1,0:T(8,128)(2,1)S(1)}) custom-call(s32[32,128]{1,0:T(8,128)} %bitcast.16, s32[4,24]{1,0:T(4,128)} %bitcast.18, f32[6,4,24]{2,1,0:T(4,128)} %bitcast.17, bf16[4,24,512]{2,1,0:T(8,128)(2,1)} %bitcast.15, f32[96,1024]{1,0:T(8,128)} %constant.6.clone.refs_4_, ...), custom_call_target="tpu_custom_call" | custom-call | tf_op jit(solution)/shard_map/pack/pallas_call | solution.py:425
  2.3 15.7 %all_to_all.5.rec_ref = bf16[32,4,640]{2,1,0:T(4,128)(2,1)S(1)} all-to-all(bf16[32,4,640]{2,1,0:T(4,128)(2,1)S(1)} %get-tuple-element.27), channel_id=1, replica_groups=mesh['server'=4,'worker'=8] {'server','worker'}, dimensions={0} | all-to-all | bytes 327680 | tf_op jit(solution)/shard_map/all_to_all | solution.py:457
  18.0 0.0 copy-start.1
  18.0 0.0 copy-start
  18.0 6.9 %owner.1 = (f32[3,16,2048]{2,1,0:T(8,128)S(1)}, bf16[3,16,2048]{2,1,0:T(8,128)(2,1)S(1)}) custom-call(bf16[32,4,640]{2,1,0:T(4,128)(2,1)S(1)} %all_to_all.5.rec_ref, bf16[18,128,2048]{2,1,0:T(8,128)(2,1)} %bitcast.14, f32[96,1024]{1,0:T(8,128)S(1)} %get-tuple-element.28.base_ref, bf16[3,128,2048]{2,1,0:T(8,128)(2,1)S(1)} %get-tuple-element.29.rows_ref), custom_call_target="tpu_custom_call" | custom-call | flops 10000000000 | bytes 20000000 | tf_op jit(solution)/shard_map/owner/pallas_call | solution.py:485
  24.9 0.5 %collective-permute-start = (bf16[3,16,2048]{2,1,0:T(8,128)(2,1)S(1)}, bf16[3,16,2048]{2,1,0:T(8,128)(2,1)S(1)}, u32[]{:S(2)}, u32[]{:S(2)}) collective-permute-start(bf16[3,16,2048]{2,1,0:T(8,128)(2,1)S(1)} %get-tuple-element.31), channel_id=1, source_target_pairs={{0,1},{1,0},{2,3},{3,2},{4,5},{5,4},{6,7},{7,6},{8,9},{9,8},{10,11... | collective-permute-start | bytes 589832 | tf_op jit(solution)/shard_map/ppermute | solution.py:395
  25.3 0.1 gain.1
  25.4 1.0 %collective-permute-done.refs_1_ = bf16[3,16,2048]{2,1,0:T(8,128)(2,1)S(1)} collective-permute-done((bf16[3,16,2048]{2,1,0:T(8,128)(2,1)S(1)}, bf16[3,16,2048]{2,1,0:T(8,128)(2,1)S(1)}, u32[]{:S(2)}, u32[]{:S(2)}) %collective-permute-start) | collective-permute-done | bytes 196640 | tf_op jit(solution)/shard_map/ppermute | solution.py:395
  26.4 0.1 sum_1.1
  26.5 1.1 %collective-permute-start.1 = (bf16[3,4,2048]{2,1,0:T(4,128)(2,1)S(1)}, bf16[3,4,2048]{2,1,0:T(4,128)(2,1)S(1)}, u32[]{:S(2)}, u32[]{:S(2)}) collective-permute-start(bf16[3,4,2048]{2,1,0:T(4,128)(2,1)S(1)} %get-tuple-element.36), channel_id=1, source_target_pairs={{0,6},{1,7},{2,4},{3,5},{4,2},{5,3},{6,0},{7,1},{8,14},{9,15},{10,... | collective-permute-start | bytes 147464 | tf_op jit(solution)/shard_map/ppermute | solution.py:395
  27.5 1.0 %collective-permute-start.2 = (bf16[3,4,2048]{2,1,0:T(4,128)(2,1)S(1)}, bf16[3,4,2048]{2,1,0:T(4,128)(2,1)S(1)}, u32[]{:S(2)}, u32[]{:S(2)}) collective-permute-start(bf16[3,4,2048]{2,1,0:T(4,128)(2,1)S(1)} %get-tuple-element.37), channel_id=1, source_target_pairs={{0,4},{1,5},{2,6},{3,7},{4,0},{5,1},{6,2},{7,3},{8,12},{9,13},{10,... | collective-permute-start | bytes 147464 | tf_op jit(solution)/shard_map/ppermute | solution.py:395
  28.6 1.5 %collective-permute-start.3 = (bf16[3,4,2048]{2,1,0:T(4,128)(2,1)S(1)}, bf16[3,4,2048]{2,1,0:T(4,128)(2,1)S(1)}, u32[]{:S(2)}, u32[]{:S(2)}) collective-permute-start(bf16[3,4,2048]{2,1,0:T(4,128)(2,1)S(1)} %get-tuple-element.38), channel_id=1, source_target_pairs={{0,2},{1,3},{2,0},{3,1},{4,6},{5,7},{6,4},{7,5},{8,10},{9,11},{10,... | collective-permute-start | bytes 147464 | tf_op jit(solution)/shard_map/ppermute | solution.py:395
  30.0 0.0 copy-done.1
  30.0 0.5 %inverse_table.2.refs_4_ = bf16[1024,512]{1,0:T(8,128)(2,1)S(1)} custom-call(f32[144,512]{1,0:T(8,128)S(1)} %copy-done.1), custom_call_target="tpu_custom_call" | custom-call | flops 1000000000 | bytes 10000000 | tf_op jit(solution)/shard_map/inverse_table/pallas_call | solution.py:402
  30.5 1.4 %collective-permute-done.1.refs_1_ = bf16[3,4,2048]{2,1,0:T(4,128)(2,1)S(1)} collective-permute-done((bf16[3,4,2048]{2,1,0:T(4,128)(2,1)S(1)}, bf16[3,4,2048]{2,1,0:T(4,128)(2,1)S(1)}, u32[]{:S(2)}, u32[]{:S(2)}) %collective-permute-start.1) | collective-permute-done | bytes 49184 | tf_op jit(solution)/shard_map/ppermute | solution.py:395
  31.9 0.2 collective-permute-done.2.refs_2_
  32.1 0.6 %collective-permute-done.3.refs_3_ = bf16[3,4,2048]{2,1,0:T(4,128)(2,1)S(1)} collective-permute-done((bf16[3,4,2048]{2,1,0:T(4,128)(2,1)S(1)}, bf16[3,4,2048]{2,1,0:T(4,128)(2,1)S(1)}, u32[]{:S(2)}, u32[]{:S(2)}) %collective-permute-start.3) | collective-permute-done | bytes 49184 | tf_op jit(solution)/shard_map/ppermute | solution.py:395
  32.7 1.5 %collective-permute-start.4 = (f32[3,1,2048]{2,1,0:T(1,128)S(1)}, f32[3,1,2048]{2,1,0:T(1,128)S(1)}, u32[]{:S(2)}, u32[]{:S(2)}) collective-permute-start(f32[3,1,2048]{2,1,0:T(1,128)S(1)} %get-tuple-element.43), channel_id=1, source_target_pairs={{0,24},{8,16},{16,8},{24,0},{1,25},{9,17},{17,9},{25,1},{2,26},{10... | collective-permute-start | bytes 73736 | tf_op jit(solution)/shard_map/ppermute | solution.py:395
  34.2 0.4 %collective-permute-start.5 = (f32[3,1,2048]{2,1,0:T(1,128)S(1)}, f32[3,1,2048]{2,1,0:T(1,128)S(1)}, u32[]{:S(2)}, u32[]{:S(2)}) collective-permute-start(f32[3,1,2048]{2,1,0:T(1,128)S(1)} %get-tuple-element.44), channel_id=1, source_target_pairs={{0,16},{8,24},{16,0},{24,8},{1,17},{9,25},{17,1},{25,9},{2,18},{10... | collective-permute-start | bytes 73736 | tf_op jit(solution)/shard_map/ppermute | solution.py:395
  34.6 2.5 %collective-permute-start.6 = (f32[3,1,2048]{2,1,0:T(1,128)S(1)}, f32[3,1,2048]{2,1,0:T(1,128)S(1)}, u32[]{:S(2)}, u32[]{:S(2)}) collective-permute-start(f32[3,1,2048]{2,1,0:T(1,128)S(1)} %get-tuple-element.45), channel_id=1, source_target_pairs={{0,8},{8,0},{16,24},{24,16},{1,9},{9,1},{17,25},{25,17},{2,10},{10... | collective-permute-start | bytes 73736 | tf_op jit(solution)/shard_map/ppermute | solution.py:395
  37.2 0.0 copy-done
  37.2 0.5 %inverse_table.3.refs_5_ = bf16[1024,512]{1,0:T(8,128)(2,1)S(1)} custom-call(f32[144,512]{1,0:T(8,128)S(1)} %copy-done), custom_call_target="tpu_custom_call" | custom-call | flops 1000000000 | bytes 10000000 | tf_op jit(solution)/shard_map/inverse_table/pallas_call | solution.py:402
  37.6 0.8 %collective-permute-done.4.refs_1_ = f32[3,1,2048]{2,1,0:T(1,128)S(1)} collective-permute-done((f32[3,1,2048]{2,1,0:T(1,128)S(1)}, f32[3,1,2048]{2,1,0:T(1,128)S(1)}, u32[]{:S(2)}, u32[]{:S(2)}) %collective-permute-start.4) | collective-permute-done | bytes 24608 | tf_op jit(solution)/shard_map/ppermute | solution.py:395
  38.4 0.5 %collective-permute-done.5.refs_2_ = f32[3,1,2048]{2,1,0:T(1,128)S(1)} collective-permute-done((f32[3,1,2048]{2,1,0:T(1,128)S(1)}, f32[3,1,2048]{2,1,0:T(1,128)S(1)}, u32[]{:S(2)}, u32[]{:S(2)}) %collective-permute-start.5) | collective-permute-done | bytes 24608 | tf_op jit(solution)/shard_map/ppermute | solution.py:395
  38.9 0.2 collective-permute-done.6.refs_3_
  39.2 1.8 %finish.1 = (f32[3,1,2048]{2,1,0:T(1,128)}, f32[3,1,44]{2,1,0:T(1,128)}) custom-call(f32[3,1,2048]{2,1,0:T(1,128)S(1)} %get-tuple-element.42.refs_0_, f32[3,1,2048]{2,1,0:T(1,128)S(1)} %collective-permute-done.4.refs_1_, f32[3,1,2048]{2,1,0:T(1,128)S(1)} %collective-permute-done.5.refs_2_, f32[3,1,2048]{2,1,0:T(1,128)S(1)} %collective-permute-done.6.refs_3_, ...), custom_call_target="tpu_custom_call" | custom-call | tf_op jit(solution)/shard_map/finish/pallas_call | solution.py:520
  (1 shorter events, 0.0 us)
Async XLA Ops:
  18.0 12.0 %copy-start.1 = (f32[144,512]{1,0:T(8,128)S(1)}, f32[144,512]{1,0:T(8,128)}, u32[]{:S(2)}) copy-start(f32[144,512]{1,0:T(8,128)} %constant.7.clone.base_ref) | copy-start | bytes 884740
  18.0 19.1 %copy-start = (f32[144,512]{1,0:T(8,128)S(1)}, f32[144,512]{1,0:T(8,128)}, u32[]{:S(2)}) copy-start(f32[144,512]{1,0:T(8,128)} %constant.8.clone.base_ref) | copy-start | bytes 884740
  24.9 1.5 %collective-permute-start = (bf16[3,16,2048]{2,1,0:T(8,128)(2,1)S(1)}, bf16[3,16,2048]{2,1,0:T(8,128)(2,1)S(1)}, u32[]{:S(2)}, u32[]{:S(2)}) collective-permute-start(bf16[3,16,2048]{2,1,0:T(8,128)(2,1)S(1)} %get-tuple-element.31), channel_id=1, source_target_pairs={{0,1},{1,0},{2,3},{3,2},{4,5},{5,4},{6,7},{7,6},{8,9},{9,8},{10,11... | collective-permute-start | bytes 589832 | tf_op jit(solution)/shard_map/ppermute | solution.py:395
  26.5 5.4 %collective-permute-start.1 = (bf16[3,4,2048]{2,1,0:T(4,128)(2,1)S(1)}, bf16[3,4,2048]{2,1,0:T(4,128)(2,1)S(1)}, u32[]{:S(2)}, u32[]{:S(2)}) collective-permute-start(bf16[3,4,2048]{2,1,0:T(4,128)(2,1)S(1)} %get-tuple-element.36), channel_id=1, source_target_pairs={{0,6},{1,7},{2,4},{3,5},{4,2},{5,3},{6,0},{7,1},{8,14},{9,15},{10,... | collective-permute-start | bytes 147464 | tf_op jit(solution)/shard_map/ppermute | solution.py:395
  27.5 4.6 %collective-permute-start.2 = (bf16[3,4,2048]{2,1,0:T(4,128)(2,1)S(1)}, bf16[3,4,2048]{2,1,0:T(4,128)(2,1)S(1)}, u32[]{:S(2)}, u32[]{:S(2)}) collective-permute-start(bf16[3,4,2048]{2,1,0:T(4,128)(2,1)S(1)} %get-tuple-element.37), channel_id=1, source_target_pairs={{0,4},{1,5},{2,6},{3,7},{4,0},{5,1},{6,2},{7,3},{8,12},{9,13},{10,... | collective-permute-start | bytes 147464 | tf_op jit(solution)/shard_map/ppermute | solution.py:395
  28.6 4.1 %collective-permute-start.3 = (bf16[3,4,2048]{2,1,0:T(4,128)(2,1)S(1)}, bf16[3,4,2048]{2,1,0:T(4,128)(2,1)S(1)}, u32[]{:S(2)}, u32[]{:S(2)}) collective-permute-start(bf16[3,4,2048]{2,1,0:T(4,128)(2,1)S(1)} %get-tuple-element.38), channel_id=1, source_target_pairs={{0,2},{1,3},{2,0},{3,1},{4,6},{5,7},{6,4},{7,5},{8,10},{9,11},{10,... | collective-permute-start | bytes 147464 | tf_op jit(solution)/shard_map/ppermute | solution.py:395
  32.7 5.7 %collective-permute-start.4 = (f32[3,1,2048]{2,1,0:T(1,128)S(1)}, f32[3,1,2048]{2,1,0:T(1,128)S(1)}, u32[]{:S(2)}, u32[]{:S(2)}) collective-permute-start(f32[3,1,2048]{2,1,0:T(1,128)S(1)} %get-tuple-element.43), channel_id=1, source_target_pairs={{0,24},{8,16},{16,8},{24,0},{1,25},{9,17},{17,9},{25,1},{2,26},{10... | collective-permute-start | bytes 73736 | tf_op jit(solution)/shard_map/ppermute | solution.py:395
  34.2 4.8 %collective-permute-start.5 = (f32[3,1,2048]{2,1,0:T(1,128)S(1)}, f32[3,1,2048]{2,1,0:T(1,128)S(1)}, u32[]{:S(2)}, u32[]{:S(2)}) collective-permute-start(f32[3,1,2048]{2,1,0:T(1,128)S(1)} %get-tuple-element.44), channel_id=1, source_target_pairs={{0,16},{8,24},{16,0},{24,8},{1,17},{9,25},{17,1},{25,9},{2,18},{10... | collective-permute-start | bytes 73736 | tf_op jit(solution)/shard_map/ppermute | solution.py:395
  34.6 4.6 %collective-permute-start.6 = (f32[3,1,2048]{2,1,0:T(1,128)S(1)}, f32[3,1,2048]{2,1,0:T(1,128)S(1)}, u32[]{:S(2)}, u32[]{:S(2)}) collective-permute-start(f32[3,1,2048]{2,1,0:T(1,128)S(1)} %get-tuple-element.45), channel_id=1, source_target_pairs={{0,8},{8,0},{16,24},{24,16},{1,9},{9,1},{17,25},{25,17},{2,10},{10... | collective-permute-start | bytes 73736 | tf_op jit(solution)/shard_map/ppermute | solution.py:395
